TPU v7x, 32 devices: a whole 2x2x4 slice. The times are simulated.
32 devices in a mesh: dp: 8 (over y, x, core), mp: 4 (over z).
Axes of the slice: x: 2, y: 2, z: 4, core: 2. Of those that a mesh axis runs over, the one named last changes fastest.
Arguments:
- tokens: bfloat16 [12288, 1024], P(('dp', 'mp')), may hold values from -6 to 6
- seg_ids: int32 [8, 1536], P('dp'), may hold values from 0 to 1, as said below
- bucket_of: int32 [128], replicated, may hold values from 0 to 31, as said below
- ln1_gain: float32 [1024], replicated, may hold values from 0.5 to 1.5
- ln1_bias: float32 [1024], replicated, may hold values from -1.2 to 1.2
- w_qkv: bfloat16 [3, 1024, 1024], P(None, None, 'mp'), may hold values from -0.1875 to 0.1875
- rel_table: float32 [32, 16], P(None, 'mp'), may hold values from -4 to 4
- w_out: bfloat16 [1024, 1024], P('mp'), may hold values from -2 to 2
- ln2_gain: float32 [1024], replicated, may hold values from 0.5 to 1.5
- ln2_bias: float32 [1024], replicated, may hold values from -1.2 to 1.2
- w_up: bfloat16 [1024, 4096], P(None, 'mp'), may hold values from -0.1875 to 0.1875
- up_bias: float32 [4096], P('mp'), may hold values from -1.2 to 1.2
- w_down: bfloat16 [4096, 1024], P('mp'), may hold values from -0.09375 to 0.09375
- down_bias: float32 [1024], replicated, may hold values from -1.2 to 1.2
- out_grad: bfloat16 [12288, 1024], P(('dp', 'mp')), may hold values from -6 to 6
Outputs:
- layer_out: bfloat16 [12288, 1024], P(('dp', 'mp'))
- grad_tokens: bfloat16 [12288, 1024], P(('dp', 'mp'))
- grad_ln1_gain: float32 [1024], replicated
- grad_ln1_bias: float32 [1024], replicated
- grad_qkv: float32 [3, 1024, 1024], P(None, None, 'mp')
- grad_table: float32 [32, 16], P(None, 'mp')
- grad_wout: float32 [1024, 1024], P('mp')
- grad_ln2_gain: float32 [1024], replicated
- grad_ln2_bias: float32 [1024], replicated
- grad_up: float32 [1024, 4096], P(None, 'mp')
- grad_up_bias: float32 [4096], P('mp')
- grad_down: float32 [4096, 1024], P('mp')
- grad_down_bias: float32 [1024], replicated
Inputs may be any that keep to these rules, and one draw needn't show every extreme that they name: `seg_ids`: each row holds 2 sequences: ids 0 then 1, never falling; each sequence has 512 to 1024 tokens, and some row has one of exactly 1024 tokens. bucket_of[d] = d for d < 16; beyond, it never falls, rises by at most one from one distance to the next, and its last entry is 31.
All inputs are finite; a program needn't handle non-finite values.
Results may differ from a plain program's by a relative error of at most 0.02.
Values may be sent and summed in bfloat16 or wider, within the bound.
No kernel may reach another device: no remote copies, remote signals or barrier semaphores. Data moves between devices by JAX's collectives and lax.ppermute only.
A program may use at most 192 MiB of HBM per device.

v0:
```python
import functools

import jax
import jax.numpy as jnp
from jax import lax
from jax.experimental import pallas as pl
from jax.experimental.pallas import tpu as pltpu
from jax.sharding import Mesh, PartitionSpec as P

EPSILON = 1e-05
HIGHEST_PRECISION = lax.Precision.HIGHEST
LIGHT = pl.CostEstimate(flops=1, bytes_accessed=1, transcendentals=0)
MIDDLE = pl.CostEstimate(flops=2 * 10**10, bytes_accessed=1, transcendentals=0)
SMALL = pl.CostEstimate(flops=1, bytes_accessed=1, transcendentals=0)
COVER = pl.CostEstimate(flops=16 * 10**9, bytes_accessed=1, transcendentals=0)
HEAVY = pl.CostEstimate(flops=10**11, bytes_accessed=1, transcendentals=0)
FEED_STEPS = 4
BLK = 256
HEAD_LANES = 64
NEAR = 128


def head_mask(rows, width, head, axis):
    place = lax.broadcasted_iota(jnp.int32, (rows, width), axis)
    return (place >= head * HEAD_LANES) & (place < (head + 1) * HEAD_LANES)


def one_head(value, head):
    keep = head_mask(value.shape[0], value.shape[1], head, 1)
    return jnp.where(keep, value, jnp.zeros_like(value))


def scaled(queries):
    return queries * jnp.asarray(HEAD_LANES ** -0.5, queries.dtype)


def dot_nt(left, right):
    return lax.dot_general(
        left, right, (((1,), (1,)), ((), ())), preferred_element_type=jnp.float32
    )


def dot_nn(left, right):
    return lax.dot_general(
        left, right, (((1,), (0,)), ((), ())), preferred_element_type=jnp.float32
    )


def attention_forward_kernel(
    cut_ref, rows_ref, weight_ref, bias_ref,
    qkv_a, qkv_b, out_ref, lse_a, lse_b, tile_ref, masked_v, score_ref,
):
    heads = masked_v.shape[0]
    width = out_ref.shape[1] // 2
    block = pl.program_id(0)
    cut = cut_ref[0]
    qkv_refs, lse_refs = (qkv_a, qkv_b), (lse_a, lse_b)

    @pl.when(block == 0)
    def _():
        weights = [
            jnp.concatenate(
                [weight_ref[slot, :, pair * width : (pair + 1) * width] for slot in range(3)],
                axis=1,
            )
            for pair in range(2)
        ]

        def one_chunk(chunk, carry):
            spot = pl.ds(pl.multiple_of(chunk * BLK, BLK), BLK)
            for pair in range(2):
                qkv_refs[pair][spot, :] = dot_nn(rows_ref[spot, :], weights[pair]).astype(
                    jnp.bfloat16
                )
            return carry

        lax.fori_loop(0, rows_ref.shape[0] // BLK, one_chunk, 0)
        for head in range(heads):
            wide = jnp.broadcast_to(bias_ref[head : head + 1, :], (BLK, 2 * BLK))
            tile_ref[head] = pltpu.roll(wide, 0, 1, stride=1, stride_axis=0)
            masked_v[head] = one_head(qkv_refs[head // 2][:, 2 * width :], head % 2)

    row_start = block * BLK
    first = jnp.where(row_start >= cut, cut // BLK, 0)
    rows = row_start + lax.broadcasted_iota(jnp.int32, (BLK, BLK), 0)
    seg_start = jnp.where(rows >= cut, cut, 0)
    columns = lax.broadcasted_iota(jnp.int32, (BLK, BLK), 1)
    own = pl.ds(pl.multiple_of(row_start, BLK), BLK)
    q_heads = [
        one_head(scaled(qkv_refs[head // 2][own, 0:width]), head % 2) for head in range(heads)
    ]

    def scores_of(key_block, tops):
        key_start = pl.multiple_of(key_block * BLK, BLK)
        keys = [ref[pl.ds(key_start, BLK), width : 2 * width] for ref in qkv_refs]
        places = key_start + columns
        allowed = (places <= rows) & (places >= seg_start)
        offset = pl.multiple_of(jnp.maximum(key_block - block + 1, 0) * BLK, BLK)
        near = key_block - block + 1 >= 0
        new_tops = []
        for head in range(heads):
            raw = dot_nt(q_heads[head], keys[head // 2])
            far = bias_ref[head : head + 1, 2 * BLK - 1 : 2 * BLK]
            bias = jnp.where(near, tile_ref[head, :, pl.ds(offset, BLK)], far)
            scores = jnp.where(allowed, raw + bias, -1e30)
            score_ref[head, :, pl.ds(key_start, BLK)] = scores
            top = tops[head]
            for lane in range(0, BLK, 128):
                top = jnp.maximum(top, scores[:, lane : lane + 128])
            new_tops.append(top)
        return tuple(new_tops)

    start = tuple(jnp.full((BLK, 128), -1e30, jnp.float32) for _ in range(heads))
    tops = lax.fori_loop(first, block + 1, scores_of, start)
    tops = [jnp.max(top, axis=1, keepdims=True) for top in tops]

    def weighted(key_block, carry):
        totals, sums = carry
        key_start = pl.multiple_of(key_block * BLK, BLK)
        new_totals, new_sums = [], []
        for pair in range(2):
            pieces, values = [], []
            for head in (2 * pair, 2 * pair + 1):
                soft = jnp.exp(score_ref[head, :, pl.ds(key_start, BLK)] - tops[head])
                part = sums[head]
                for lane in range(0, BLK, 128):
                    part = part + soft[:, lane : lane + 128]
                new_sums.append(part)
                pieces.append(soft.astype(jnp.bfloat16))
                values.append(masked_v[head, pl.ds(key_start, BLK), :])
            new_totals.append(
                totals[pair]
                + dot_nn(jnp.concatenate(pieces, axis=1), jnp.concatenate(values, axis=0))
            )
        return tuple(new_totals), tuple(new_sums)

    totals, sums = lax.fori_loop(
        first,
        block + 1,
        weighted,
        (
            tuple(jnp.zeros((BLK, width), jnp.float32) for _ in range(2)),
            tuple(jnp.zeros((BLK, 128), jnp.float32) for _ in range(heads)),
        ),
    )
    lanes = lax.broadcasted_iota(jnp.int32, (BLK, width), 1)
    for pair in range(2):
        scale = jnp.zeros((BLK, width), jnp.float32)
        logs = jnp.zeros((BLK, width), jnp.float32)
        for place in range(2):
            head = 2 * pair + place
            sum_one = jnp.sum(sums[head], axis=1, keepdims=True)
            scale = jnp.where(lanes // HEAD_LANES == place, 1.0 / sum_one, scale)
            logs = jnp.where(lanes == place, tops[head] + jnp.log(sum_one), logs)
        out_ref[:, pair * width : (pair + 1) * width] = (totals[pair] * scale).astype(jnp.bfloat16)
        lse_refs[pair][...] = jnp.transpose(logs)[0:8, :]


def attention_forward(cut, normed, weights, near_bias):
    length, depth = normed.shape
    width = weights.shape[2] // 2
    heads = 2 * width // HEAD_LANES
    whole = lambda block, cut: (0, 0)
    full = pl.BlockSpec((length, 3 * width), whole)
    row = pl.BlockSpec((BLK, 2 * width), lambda block, cut: (block, 0))
    line = pl.BlockSpec((8, BLK), lambda block, cut: (0, block))
    return pl.pallas_call(
        attention_forward_kernel,
        grid_spec=pltpu.PrefetchScalarGridSpec(
            num_scalar_prefetch=1,
            grid=(length // BLK,),
            in_specs=[
                pl.BlockSpec((length, depth), whole, pipeline_mode=pl.Buffered(1)),
                pl.BlockSpec(
                    weights.shape, lambda block, cut: (0, 0, 0), pipeline_mode=pl.Buffered(1)
                ),
                pl.BlockSpec((8, 2 * BLK), whole),
            ],
            out_specs=[full, full, row, line, line],
            scratch_shapes=[
                pltpu.VMEM((heads, BLK, 2 * BLK), jnp.float32),
                pltpu.VMEM((heads, length, width), jnp.bfloat16),
                pltpu.VMEM((heads, BLK, length), jnp.float32),
            ],
        ),
        out_shape=[jax.ShapeDtypeStruct((length, 3 * width), jnp.bfloat16)] * 2
        + [jax.ShapeDtypeStruct((length, 2 * width), jnp.bfloat16)]
        + [jax.ShapeDtypeStruct((8, length), jnp.float32)] * 2,
        compiler_params=pltpu.CompilerParams(
            dimension_semantics=("arbitrary",), vmem_limit_bytes=48 * 1024 * 1024
        ),
        cost_estimate=LIGHT,
        name="attention_forward",
    )(cut, normed, weights, near_bias)


def attention_backward_kernel(
    cut_ref, qkv_a, qkv_b, grad_ref, att_ref, lse_a, lse_b, bias_ref,
    dqkv_a, dqkv_b, table_ref,
    tile_ref, q_masked, grad_masked, delta_ref, dq_sum, near_sum, far_sum,
):
    heads = q_masked.shape[0]
    block = pl.program_id(0)
    n_blocks = pl.num_programs(0)
    length = grad_ref.shape[0]
    width = att_ref.shape[1] // 2
    cut = cut_ref[0]
    qkv_refs, lse_refs, out_refs = (qkv_a, qkv_b), (lse_a, lse_b), (dqkv_a, dqkv_b)

    @pl.when(block == 0)
    def _():
        row = lax.broadcasted_iota(jnp.int32, (16, width), 0)
        lane = lax.broadcasted_iota(jnp.int32, (16, width), 1)
        pick = jnp.where(lane // HEAD_LANES == row, 1.0, 0.0).astype(jnp.bfloat16)
        for pair in range(2):
            lanes = slice(pair * width, (pair + 1) * width)
            grad_pair = grad_ref[:, lanes]
            product = grad_pair.astype(jnp.float32) * att_ref[:, lanes].astype(jnp.float32)
            high = product.astype(jnp.bfloat16)
            rest = (product - high.astype(jnp.float32)).astype(jnp.bfloat16)
            delta_ref[pair] = (dot_nt(pick, high) + dot_nt(pick, rest))[0:8, :]
            queries = scaled(qkv_refs[pair][:, 0:width])
            for place in range(2):
                head = 2 * pair + place
                q_masked[head] = one_head(queries, place)
                grad_masked[head] = one_head(grad_pair, place)
        for head in range(heads):
            wide = jnp.broadcast_to(bias_ref[head : head + 1, :], (BLK, 2 * BLK))
            tile_ref[head] = pltpu.roll(wide, 0, 1, stride=1, stride_axis=0)
        dq_sum[...] = jnp.zeros_like(dq_sum)
        near_sum[...] = jnp.zeros_like(near_sum)
        far_sum[...] = jnp.zeros_like(far_sum)

    key_start = pl.multiple_of(block * BLK, BLK)
    keys = [ref[pl.ds(key_start, BLK), width : 2 * width] for ref in qkv_refs]
    values = [ref[pl.ds(key_start, BLK), 2 * width :] for ref in qkv_refs]
    keys_t = [jnp.transpose(one) for one in keys]
    places = key_start + lax.broadcasted_iota(jnp.int32, (BLK, BLK), 0)
    columns = lax.broadcasted_iota(jnp.int32, (BLK, BLK), 1)
    last = jnp.where(key_start + BLK <= cut, (cut + BLK - 1) // BLK, n_blocks)

    def one_block(query_block, carry):
        row_start = pl.multiple_of(query_block * BLK, BLK)
        rows = row_start + columns
        allowed = (places <= rows) & (places >= jnp.where(rows >= cut, cut, 0))
        distance = query_block - block
        near = distance <= 1
        offset = pl.multiple_of(jnp.minimum(distance, 1) * BLK, BLK)
        results = []
        for pair in range(2):
            soft_pieces, grad_pieces, q_pieces, out_pieces = [], [], [], []
            for place in range(2):
                head = 2 * pair + place
                q_head = q_masked[head, pl.ds(row_start, BLK), :]
                grad_head = grad_masked[head, pl.ds(row_start, BLK), :]
                far = bias_ref[head : head + 1, BLK - 1 : BLK]
                bias = jnp.where(near, tile_ref[head, :, pl.ds(offset, BLK)], far)
                scores = dot_nt(keys[pair], q_head) + bias
                log_total = lse_refs[pair][place : place + 1, pl.ds(row_start, BLK)]
                soft = jnp.exp(jnp.where(allowed, scores - log_total, -1e30))
                grad_soft = dot_nt(values[pair], grad_head)
                delta = delta_ref[pair, place : place + 1, pl.ds(row_start, BLK)]
                grad_scores = soft * (grad_soft - delta)
                grad_low = grad_scores.astype(jnp.bfloat16)

                @pl.when(near)
                def _():
                    near_sum[head, :, pl.ds(offset, BLK)] += grad_scores

                @pl.when(jnp.logical_not(near))
                def _():
                    far_sum[head] += jnp.sum(
                        grad_scores.reshape(BLK // 8, 8, BLK), axis=0
                    )

                own = slice(place * HEAD_LANES, (place + 1) * HEAD_LANES)
                spot = slice(head * HEAD_LANES, (head + 1) * HEAD_LANES)
                dq_sum[spot, pl.ds(row_start, BLK)] += dot_nn(keys_t[pair][own, :], grad_low)
                soft_pieces.append(soft.astype(jnp.bfloat16))
                grad_pieces.append(grad_low)
                q_pieces.append(q_head)
                out_pieces.append(grad_head)
            dk, dv = carry[pair]
            dv = dv + dot_nn(
                jnp.concatenate(soft_pieces, axis=1), jnp.concatenate(out_pieces, axis=0)
            )
            dk = dk + dot_nn(
                jnp.concatenate(grad_pieces, axis=1), jnp.concatenate(q_pieces, axis=0)
            )
            results.append((dk, dv))
        return tuple(results)

    empty = jnp.zeros((BLK, width), jnp.float32)
    results = lax.fori_loop(block, last, one_block, ((empty, empty), (empty, empty)))
    for pair in range(2):
        dk, dv = results[pair]
        out_refs[pair][pl.ds(key_start, BLK), width : 2 * width] = dk.astype(jnp.bfloat16)
        out_refs[pair][pl.ds(key_start, BLK), 2 * width :] = dv.astype(jnp.bfloat16)

    @pl.when(block == n_blocks - 1)
    def _():
        for query_block in range(length // BLK):
            spot = slice(query_block * BLK, (query_block + 1) * BLK)
            turned = (jnp.transpose(dq_sum[:, spot]) * (HEAD_LANES ** -0.5)).astype(jnp.bfloat16)
            for pair in range(2):
                out_refs[pair][spot, 0:width] = turned[:, pair * width : (pair + 1) * width]
        for head in range(heads):
            lined = jnp.zeros((8, 2 * BLK), jnp.float32)
            for group in range(BLK // 8):
                piece = near_sum[head, group * 8 : group * 8 + 8, :]
                shift = (2 * BLK - group * 8) % (2 * BLK)
                lined = lined + (pltpu.roll(piece, shift, 1) if shift else piece)
            total = lined[0:1, :]
            for row in range(1, 8):
                total = total + pltpu.roll(lined, 2 * BLK - row, 1)[row : row + 1, :]
            table_ref[head : head + 1, :] = total
            rest = jnp.sum(far_sum[head], axis=0, keepdims=True)
            table_ref[heads + head : heads + head + 1, :] = jnp.concatenate(
                [rest, jnp.zeros_like(rest)], axis=1
            )


def attention_backward(cut, projected, grad_att, attended, logs, near_bias):
    length, width = attended.shape[0], attended.shape[1] // 2
    heads = 2 * width // HEAD_LANES
    whole = lambda block, cut: (0, 0)
    full = lambda columns: pl.BlockSpec((length, columns), whole)
    lse = pl.BlockSpec((8, length), whole)
    return pl.pallas_call(
        attention_backward_kernel,
        grid_spec=pltpu.PrefetchScalarGridSpec(
            num_scalar_prefetch=1,
            grid=(length // BLK,),
            in_specs=[
                full(3 * width), full(3 * width), full(2 * width), full(2 * width),
                lse, lse, pl.BlockSpec((8, 2 * BLK), whole),
            ],
            out_specs=[
                full(3 * width), full(3 * width), pl.BlockSpec((8, 2 * BLK), whole),
            ],
            scratch_shapes=[
                pltpu.VMEM((heads, BLK, 2 * BLK), jnp.float32),
                pltpu.VMEM((heads, length, width), jnp.bfloat16),
                pltpu.VMEM((heads, length, width), jnp.bfloat16),
                pltpu.VMEM((2, 8, length), jnp.float32),
                pltpu.VMEM((2 * width, length), jnp.float32),
                pltpu.VMEM((heads, BLK, 2 * BLK), jnp.float32),
                pltpu.VMEM((heads, 8, BLK), jnp.float32),
            ],
        ),
        out_shape=[
            jax.ShapeDtypeStruct((length, 3 * width), jnp.bfloat16),
            jax.ShapeDtypeStruct((length, 3 * width), jnp.bfloat16),
            jax.ShapeDtypeStruct((8, 2 * BLK), jnp.float32),
        ],
        compiler_params=pltpu.CompilerParams(
            dimension_semantics=("arbitrary",), vmem_limit_bytes=48 * 1024 * 1024
        ),
        cost_estimate=MIDDLE,
        name="attention_backward",
    )(cut, *projected, grad_att, attended, *logs, near_bias)


def distance_bias(rel_table, bucket_of):
    hot = (
        bucket_of[:, None] == jnp.arange(rel_table.shape[0], dtype=jnp.int32)[None, :]
    ).astype(jnp.float32)
    by_distance = jnp.einsum(
        "dn,nh->hd", hot, rel_table, precision=HIGHEST_PRECISION,
        preferred_element_type=jnp.float32,
    )
    return hot, by_distance


def near_tables(by_distance):
    heads, reach = by_distance.shape
    far = by_distance[:, reach - 1 :]
    forward = jnp.concatenate(
        [
            jnp.broadcast_to(far, (heads, BLK - reach + 1)),
            by_distance[:, ::-1],
            jnp.broadcast_to(far, (heads, BLK - 1)),
        ],
        axis=1,
    )
    backward = jnp.concatenate(
        [by_distance, jnp.broadcast_to(far, (heads, 2 * BLK - reach))], axis=1
    )
    rows = ((0, 8 - heads), (0, 0))
    return jnp.pad(forward, rows), jnp.pad(backward, rows)


def table_gradient(hot, near_sums, far_sums):
    reach = hot.shape[0]
    near = near_sums[:, : reach - 1]
    far = jnp.sum(near_sums[:, reach - 1 :], axis=1) + jnp.sum(far_sums, axis=1)
    by_distance = jnp.concatenate([near, far[:, None]], axis=1)
    return jnp.einsum(
        "dn,hd->nh", hot, by_distance, precision=HIGHEST_PRECISION,
        preferred_element_type=jnp.float32,
    )


TEAM = 4


def after(value, *gates):
    return lax.optimization_barrier((value,) + gates)[0]


def flip(value, axis, bit):
    size = lax.axis_size(axis)
    return lax.ppermute(value, axis, [(i, i ^ bit) for i in range(size)])


def halve(value, dim, axis, bit):
    mine = (lax.axis_index(axis) // bit) % 2
    keep = lax.dynamic_index_in_dim(value, mine, dim, keepdims=False)
    send = lax.dynamic_index_in_dim(value, 1 - mine, dim, keepdims=False)
    received = flip(send.astype(jnp.bfloat16), axis, bit)
    return (keep.astype(jnp.float32) + received.astype(jnp.float32)).astype(jnp.bfloat16)


def halve_start(value, dim, axis, bit):
    mine = (lax.axis_index(axis) // bit) % 2
    keep = lax.dynamic_index_in_dim(value, mine, dim, keepdims=False)
    send = lax.dynamic_index_in_dim(value, 1 - mine, dim, keepdims=False)
    return keep, flip(send, axis, bit)


def halve_end(pair):
    return (pair[0].astype(jnp.float32) + pair[1].astype(jnp.float32)).astype(jnp.bfloat16)


def double(value, axis, bit):
    mine = (lax.axis_index(axis) // bit) % 2
    other = flip(value, axis, bit)
    return jnp.where(mine == 0, jnp.stack([value, other]), jnp.stack([other, value]))


def bits_of(size):
    bits = []
    bit = 1
    while bit < size:
        bits.append(bit)
        bit *= 2
    return bits


def with_partner(own):
    return jnp.concatenate([own, flip(own, "team", 1)], axis=0)


def feed_grads_kernel(core_ref, own_ref, got_ref, up_ref, down_ref, *, spots):
    unit = own_ref.shape[2]
    half = len(spots) // 2

    def write(piece_ref, places):
        for index, spot in enumerate(places):
            where = slice(spot * unit, (spot + 1) * unit)
            up_ref[:, where] = jnp.transpose(piece_ref[index, 0].astype(jnp.float32))
            down_ref[where, :] = piece_ref[index, 1].astype(jnp.float32)

    def both(core):
        write(own_ref, spots[core * half : (core + 1) * half])
        write(got_ref, spots[(1 - core) * half : (2 - core) * half])

    for core in range(2):
        pl.when(core_ref[0] == core)(functools.partial(both, core))


def feed_grads_out(core, own, got, copies):
    count, _, unit, depth = own.shape
    merge = max(1, 128 // unit)
    if merge > 1:
        own, got = (
            jnp.transpose(
                one.reshape(count // merge, merge, 2, unit, depth), (0, 2, 1, 3, 4)
            ).reshape(count // merge, 2, merge * unit, depth)
            for one in (own, got)
        )
    count, _, unit, depth = own.shape
    each = copies // merge
    spots = []
    for step in range(2 * count):
        half, side, place = place_in_group(step, each)
        spots.append((side * 2 + half) * each + place)
    take = depth // 4
    piece = pl.BlockSpec((count, 2, unit, take), lambda step, core: (0, 0, 0, step))
    return pl.pallas_call(
        functools.partial(feed_grads_kernel, spots=spots),
        grid_spec=pltpu.PrefetchScalarGridSpec(
            num_scalar_prefetch=1,
            grid=(4,),
            in_specs=[piece, piece],
            out_specs=[
                pl.BlockSpec((take, 2 * count * unit), lambda step, core: (step, 0)),
                pl.BlockSpec((2 * count * unit, take), lambda step, core: (0, step)),
            ],
        ),
        out_shape=[
            jax.ShapeDtypeStruct((depth, 2 * count * unit), jnp.float32),
            jax.ShapeDtypeStruct((2 * count * unit, depth), jnp.float32),
        ],
        compiler_params=pltpu.CompilerParams(dimension_semantics=("arbitrary",)),
        cost_estimate=LIGHT,
        name="feed_grads_out",
    )(core, own, got)


def attention_grads_kernel(core_ref, own_ref, got_ref, qkv_ref, out_ref, *, spots):
    group = own_ref.shape[0]
    rows, width = qkv_ref.shape[1] // group, qkv_ref.shape[2]
    few = out_ref.shape[0] // group

    def place_all(piece_ref, core):
        for item in range(group):
            spot = spots[core * group + item] - core * group
            for slot in range(3):
                qkv_ref[slot, spot * rows : (spot + 1) * rows, :] = piece_ref[
                    item, slot * rows : (slot + 1) * rows, :
                ].astype(jnp.float32)
            for place in range(out_ref.shape[1] // width):
                start = 3 * rows + place * few
                out_ref[
                    spot * few : (spot + 1) * few, place * width : (place + 1) * width
                ] = piece_ref[item, start : start + few, :].astype(jnp.float32)

    step = pl.program_id(0)
    for core in range(2):
        mine = (step == core) & (core_ref[0] == core)
        other = (step == core) & (core_ref[0] != core)
        pl.when(mine)(functools.partial(place_all, own_ref, core))
        pl.when(other)(functools.partial(place_all, got_ref, core))


def attention_grads_out(core, own, got, depth, head_width):
    half = own.shape[0]
    copies = half // 2
    spots = []
    for step in range(2 * half):
        side_core, side, place = place_in_group(step, copies)
        spots.append((side_core * 2 + side) * copies + place)
    whole = pl.BlockSpec(own.shape, lambda step, core: (0, 0, 0))
    return pl.pallas_call(
        functools.partial(attention_grads_kernel, spots=spots),
        grid_spec=pltpu.PrefetchScalarGridSpec(
            num_scalar_prefetch=1,
            grid=(2,),
            in_specs=[whole, whole],
            out_specs=[
                pl.BlockSpec((3, depth // 2, head_width), lambda step, core: (0, step, 0)),
                pl.BlockSpec((head_width // 2, depth), lambda step, core: (step, 0)),
            ],
        ),
        out_shape=[
            jax.ShapeDtypeStruct((3, depth, head_width), jnp.float32),
            jax.ShapeDtypeStruct((head_width, depth), jnp.float32),
        ],
        compiler_params=pltpu.CompilerParams(dimension_semantics=("arbitrary",)),
        cost_estimate=LIGHT,
        name="attention_grads_out",
    )(core, own, got)


def qkv_grad_kernel(core_ref, rows_ref, grad_a, grad_b, send_ref, keep_ref):
    width = grad_a.shape[1]
    both = [dot_tn(rows_ref[...], grad[...]).astype(jnp.bfloat16) for grad in (grad_a, grad_b)]

    @pl.when(pl.program_id(0) == 0)
    def _():
        send_ref[:, 0:width] = both[0]
        send_ref[:, width:] = both[1]

    @pl.when(pl.program_id(0) == 1)
    def _():
        keep_ref[:, 0:width] = both[0]
        keep_ref[:, width:] = both[1]


def qkv_weight_grad(core, rows, grads):
    length, depth = rows.shape
    width = grads[0].shape[1]
    half = depth // 2
    whole = pl.BlockSpec((length, width), lambda step, core: (0, 0))
    out = pl.BlockSpec((half, 2 * width), lambda step, core: (0, 0))
    return pl.pallas_call(
        qkv_grad_kernel,
        grid_spec=pltpu.PrefetchScalarGridSpec(
            num_scalar_prefetch=1,
            grid=(2,),
            in_specs=[
                pl.BlockSpec((length, half), lambda step, core: (0, 1 - core[0] ^ step)),
                whole, whole,
            ],
            out_specs=[out, out],
        ),
        out_shape=[jax.ShapeDtypeStruct((half, 2 * width), jnp.bfloat16)] * 2,
        compiler_params=pltpu.CompilerParams(
            dimension_semantics=("arbitrary",), vmem_limit_bytes=40 * 1024 * 1024
        ),
        cost_estimate=SMALL,
        name="qkv_weight_grad",
    )(core, rows, *grads)


def branch_kernel(*refs, count):
    pieces = refs[:count]
    weight_ref, token_ref, line_ref, hidden_ref, second_ref, left_ref = refs[count:]
    left = jnp.concatenate([piece[...] for piece in pieces], axis=1)
    left_ref[...] = left
    hidden = token_ref[...].astype(jnp.float32) + dot_nn(left, weight_ref[...])
    unit, _ = normalize(hidden)
    hidden_ref[...] = hidden
    second_ref[...] = (unit * line_ref[0:1, :] + line_ref[1:2, :]).astype(jnp.bfloat16)


def branch_and_norm(pieces, weights, tokens, lines):
    rows, depth = tokens.shape
    return pl.pallas_call(
        functools.partial(branch_kernel, count=len(pieces)),
        out_shape=[
            jax.ShapeDtypeStruct((rows, depth), jnp.float32),
            jax.ShapeDtypeStruct((rows, depth), jnp.bfloat16),
            jax.ShapeDtypeStruct((rows, weights.shape[0]), jnp.bfloat16),
        ],
        compiler_params=pltpu.CompilerParams(vmem_limit_bytes=32 * 1024 * 1024),
        cost_estimate=LIGHT,
        name="branch_and_norm",
    )(*pieces, weights, tokens, lines)


def row_grads_kernel(
    own_ref, core_ref, across_ref, grad_ref, hidden_ref, weight_ref, line_ref,
    total_ref, branch_ref, *refs,
):
    block_refs, sum_ref = refs[:-1], refs[-1]
    second = (
        own_ref[...].astype(jnp.float32) + core_ref[...].astype(jnp.float32)
        + across_ref[...].astype(jnp.float32)
    )
    grad = grad_ref[...].astype(jnp.float32)
    unit, inverse = normalize(hidden_ref[...])
    total = grad + normalize_backward(second, line_ref[0:1, :], unit, inverse)
    branch = total.astype(jnp.bfloat16)
    total_ref[...] = total
    branch_ref[...] = branch
    width = block_refs[0].shape[1]
    for index, block_ref in enumerate(block_refs):
        block_ref[...] = dot_nt(
            branch, weight_ref[index * width : (index + 1) * width, :]
        ).astype(jnp.bfloat16)
    sums = [jnp.sum(one, axis=0, keepdims=True) for one in (second * unit, second, grad)]
    lines = jnp.concatenate(sums + [jnp.zeros((5, sums[0].shape[1]), jnp.float32)])

    sum_ref[...] = lines


def row_grads(backs, grad, hidden, weights, lines, parts):
    rows, depth = hidden.shape
    width = weights.shape[0] // parts
    return pl.pallas_call(
        row_grads_kernel,
        out_shape=[
            jax.ShapeDtypeStruct((rows, depth), jnp.float32),
            jax.ShapeDtypeStruct((rows, depth), jnp.bfloat16),
        ]
        + [jax.ShapeDtypeStruct((rows, width), jnp.bfloat16)] * parts
        + [jax.ShapeDtypeStruct((8, depth), jnp.float32)],
        compiler_params=pltpu.CompilerParams(vmem_limit_bytes=40 * 1024 * 1024),
        cost_estimate=LIGHT,
        name="row_grads",
    )(*backs, grad, hidden, weights, lines)


def out_grad_kernel(core_ref, left_ref, right_ref, keep_ref, send_ref):
    parts, half, _ = keep_ref.shape

    def columns(core):
        return jnp.concatenate(
            [
                left_ref[:, pl.ds(pl.multiple_of((2 * part + core) * half, 128), half)]
                for part in range(parts)
            ],
            axis=1,
        )

    for out_ref, core in ((keep_ref, core_ref[0]), (send_ref, 1 - core_ref[0])):
        grad = dot_tn(columns(core), right_ref[...]).astype(jnp.bfloat16)
        for part in range(parts):
            out_ref[part] = grad[part * half : (part + 1) * half]


def out_weight_grad(core, own_rows, grads, parts):
    rows, depth = grads.shape
    half = own_rows.shape[1] // parts // 2
    whole = pl.BlockSpec((rows, depth), lambda step, core: (0, 0))
    out = pl.BlockSpec((parts, half, depth), lambda step, core: (0, 0, 0))
    return pl.pallas_call(
        out_grad_kernel,
        grid_spec=pltpu.PrefetchScalarGridSpec(
            num_scalar_prefetch=1,
            grid=(1,),
            in_specs=[
                pl.BlockSpec(own_rows.shape, lambda step, core: (0, 0)), whole,
            ],
            out_specs=[out, out],
        ),
        out_shape=[jax.ShapeDtypeStruct((parts, half, depth), jnp.bfloat16)] * 2,
        compiler_params=pltpu.CompilerParams(dimension_semantics=("arbitrary",)),
        cost_estimate=COVER,
        name="out_weight_grad",
    )(core, own_rows, grads)


def normalize(inputs):
    center = inputs - jnp.mean(inputs, axis=-1, keepdims=True)
    spread = jnp.mean(center * center, axis=-1, keepdims=True)
    inverse = lax.rsqrt(spread + EPSILON)
    return center * inverse, inverse


def normalize_backward(grad, gain, unit, inverse):
    scaled_grad = grad * gain
    middle = jnp.mean(scaled_grad, axis=-1, keepdims=True)
    along = jnp.mean(scaled_grad * unit, axis=-1, keepdims=True)
    return (scaled_grad - middle - unit * along) * inverse


def dot_tn(left, right):
    return lax.dot_general(
        left, right, (((0,), (0,)), ((), ())), preferred_element_type=jnp.float32
    )


def copies_of(value, size):
    halves = [value[None]]
    for bit in bits_of(size):
        value = halves[0] if len(halves) == 1 else jnp.concatenate(halves)
        halves = [value, flip(value, "copy", bit)]
    return halves


def untangle(value, axis, index, size):
    for bit in bits_of(size):
        shape = value.shape
        split = value.reshape(
            shape[:axis] + (size // (2 * bit), 2, bit) + shape[axis + 1 :]
        )
        split = jnp.where((index // bit) % 2 == 1, jnp.flip(split, axis + 1), split)
        value = split.reshape(shape)
    return value


def orders(copies):
    first = [("copy", bit) for bit in bits_of(copies)] + [("team", 2)]
    return first, first[::-1] if copies == 2 else first


def spread_group(value, step, copies):
    choices = [order[step] for order in orders(copies)]
    moves = []
    for place in range(copies * TEAM):
        axis, bit = choices[place % 2]
        moves.append((place, place ^ (bit if axis == "team" else bit * TEAM)))
    got = lax.ppermute(value, ("copy", "team"), moves)
    mine = [(lax.axis_index(axis) // bit) % 2 for axis, bit in choices]
    mine = jnp.where(lax.axis_index("team") % 2 == 0, mine[0], mine[1])
    return jnp.where(mine == 0, jnp.stack([value, got]), jnp.stack([got, value]))


def place_in_group(step, copies):
    core, index = step // (2 * copies), step % (2 * copies)
    if copies != 2:
        return core, index // copies, index % copies
    outer, inner = index // 2, index % 2
    return core, outer + core * (inner - outer), inner + core * (outer - inner)


def exchange(blocks):
    return [blocks[0]] + [flip(blocks[k], "mp", k) for k in range(1, len(blocks))]


def cotangent_kernel(grad_a, grad_b, weight_a, weight_b, normed_ref, line_ref, out_ref, sum_ref):
    grad = sum(
        dot_nt(grad_ref[...], jnp.concatenate([weight_ref[slot] for slot in range(3)], axis=1))
        for grad_ref, weight_ref in ((grad_a, weight_a), (grad_b, weight_b))
    )
    unit = (normed_ref[...].astype(jnp.float32) - line_ref[0:1, :]) * line_ref[1:2, :]
    out_ref[...] = grad.astype(jnp.bfloat16)
    rows, depth = grad.shape
    both = jnp.concatenate(
        [
            jnp.sum((grad * unit).reshape(rows // 8, 8, depth), axis=0),
            jnp.sum(grad.reshape(rows // 8, 8, depth), axis=0),
        ],
        axis=0,
    )

    @pl.when(pl.program_id(0) == 0)
    def _():
        sum_ref[...] = both

    @pl.when(pl.program_id(0) > 0)
    def _():
        sum_ref[...] += both


def input_cotangent(grads, weights, normed, lines):
    length, width = grads[0].shape
    depth = weights.shape[1]
    row = pl.BlockSpec((BLK, width), lambda step: (step, 0))
    part_a = pl.BlockSpec((3, depth, width // 3), lambda step: (0, 0, 0))
    part_b = pl.BlockSpec((3, depth, width // 3), lambda step: (0, 0, 1))
    return pl.pallas_call(
        cotangent_kernel,
        grid=(length // BLK,),
        in_specs=[
            row, row, part_a, part_b,
            pl.BlockSpec((BLK, depth), lambda step: (step, 0)),
            pl.BlockSpec((2, depth), lambda step: (0, 0)),
        ],
        out_specs=[
            pl.BlockSpec((BLK, depth), lambda step: (step, 0)),
            pl.BlockSpec((16, depth), lambda step: (0, 0)),
        ],
        out_shape=[
            jax.ShapeDtypeStruct((length, depth), jnp.bfloat16),
            jax.ShapeDtypeStruct((16, depth), jnp.float32),
        ],
        compiler_params=pltpu.CompilerParams(dimension_semantics=("arbitrary",)),
        cost_estimate=SMALL,
        name="input_cotangent",
    )(*grads, weights, weights, normed, lines)


def feed_kernel(*refs, unit, count):
    weight_refs = refs[:count]
    (
        bias_ref, second_ref, grad_ref,
        act_ref, pre_ref, back_own, back_other, out_own, out_other, sum_ref,
    ) = refs[count:]
    w_up, w_down = (
        jnp.concatenate(
            [
                ref[:, start : start + unit, :].reshape(ref.shape[0] * unit, ref.shape[2])
                for ref in weight_refs
            ]
        )
        for start in (0, unit)
    )
    pre = dot_nt(second_ref[...], w_up) + bias_ref[...]
    grad_act = dot_nt(grad_ref[...], w_down)
    cdf = 0.5 + 0.5 * lax.erf(pre * 0.7071067811865476)
    pdf = jnp.exp(pre * pre * -0.5) * 0.3989422804014327
    active = (pre * cdf).astype(jnp.bfloat16)
    grad_pre = ((cdf + pre * pdf) * grad_act).astype(jnp.bfloat16)
    act_ref[...] = active
    pre_ref[...] = grad_pre
    line = jnp.sum(grad_pre.astype(jnp.float32), axis=0, keepdims=True)
    back = dot_nn(grad_pre, w_up).astype(jnp.bfloat16)
    out = dot_nn(active, w_down).astype(jnp.bfloat16)

    step = pl.program_id(0)
    middle = pl.num_programs(0) // 2

    @pl.when(step < middle)
    def _():
        back_own[...] = back
        out_own[...] = out

    @pl.when(step >= middle)
    def _():
        back_other[...] = back
        out_other[...] = out

    @pl.when(step == 0)
    def _():
        sum_ref[...] = line

    @pl.when(step > 0)
    def _():
        sum_ref[...] += line


def feed_forward(weights, bias_row, second, grad, unit):
    depth = weights[0].shape[2]
    rows = second.shape[0]
    width = unit * sum(one.shape[0] for one in weights)
    steps = FEED_STEPS
    take = rows // steps
    middle = steps // 2
    row = pl.BlockSpec((take, depth), lambda step: (step, 0))
    near = pl.BlockSpec((take, depth), lambda step: (jnp.minimum(step, middle - 1), 0))
    far = pl.BlockSpec((take, depth), lambda step: (jnp.maximum(step - middle, 0), 0))
    wide = pl.BlockSpec((take, width), lambda step: (step, 0))
    line = pl.BlockSpec((1, width), lambda step: (0, 0))
    part = jax.ShapeDtypeStruct((rows // 2, depth), jnp.bfloat16)
    return pl.pallas_call(
        functools.partial(feed_kernel, unit=unit, count=len(weights)),
        grid=(steps,),
        in_specs=[pl.BlockSpec(each.shape, lambda step: (0, 0, 0)) for each in weights]
        + [line, row, row],
        out_specs=[wide, wide, near, far, near, far, line],
        out_shape=[
            jax.ShapeDtypeStruct((rows, width), jnp.bfloat16),
            jax.ShapeDtypeStruct((rows, width), jnp.bfloat16),
            part, part, part, part,
            jax.ShapeDtypeStruct((1, width), jnp.float32),
        ],
        compiler_params=pltpu.CompilerParams(
            dimension_semantics=("arbitrary",), vmem_limit_bytes=48 * 1024 * 1024
        ),
        cost_estimate=LIGHT,
        name="feed_forward",
    )(*weights, bias_row, second, grad)


def weight_grad_kernel(
    part_ref, act_a, act_b, pre_a, pre_b, second_a, second_b, grad_a, grad_b, *out_refs
):
    _, places, _, unit, _ = out_refs[0].shape
    up = dot_tn(pre_a[...], second_a[...]) + dot_tn(pre_b[...], second_b[...])
    down = dot_tn(act_a[...], grad_a[...]) + dot_tn(act_b[...], grad_b[...])
    for index, out_ref in enumerate(out_refs):
        for place in range(places):
            start = (index * places + place) * unit
            out_ref[0, place, 0] = up[start : start + unit].astype(jnp.bfloat16)
            out_ref[0, place, 1] = down[start : start + unit].astype(jnp.bfloat16)


def weight_grads(part, acts, pres, seconds, grads, parts, copies):
    rows, width = acts[0].shape
    depth = seconds[0].shape[1]
    unit = width // (parts * copies)
    count = 2 if copies > 1 else 1
    places = copies // count
    column = pl.BlockSpec((rows, width // parts), lambda step, part: (0, step))
    whole = pl.BlockSpec((rows, depth), lambda step, part: (0, 0))
    out = pl.BlockSpec(
        (1, places, 2, unit, depth), lambda step, part: (part[0] ^ step, 0, 0, 0, 0)
    )
    return pl.pallas_call(
        weight_grad_kernel,
        grid_spec=pltpu.PrefetchScalarGridSpec(
            num_scalar_prefetch=1,
            grid=(parts,),
            in_specs=[column] * 4 + [whole] * 4,
            out_specs=[out] * count,
        ),
        out_shape=[jax.ShapeDtypeStruct((parts, places, 2, unit, depth), jnp.bfloat16)] * count,
        compiler_params=pltpu.CompilerParams(
            dimension_semantics=("arbitrary",), vmem_limit_bytes=56 * 1024 * 1024
        ),
        cost_estimate=HEAVY,
        name="weight_grads",
    )(part, *acts, *pres, *seconds, *grads)


def fold_copies(halves, got):
    if len(halves) == 1:
        return halves[0]
    value = halve_end((halves[0], got))
    while value.shape[1] > 1:
        half = value.shape[1] // 2
        value = halve_end((value[:, :half], flip(value[:, half:], "copy", half)))
    return value


def sync(*values):
    return lax.optimization_barrier(values)


def body(
    tokens, seg_ids, bucket_of, ln1_gain, ln1_bias, w_qkv, rel_table, w_out,
    ln2_gain, ln2_bias, w_up, up_bias, w_down, down_bias, out_grad,
):
    low = jnp.bfloat16
    wide = jnp.float32
    copies = lax.axis_size("copy")
    parts = lax.axis_size("mp")
    copy = lax.axis_index("copy")
    member = lax.axis_index("team")
    part = lax.axis_index("mp")
    core = member % 2
    rows, depth = tokens.shape
    head_width = w_out.shape[0]
    pair_width = head_width // 2
    pairs = 2
    team_units = w_up.shape[1] // TEAM
    unit = team_units // copies
    out_rows = head_width // (2 * copies)
    seg_row = seg_ids[0]
    to_right = [(i, i + 1) for i in range(parts - 1)]
    to_left = [(i + 1, i) for i in range(parts - 1)]

    def relay(right, left, step):
        return (
            lax.ppermute(right, "mp", to_right[step - 1 :]),
            lax.ppermute(left, "mp", to_left[: parts - step]),
        )

    def corner_of(right1, left1, right3, left3):
        return jnp.where(
            (part == 0) | (part == parts - 1), right3 + left3, jnp.where(part == 1, left1, right1)
        )

    x_part = tokens.astype(wide)
    unit1, inverse1 = normalize(x_part)
    normed = lax.all_gather(
        (unit1 * ln1_gain + ln1_bias).astype(low), "mp", axis=0, tiled=True
    )
    def own_units(place):
        first = member * team_units + (copy ^ place) * unit
        return jnp.concatenate(
            [
                jnp.transpose(lax.dynamic_slice_in_dim(w_up, first, unit, 1)),
                lax.dynamic_slice_in_dim(w_down, first, unit, 0),
            ]
        )

    own_slot = jnp.stack([own_units(place) for place in range(copies)])
    out_own = lax.dynamic_slice_in_dim(w_out, (copy * 2 + core) * out_rows, out_rows, 0)
    own_biases = [
        lax.dynamic_slice_in_dim(up_bias, member * team_units + (copy ^ place) * unit, unit, 0)
        for place in range(copies)
    ]
    high = lax.reduce_precision(own_biases[0], 8, 7)
    middle = lax.reduce_precision(own_biases[0] - high, 8, 7)
    bias_lines = jnp.stack([high, middle, own_biases[0] - high - middle]).astype(low)
    bias_lines = jnp.pad(bias_lines, ((0, 5), (0, depth - unit)))
    piece = jnp.concatenate([own_slot[0], out_own, bias_lines])
    w_right1, w_left1 = relay(piece, piece, 1)
    w_right2, w_left2 = relay(w_right1, w_left1, 2)
    beside = copies_of(jnp.where(part % 2 == 0, w_left1, w_right1), copies)
    grad_across = flip(out_grad, "team", 2)
    grad_near = with_partner(out_grad)
    grad_far = with_partner(grad_across)
    hot, by_distance = distance_bias(rel_table, bucket_of)
    forward_bias, backward_bias = near_tables(by_distance)
    cut = jnp.sum((seg_row == seg_row[0]).astype(jnp.int32)).reshape(1)
    normed = after(
        normed, grad_near, grad_far, own_slot, forward_bias, backward_bias, cut,
        w_right2, w_left2, beside[1],
    )

    def whole_out(halves):
        mine = jnp.concatenate([half[:, 2 * unit : 2 * unit + out_rows] for half in halves])
        mine = untangle(mine, 0, copy, copies)
        other = flip(mine, "team", 1)
        return jnp.where(
            core == 0, jnp.stack([mine, other], axis=1), jnp.stack([other, mine], axis=1)
        ).reshape(head_width, depth)

    w_right2, w_left2 = after(w_right2, normed), after(w_left2, normed)
    w_right3, w_left3 = relay(w_right2, w_left2, 3)
    across = copies_of(w_right2 + w_left2, copies)
    *results, = attention_forward(cut, after(normed, across[0]), w_qkv, forward_bias)
    projected, attended, logs = results[0:2], results[2], results[3:5]
    w_right3, w_left3, across[1], attended = sync(w_right3, w_left3, across[1], attended)
    corner = copies_of(corner_of(w_right1, w_left1, w_right3, w_left3), copies)
    stack = attended.reshape(parts, rows, head_width)
    moved = exchange(
        [lax.dynamic_index_in_dim(stack, part ^ k, 0, keepdims=False) for k in range(parts)]
    )
    w_out_full = jnp.concatenate(
        [w_out] + [whole_out(halves) for halves in (beside, across, corner)]
    )
    weights = [own_slot] + beside + across + corner
    bias_row = jnp.concatenate(
        own_biases
        + [
            jnp.sum(half[:, -8:-5, :unit].astype(wide), axis=1).reshape(-1)
            for half in weights[1:]
        ]
    )[None]

    hidden_in, second, own_rows = branch_and_norm(
        moved, w_out_full, tokens, jnp.stack([ln2_gain, ln2_bias])
    )
    second_across = flip(second, "team", 2)
    second_near = with_partner(second)
    act_near, pre_near, back_own, back_core, feed_own, feed_core, sums_near = feed_forward(
        weights, bias_row, second_near, grad_near, unit
    )
    second_across = after(second_across, back_own)
    back_core = flip(back_core, "team", 1)
    second_far = with_partner(second_across)
    act_far, pre_far, back_side, back_corner, feed_side, feed_corner, sums_far = feed_forward(
        weights, bias_row, second_far, grad_far, unit
    )
    onward = (
        back_side.astype(wide) + flip(back_corner, "team", 1).astype(wide)
    ).astype(low)
    back_across = flip(onward, "team", 2)
    feed_stack = jnp.stack([after(feed_corner, onward), feed_core])
    feed_beside = flip(feed_stack, "team", 1)
    ff_grads = weight_grads(
        part.reshape(1), (act_near, after(act_far, onward, feed_stack)), (pre_near, pre_far),
        (second_near, second_far), (grad_near, grad_far), parts, copies,
    )
    ff_got = flip(ff_grads[-1], "copy", max(1, copies // 2)) if copies > 1 else ff_grads[0]
    back_across = after(back_across, ff_grads[0])
    grad_hidden, grad_branch, *grad_rows = row_grads(
        (back_own, back_core, back_across), out_grad, hidden_in, w_out_full, ln2_gain[None], parts
    )
    row_sums = grad_rows.pop()
    received = exchange(grad_rows)
    wout_keep, wout_send = out_weight_grad(core.reshape(1), own_rows, grad_branch, parts)
    received[0] = after(received[0], wout_keep)
    wout_got = flip(wout_send, "team", 1)
    results = sync(wout_got, feed_beside, ff_got, *received)
    wout_got, feed_beside, ff_got = results[:3]
    received = results[3:]
    wout_grad = halve_end((wout_keep, wout_got)).reshape(parts, 2, copies, -1, depth)
    wout_pair = halve_start(wout_grad, 1, "team", 2)
    ff_value = fold_copies(ff_grads, ff_got).reshape(parts, 2 * unit, depth)
    ff_piece = lax.psum_scatter(ff_value, "mp", scatter_dimension=0, tiled=False)
    feed_sum = (feed_side.astype(wide) + feed_beside[0].astype(wide)).astype(low)
    feed_across = flip(feed_sum, "team", 2)
    natural = jnp.zeros((parts, rows, head_width), low)
    for k in range(parts):
        natural = lax.dynamic_update_index_in_dim(natural, received[k], part ^ k, 0)
    grad_att = after(natural.reshape(parts * rows, head_width), wout_pair[0], feed_sum, ff_value)
    first_grads, last_grads, table_sums = attention_backward(
        cut, projected, grad_att, attended, logs, backward_bias
    )
    first_grads, last_grads, wout_last, feed_across = sync(
        first_grads, last_grads, wout_pair[1], feed_across
    )
    dqkv = [first_grads, last_grads]
    wout_grad = halve_end((wout_pair[0], wout_last))
    for bit in reversed(bits_of(copies)):
        wout_grad = wout_grad.reshape((parts, 2, -1) + wout_grad.shape[2:])
        wout_pair = halve_start(wout_grad, 1, "copy", bit)
        if bit > 1:
            wout_grad = halve_end(wout_pair)
    wout_keep, wout_last = wout_pair
    qkv_send, qkv_keep = qkv_weight_grad(
        core.reshape(1), normed, [after(dqkv[0], wout_keep), dqkv[1]]
    )
    wout_last, qkv_keep, qkv_send = sync(wout_last, qkv_keep, qkv_send)
    qkv_got = flip(qkv_send, "team", 1)
    wout_grad = halve_end((wout_keep, wout_last)).reshape(parts, -1, depth)
    dqkv[0], wout_grad = sync(dqkv[0], wout_grad)
    wout_got = flip(wout_grad[2:], "mp", 2)
    running, line_sums = input_cotangent(
        dqkv, w_qkv, normed,
        jnp.stack([after(ln1_bias, dqkv[0]), 1.0 / ln1_gain]),
    )
    grad_first = lax.psum_scatter(running, "mp", scatter_dimension=0, tiled=True).astype(wide)
    qkv_got, running, ff_piece = sync(qkv_got, running, ff_piece)
    qkv_grad = halve_end((qkv_keep, qkv_got))
    table_sums = after(table_sums, running)
    table_line = table_gradient(
        hot, table_sums[: table_sums.shape[0] // 2], table_sums[table_sums.shape[0] // 2 :]
    ).reshape(1, -1)
    table_all = lax.dynamic_update_slice_in_dim(
        jnp.zeros((parts, table_line.shape[1]), wide), table_line, part, 0
    )
    sums = (after(sums_near, running) + sums_far).reshape(parts, copies, unit)
    sums = untangle(untangle(sums, 0, part, parts), 1, copy, copies)
    up_sums = lax.dynamic_update_slice_in_dim(
        jnp.zeros((parts, TEAM * team_units), wide), sums.reshape(parts, team_units),
        member * team_units, 1,
    )
    early_lines = jnp.concatenate([row_sums[0:3].reshape(-1), up_sums.reshape(-1)])
    small = jnp.concatenate(
        [
            jnp.sum(line_sums[0:8], axis=0), jnp.sum(line_sums[8:16], axis=0),
            early_lines, table_all.reshape(-1),
        ]
    )
    small = jnp.pad(small, (0, -small.shape[0] % 1024)).reshape(-1, 1024)

    qkv_pair = halve_start(qkv_grad.reshape(2, copies, -1, qkv_grad.shape[1]), 0, "team", 2)
    ff_all = spread_group(ff_piece, 0, copies)
    small_got = flip(small, "team", 1)
    feed_own = feed_own.astype(wide) + feed_beside[1].astype(wide) + feed_across.astype(wide)
    layer_out = (hidden_in + feed_own + down_bias).astype(low)
    qkv_last, ff_all, small_got, layer_out, wout_got = sync(
        qkv_pair[1], ff_all, small_got, layer_out, wout_got
    )
    wout_grad = (wout_grad[:2].astype(wide) + wout_got.astype(wide)).astype(low)
    qkv_grad = halve_end((qkv_pair[0], qkv_last))
    small = small + small_got

    for bit in reversed(bits_of(copies)):
        qkv_grad = halve(qkv_grad.reshape((2, -1) + qkv_grad.shape[1:]), 0, "copy", bit)
    for step in range(1, len(orders(copies)[0])):
        ff_all = spread_group(ff_all, step, copies)
    wout_got = flip(wout_grad[1:], "mp", 1)
    small = small + flip(small, "mp", 1)
    wout_grad = (wout_grad[:1].astype(wide) + wout_got.astype(wide)).astype(low)
    wout_grad = wout_grad.reshape(-1, depth)
    qkv_grad = qkv_grad.reshape(-1, 3 * head_width)
    columns = [
        jnp.concatenate(
            [
                qkv_grad[:, (3 * pair + slot) * pair_width : (3 * pair + slot + 1) * pair_width]
                for pair in range(pairs)
            ],
            axis=1,
        )
        for slot in range(3)
    ] + [wout_grad[:, start : start + head_width] for start in range(0, depth, head_width)]
    flat, ff_all, small = sync(jnp.concatenate(columns), ff_all, small)

    ff_got = flip(ff_all, "team", 1)
    flat = spread_group(flat, 0, copies)
    small = small + flip(small, "mp", 2)
    flat, small, ff_got = sync(flat, small, ff_got)

    for step in range(1, len(orders(copies)[0])):
        flat = spread_group(flat, step, copies)
    small = small + flip(small, "team", 2)
    grad_up, grad_down = feed_grads_out(
        core.reshape(1), ff_all.reshape(2 * copies, 2, unit, depth),
        ff_got.reshape(2 * copies, 2, unit, depth), copies,
    )
    flat, small, grad_up, grad_down = sync(flat, small, grad_up, grad_down)

    flat_got = flip(flat, "team", 1)
    for bit in bits_of(copies):
        small = small + flip(small, "copy", bit)
    flat_got, small, grad_first = sync(flat_got, small, grad_first)
    grad_qkv, grad_wout = attention_grads_out(
        core.reshape(1), flat.reshape(2 * copies, -1, head_width),
        flat_got.reshape(2 * copies, -1, head_width), depth, head_width,
    )

    small = small.reshape(-1)
    lines = [small[index * depth : (index + 1) * depth] for index in range(5)]
    start = 5 * depth
    count = TEAM * team_units
    up_sums = small[start : start + parts * count].reshape(parts, count)
    grad_up_bias = lax.dynamic_index_in_dim(up_sums, part, 0, keepdims=False)
    start = start + parts * count
    count = rel_table.size
    table_all = small[start : start + parts * count].reshape(parts, count)
    grad_table = lax.dynamic_index_in_dim(table_all, part, 0, keepdims=False).reshape(
        rel_table.shape
    )

    grad_first = after(grad_first, grad_qkv, grad_wout)
    unit1, inverse1 = normalize(after(tokens, grad_first).astype(wide))
    grad_first_norm = normalize_backward(grad_first, ln1_gain, unit1, inverse1)
    grad_tokens = (grad_hidden + grad_first_norm).astype(low)
    return (
        layer_out, grad_tokens, lines[0], lines[1], grad_qkv, grad_table, grad_wout,
        lines[2], lines[3], grad_up, grad_up_bias, grad_down, lines[4],
    )


def solution(mesh):
    groups, parts = mesh.shape["dp"], mesh.shape["mp"]
    split = Mesh(
        mesh.devices.reshape(groups // TEAM, TEAM, parts), ("copy", "team", "mp")
    )
    every = ("copy", "team", "mp")
    return jax.shard_map(
        body,
        mesh=split,
        in_specs=(
            P(every, None), P(("copy", "team"), None), P(), P(), P(), P(None, None, "mp"),
            P(None, "mp"), P("mp", None), P(), P(), P(None, "mp"), P("mp"), P("mp", None), P(),
            P(every, None),
        ),
        out_specs=(
            P(every, None), P(every, None), P(), P(), P(None, None, "mp"), P(None, "mp"),
            P("mp", None), P(), P(), P(None, "mp"), P("mp"), P("mp", None), P(),
        ),
        check_vma=False,
    )
```

profile of v0, /device:TPU:0, one launch (start us, length us, event | category | flops | bytes accessed | tf_op | source)
XLA Modules:
  0.0 423.4 jit_solution(17790399885152589601)
XLA Ops:
  8.7 1.5 fusion.12
  16.6 5.0 %collective-permute-start = (bf16[328,1024]{1,0:T(8,128)(2,1)}, bf16[328,1024]{1,0:T(8,128)(2,1)S(1)}, u32[]{:S(2)}, u32[]{:S(2)}) collective-permute-start(bf16[328,1024]{1,0:T(8,128)(2,1)} %pad_maximum_fusion.3), channel_id=1, source_target_pairs={{0,1},{1,2},{2,3},{4,5},{5,6},{6,7},{8,9},{9,10},{10,11},{12,13},{... | collective-permute-start | bytes 2015240 | tf_op jit(solution)/shard_map/ppermute | solution.py:999
  22.8 1.6 collective-permute-start.3
  28.8 2.0 maximum_bitcast_fusion
  30.9 19.6 %collective-permute-done = bf16[328,1024]{1,0:T(8,128)(2,1)S(1)} collective-permute-done((bf16[328,1024]{1,0:T(8,128)(2,1)}, bf16[328,1024]{1,0:T(8,128)(2,1)S(1)}, u32[]{:S(2)}, u32[]{:S(2)}) %collective-permute-start) | collective-permute-done | bytes 671776 | tf_op jit(solution)/shard_map/ppermute | solution.py:999
  50.5 18.9 %collective-permute-done.5 = bf16[328,1024]{1,0:T(8,128)(2,1)} collective-permute-done((bf16[328,1024]{1,0:T(8,128)(2,1)}, bf16[328,1024]{1,0:T(8,128)(2,1)}, u32[]{:S(2)}, u32[]{:S(2)}) %collective-permute-start.5) | collective-permute-done | bytes 671776 | tf_op jit(solution)/shard_map/ppermute | solution.py:1000
  70.5 1.7 collective-permute-start.7
  72.9 2.4 pad_maximum_fusion.2.refs_0_
  77.5 2.1 constant_dynamic-update-slice_fusion.3
  80.8 5.4 %collective-permute-done.7.refs_2_ = bf16[1,328,1024]{2,1,0:T(8,128)(2,1)S(1)} collective-permute-done((bf16[1,328,1024]{2,1,0:T(8,128)(2,1)S(1)}, bf16[1,328,1024]{2,1,0:T(8,128)(2,1)S(1)}, u32[]{:S(2)}, u32[]{:S(2)}) %collective-permute-start.7) | collective-permute-done | bytes 671776 | tf_op jit(solution)/shard_map/ppermute | solution.py:413
  88.2 16.2 %collective-permute-done.6 = bf16[328,1024]{1,0:T(8,128)(2,1)} collective-permute-done((bf16[328,1024]{1,0:T(8,128)(2,1)}, bf16[328,1024]{1,0:T(8,128)(2,1)}, u32[]{:S(2)}, u32[]{:S(2)}) %collective-permute-start.6) | collective-permute-done | bytes 671776 | tf_op jit(solution)/shard_map/ppermute | solution.py:1000
  108.3 1.5 collective-permute-start.10
  110.1 24.5 %attention_forward.1 = (bf16[1536,384]{1,0:T(8,128)(2,1)S(1)}, bf16[1536,384]{1,0:T(8,128)(2,1)S(1)}, bf16[1536,256]{1,0:T(8,128)(2,1)S(1)}, f32[8,1536]{1,0:T(8,128)S(1)}, f32[8,1536]{1,0:T(8,128)S(1)}) custom-call(s32[1]{0:T(128)} %bitcast.10.cut_ref, bf16[1536,1024]{1,0:T(8,128)(2,1)} %all-gather.2.cloned.1.call-done.rows_ref.normed_ref, ...), custom_call_target="tpu_custom_call" | custom-call | flops 1 | bytes 1 | tf_op jit(solution)/shard_map/attention_forward/pallas_call | solution.py:167
  136.8 3.3 collective-permute-start.11
  140.2 2.4 collective-permute-start.13
  142.7 10.0 %collective-permute-done.16.refs_6_ = bf16[1,328,1024]{2,1,0:T(8,128)(2,1)S(1)} collective-permute-done((bf16[1,328,1024]{2,1,0:T(8,128)(2,1)S(1)}, bf16[1,328,1024]{2,1,0:T(8,128)(2,1)S(1)}, u32[]{:S(2)}, u32[]{:S(2)}) %collective-permute-start.16) | collective-permute-done | bytes 671776 | tf_op jit(solution)/shard_map/ppermute | solution.py:413
  154.7 2.6 collective-permute-done.12.refs_2_
  159.6 1.5 collective-permute-start.20
  163.1 13.1 %feed_forward.2 = (bf16[768,1024]{1,0:T(8,128)(2,1)}, bf16[768,1024]{1,0:T(8,128)(2,1)}, bf16[384,1024]{1,0:T(8,128)(2,1)S(1)}, bf16[384,1024]{1,0:T(8,128)(2,1)...) custom-call(bf16[2,256,1024]{2,1,0:T(8,128)(2,1)} %pad_maximum_fusion.2.refs_0_, ...), custom_call_target="tpu_custom_call" | custom-call | flops 1 | bytes 1 | tf_op jit(solution)/shard_map/feed_forward/pallas_call | solution.py:899
  176.2 3.4 collective-permute-done.20
  179.7 2.2 collective-permute-done.21
  183.1 13.0 %feed_forward.3 = (bf16[768,1024]{1,0:T(8,128)(2,1)}, bf16[768,1024]{1,0:T(8,128)(2,1)}, bf16[384,1024]{1,0:T(8,128)(2,1)S(1)}, bf16[384,1024]{1,0:T(8,128)(2,1)...) custom-call(bf16[2,256,1024]{2,1,0:T(8,128)(2,1)} %pad_maximum_fusion.2.refs_0_, ...), custom_call_target="tpu_custom_call" | custom-call | flops 1 | bytes 1 | tf_op jit(solution)/shard_map/feed_forward/pallas_call | solution.py:899
  196.7 1.8 collective-permute-done.22
  198.7 1.5 collective-permute-start.23
  201.6 12.2 %weight_grads.1 = (bf16[4,1,2,128,1024]{4,3,2,1,0:T(8,128)(2,1)}, bf16[4,1,2,128,1024]{4,3,2,1,0:T(8,128)(2,1)}) custom-call(s32[1]{0:T(128)} %bitcast.31.part_ref, bf16[768,1024]{1,0:T(8,128)(2,1)} %get-tuple-element.130.act_a, bf16[768,1024]{1,0:T(8,128)(2,1)} %get-tuple-element.135.act_b, bf16[768,1024]{1,0:T(8,128)(2,1)} %get-tuple-element.136.pre_a, ...), custom_call_target="tpu_custom_call" | custom-call | flops 99999997952 | bytes 1 | tf_op jit(solution)/shard_map/weight_grads/pallas_call | solution.py:943
  213.8 1.5 collective-permute-start.26
  215.2 3.3 collective-permute-done.23.across_ref
  218.5 3.4 row_grads.1
  224.0 3.7 out_weight_grad.1
  227.6 4.0 collective-permute-start.27
  231.7 8.5 %collective-permute-done.27 = bf16[384,256]{1,0:T(8,128)(2,1)S(1)} collective-permute-done((bf16[384,256]{1,0:T(8,128)(2,1)S(1)}, bf16[384,256]{1,0:T(8,128)(2,1)S(1)}, u32[]{:S(2)}, u32[]{:S(2)}) %collective-permute-start.27) | collective-permute-done | bytes 196640 | tf_op jit(solution)/shard_map/ppermute | solution.py:413
  240.1 2.5 collective-permute-start.29
  242.7 2.0 collective-permute-done.28
  244.7 4.2 collective-permute-done.29
  248.9 13.2 %collective-permute-done.26 = bf16[4,1,2,128,1024]{4,3,2,1,0:T(8,128)(2,1)} collective-permute-done((bf16[4,1,2,128,1024]{4,3,2,1,0:T(8,128)(2,1)}, bf16[4,1,2,128,1024]{4,3,2,1,0:T(8,128)(2,1)}, u32[]{:S(2)}, u32[]{:S(2)}) %collective-permute-start.26) | collective-permute-done | bytes 2097184 | tf_op jit(solution)/shard_map/ppermute | solution.py:413
  262.1 1.9 add_convert_fusion.1
  265.9 3.9 add_convert_fusion
  269.8 1.7 fusion.20
  274.0 31.4 %attention_backward.1 = (bf16[1536,384]{1,0:T(8,128)(2,1)S(1)}, bf16[1536,384]{1,0:T(8,128)(2,1)S(1)}, f32[8,512]{1,0:T(8,128)S(1)}) custom-call(s32[1]{0:T(128)} %bitcast.10.cut_ref, bf16[1536,384]{1,0:T(8,128)(2,1)S(1)} %copy-done.23, bf16[1536,384]{1,0:T(8,128)(2,1)} %copy-done.24, bf16[1536,256]{1,0:T(8,128)(2,1)S(1)} %bitcast.127, ...), custom_call_target="tpu_custom_call" | custom-call | flops 20000000000 | bytes 1 | tf_op jit(solution)/shard_map/attention_backward/pallas_call | solution.py:329
  307.4 1.5 add_convert_fusion.4
  308.9 1.6 collective-permute-start.32
  310.5 1.9 copy-done.3
  315.0 5.0 %qkv_weight_grad.1 = (bf16[512,768]{1,0:T(8,128)(2,1)}, bf16[512,768]{1,0:T(8,128)(2,1)S(1)}) custom-call(s32[1]{0:T(128)} %bitcast.core_ref, bf16[1536,1024]{1,0:T(8,128)(2,1)S(1)} %copy-done.3, bf16[1536,384]{1,0:T(8,128)(2,1)S(1)} %copy-done.6, bf16[1536,384]{1,0:T(8,128)(2,1)S(1)} %copy-done.8), custom_call_target="tpu_custom_call" | custom-call | flops 1 | bytes 1 | tf_op jit(solution)/shard_map/qkv_weight_grad/pallas_call | solution.py:587
  321.6 2.6 fusion.19
  324.2 8.6 %input_cotangent.1 = (bf16[1536,1024]{1,0:T(8,128)(2,1)}, f32[16,1024]{1,0:T(8,128)}) custom-call(bf16[1536,384]{1,0:T(8,128)(2,1)} %copy-done.5, bf16[1536,384]{1,0:T(8,128)(2,1)} %copy-done.7, bf16[3,1024,256]{2,1,0:T(8,128)(2,1)} %weight_b.1, bf16[3,1024,256]{2,1,0:T(8,128)(2,1)} %weight_b.1, ...), custom_call_target="tpu_custom_call" | custom-call | flops 1 | bytes 1 | tf_op jit(solution)/shard_map/input_cotangent/pallas_call | solution.py:815
  332.8 4.1 collective-permute-start.37
  342.0 5.7 %collective-permute-done.35 = bf16[256,1024]{1,0:T(8,128)(2,1)} collective-permute-done((bf16[256,1024]{1,0:T(8,128)(2,1)}, bf16[256,1024]{1,0:T(8,128)(2,1)}, u32[]{:S(2)}, u32[]{:S(2)}) %collective-permute-start.35) | collective-permute-done | bytes 524320 | tf_op jit(solution)/shard_map/ppermute | solution.py:766
  347.8 1.7 maximum_select_fusion.1
  349.5 2.7 collective-permute-done.34
  353.5 1.7 collective-permute-start.39
  355.4 1.6 collective-permute-start.38
  356.9 1.5 collective-permute-done.41
  358.4 4.9 %collective-permute-done.39 = bf16[1,32,1024]{2,1,0:T(8,128)(2,1)S(1)} collective-permute-done((bf16[1,32,1024]{2,1,0:T(8,128)(2,1)S(1)}, bf16[1,32,1024]{2,1,0:T(8,128)(2,1)S(1)}, u32[]{:S(2)}, u32[]{:S(2)}) %collective-permute-start.39) | collective-permute-done | bytes 65568 | tf_op jit(solution)/shard_map/ppermute | solution.py:413
  363.6 3.7 collective-permute-done.40
  367.6 7.0 %collective-permute-start.44 = (bf16[2,2,256,1024]{3,2,1,0:T(8,128)(2,1)S(1)}, bf16[2,2,256,1024]{3,2,1,0:T(8,128)(2,1)S(1)}, u32[]{:S(2)}, u32[]{:S(2)}) collective-permute-start(bf16[2,2,256,1024]{3,2,1,0:T(8,128)(2,1)S(1)} %maximum_select_fusion), channel_id=1, source_target_pairs={{0,4},{4,0},{8,12},{12,8},{1,5},{5,1},{9,13},{13,9},{2,6},{6,2},{1... | collective-permute-start | bytes 6291464 | tf_op jit(solution)/shard_map/ppermute | solution.py:413
  375.2 2.6 collective-permute-start.43
  377.8 9.0 %collective-permute-done.43 = f32[10,1024]{1,0:T(8,128)S(1)} collective-permute-done((f32[10,1024]{1,0:T(8,128)S(1)}, f32[10,1024]{1,0:T(8,128)S(1)}, u32[]{:S(2)}, u32[]{:S(2)}) %collective-permute-start.43) | collective-permute-done | bytes 40992 | tf_op jit(solution)/shard_map/ppermute | solution.py:413
  388.3 1.5 collective-permute-start.45
  390.3 6.2 %feed_grads_out.1 = (f32[1024,1024]{1,0:T(8,128)}, f32[1024,1024]{1,0:T(8,128)}) custom-call(s32[1]{0:T(128)} %bitcast.core_ref, bf16[4,2,128,1024]{3,2,1,0:T(8,128)(2,1)} %bitcast.133, bf16[4,2,128,1024]{3,2,1,0:T(8,128)(2,1)} %bitcast.142), custom_call_target="tpu_custom_call" | custom-call | flops 1 | bytes 1 | tf_op jit(solution)/shard_map/feed_grads_out/pallas_call | solution.py:490
  396.5 2.5 collective-permute-done.46
  399.8 1.4 maximum_select_fusion.2
  402.3 2.4 convert_element_type.217
  406.9 3.7 attention_grads_out.1
  414.0 2.9 fusion.10
  (336 shorter events, 66.0 us)
Async XLA Ops:
  7.2 17.2 %copy-start = (f32[32,4]{0,1:T(4,128)S(1)}, f32[32,4]{0,1:T(4,128)}, u32[]{:S(2)}) copy-start(f32[32,4]{0,1:T(4,128)} %param.21) | copy-start | bytes 1540
  7.2 97.2 %all-gather.2.cloned.1.call-start = ((), (), s32[]{:S(2)}) async-start(), calls=%async_computation.2 | async-start | bytes 3932160 | tf_op jit(solution)/shard_map/all_gather | solution.py:1010
  11.4 326.4 %reduce-scatter.3.cloned.1.call-start = ((), (), s32[]{:S(2)}) async-start(), calls=%async_computation.3 | async-start | bytes 2621440 | tf_op jit(solution)/shard_map/reduce_scatter | solution.py:1118
  12.6 11.8 %copy-start.58 = (s32[128]{0:T(128)S(1)}, s32[128]{0:T(128)}, u32[]{:S(2)}) copy-start(s32[128]{0:T(128)} %param.17) | copy-start | bytes 1540
  12.6 12.0 %copy-start.55 = (s32[1,1536]{1,0:T(1,128)S(1)}, s32[1,1536]{1,0:T(1,128)}, u32[]{:S(2)}) copy-start(s32[1,1536]{1,0:T(1,128)} %param.16) | copy-start | bytes 18436
  15.6 12.3 %copy-start.21 = (f32[1024]{0:T(1024)S(1)}, f32[1024]{0:T(1024)}, u32[]{:S(2)}) copy-start(f32[1024]{0:T(1024)} %param.23) | copy-start | bytes 12292
  15.7 12.3 %copy-start.56 = (f32[1024]{0:T(1024)S(1)}, f32[1024]{0:T(1024)}, u32[]{:S(2)}) copy-start(f32[1024]{0:T(1024)} %param.24) | copy-start | bytes 12292
  16.6 33.9 %collective-permute-start = (bf16[328,1024]{1,0:T(8,128)(2,1)}, bf16[328,1024]{1,0:T(8,128)(2,1)S(1)}, u32[]{:S(2)}, u32[]{:S(2)}) collective-permute-start(bf16[328,1024]{1,0:T(8,128)(2,1)} %pad_maximum_fusion.3), channel_id=1, source_target_pairs={{0,1},{1,2},{2,3},{4,5},{5,6},{6,7},{8,9},{9,10},{10,11},{12,13},{... | collective-permute-start | bytes 2015240 | tf_op jit(solution)/shard_map/ppermute | solution.py:999
  21.5 47.8 %collective-permute-start.5 = (bf16[328,1024]{1,0:T(8,128)(2,1)}, bf16[328,1024]{1,0:T(8,128)(2,1)}, u32[]{:S(2)}, u32[]{:S(2)}) collective-permute-start(bf16[328,1024]{1,0:T(8,128)(2,1)} %pad_maximum_fusion.3), channel_id=1, source_target_pairs={{1,0},{2,1},{3,2},{5,4},{6,5},{7,6},{9,8},{10,9},{11,10},{13,12},{... | collective-permute-start | bytes 2015240 | tf_op jit(solution)/shard_map/ppermute | solution.py:1000
  22.8 52.6 %collective-permute-start.3 = (bf16[384,1024]{1,0:T(8,128)(2,1)S(1)}, bf16[384,1024]{1,0:T(8,128)(2,1)}, u32[]{:S(2)}, u32[]{:S(2)}) collective-permute-start(bf16[384,1024]{1,0:T(8,128)(2,1)S(1)} %copy-done.11), channel_id=1, source_target_pairs={{0,8},{4,12},{8,0},{12,4},{1,9},{5,13},{9,1},{13,5},{2,10},{6,14},... | collective-permute-start | bytes 2359304 | tf_op jit(solution)/shard_map/ppermute | solution.py:413
  24.4 55.2 %collective-permute-start.2 = (bf16[384,1024]{1,0:T(8,128)(2,1)S(1)}, bf16[384,1024]{1,0:T(8,128)(2,1)}, u32[]{:S(2)}, u32[]{:S(2)}) collective-permute-start(bf16[384,1024]{1,0:T(8,128)(2,1)S(1)} %copy-done.11), channel_id=1, source_target_pairs={{0,4},{4,0},{8,12},{12,8},{1,5},{5,1},{9,13},{13,9},{2,6},{6,2},{1... | collective-permute-start | bytes 2359304 | tf_op jit(solution)/shard_map/ppermute | solution.py:413
  50.5 18.9 %copy-start.34 = (bf16[328,1024]{1,0:T(8,128)(2,1)}, bf16[328,1024]{1,0:T(8,128)(2,1)S(1)}, u32[]{:S(2)}) copy-start(bf16[328,1024]{1,0:T(8,128)(2,1)S(1)} %collective-permute-done) | copy-start | bytes 2015236
  70.5 15.7 %collective-permute-start.7 = (bf16[1,328,1024]{2,1,0:T(8,128)(2,1)S(1)}, bf16[1,328,1024]{2,1,0:T(8,128)(2,1)S(1)}, u32[]{:S(2)}, u32[]{:S(2)}) collective-permute-start(bf16[1,328,1024]{2,1,0:T(8,128)(2,1)S(1)} %select_bitcast_fusion.1.refs_1_), channel_id=1, source_target_pairs={{0,16},{16,0},{1,17},{17,1},{2,18},{18,2},{3,19},{19,3},{4,20},{20... | collective-permute-start | bytes 2015240 | tf_op jit(solution)/shard_map/ppermute | solution.py:413
  75.4 11.0 %collective-permute-start.4 = (bf16[384,1024]{1,0:T(8,128)(2,1)}, bf16[384,1024]{1,0:T(8,128)(2,1)S(1)}, u32[]{:S(2)}, u32[]{:S(2)}) collective-permute-start(bf16[384,1024]{1,0:T(8,128)(2,1)} %collective-permute-done.3), channel_id=1, source_target_pairs={{0,4},{4,0},{8,12},{12,8},{1,5},{5,1},{9,13},{13,9},{2,6},{6,2},{1... | collective-permute-start | bytes 2359304 | tf_op jit(solution)/shard_map/ppermute | solution.py:413
  75.5 11.9 %collective-permute-start.1 = (bf16[328,1024]{1,0:T(8,128)(2,1)S(1)}, bf16[328,1024]{1,0:T(8,128)(2,1)S(1)}, u32[]{:S(2)}, u32[]{:S(2)}) collective-permute-start(bf16[328,1024]{1,0:T(8,128)(2,1)S(1)} %copy-done.35), channel_id=1, source_target_pairs={{1,2},{2,3},{5,6},{6,7},{9,10},{10,11},{13,14},{14,15},{17,18},{18... | collective-permute-start | bytes 2015240 | tf_op jit(solution)/shard_map/ppermute | solution.py:999
  76.2 28.2 %collective-permute-start.6 = (bf16[328,1024]{1,0:T(8,128)(2,1)}, bf16[328,1024]{1,0:T(8,128)(2,1)}, u32[]{:S(2)}, u32[]{:S(2)}) collective-permute-start(bf16[328,1024]{1,0:T(8,128)(2,1)} %collective-permute-done.5), channel_id=1, source_target_pairs={{1,0},{2,1},{5,4},{6,5},{9,8},{10,9},{13,12},{14,13},{17,16},{18,1... | collective-permute-start | bytes 2015240 | tf_op jit(solution)/shard_map/ppermute | solution.py:1000
  86.2 21.1 %copy-start.9 = (bf16[1,328,1024]{2,1,0:T(8,128)(2,1)}, bf16[1,328,1024]{2,1,0:T(8,128)(2,1)S(1)}, u32[]{:S(2)}) copy-start(bf16[1,328,1024]{2,1,0:T(8,128)(2,1)S(1)} %collective-permute-done.7.refs_2_) | copy-start | bytes 2015236
  86.3 23.6 %collective-permute-start.14 = (bf16[2,64,1024]{2,1,0:T(8,128)(2,1)S(1)}, bf16[2,64,1024]{2,1,0:T(8,128)(2,1)S(1)}, u32[]{:S(2)}, u32[]{:S(2)}) collective-permute-start(bf16[2,64,1024]{2,1,0:T(8,128)(2,1)S(1)} %reverse_select_fusion.2), channel_id=1, source_target_pairs={{0,4},{4,0},{8,12},{12,8},{1,5},{5,1},{9,13},{13,9},{2,6},{6,2},{1... | collective-permute-start | bytes 786440 | tf_op jit(solution)/shard_map/ppermute | solution.py:413
  104.4 30.2 %collective-permute-start.9 = (bf16[328,1024]{1,0:T(8,128)(2,1)}, bf16[328,1024]{1,0:T(8,128)(2,1)S(1)}, u32[]{:S(2)}, u32[]{:S(2)}) collective-permute-start(bf16[328,1024]{1,0:T(8,128)(2,1)} %collective-permute-done.6), channel_id=1, source_target_pairs={{1,0},{5,4},{9,8},{13,12},{17,16},{21,20},{25,24},{29,28}} | collective-permute-start | bytes 2015240 | tf_op jit(solution)/shard_map/ppermute | solution.py:1000
  107.3 27.4 %collective-permute-start.8 = (bf16[328,1024]{1,0:T(8,128)(2,1)S(1)}, bf16[328,1024]{1,0:T(8,128)(2,1)S(1)}, u32[]{:S(2)}, u32[]{:S(2)}) collective-permute-start(bf16[328,1024]{1,0:T(8,128)(2,1)S(1)} %copy-done.47), channel_id=1, source_target_pairs={{2,3},{6,7},{10,11},{14,15},{18,19},{22,23},{26,27},{30,31}} | collective-permute-start | bytes 2015240 | tf_op jit(solution)/shard_map/ppermute | solution.py:999
  108.3 26.4 %collective-permute-start.10 = (bf16[1,328,1024]{2,1,0:T(8,128)(2,1)S(1)}, bf16[1,328,1024]{2,1,0:T(8,128)(2,1)S(1)}, u32[]{:S(2)}, u32[]{:S(2)}) collective-permute-start(bf16[1,328,1024]{2,1,0:T(8,128)(2,1)S(1)} %add_bitcast_fusion.refs_3_), channel_id=1, source_target_pairs={{0,16},{16,0},{1,17},{17,1},{2,18},{18,2},{3,19},{19,3},{4,20},{20... | collective-permute-start | bytes 2015240 | tf_op jit(solution)/shard_map/ppermute | solution.py:413
  110.0 24.6 %copy-start.36 = (bf16[328,1024]{1,0:T(8,128)(2,1)S(1)}, bf16[328,1024]{1,0:T(8,128)(2,1)}, u32[]{:S(2)}) copy-start(bf16[328,1024]{1,0:T(8,128)(2,1)} %copy-done.34) | copy-start | bytes 2015236
  136.0 16.7 %collective-permute-start.16 = (bf16[1,328,1024]{2,1,0:T(8,128)(2,1)S(1)}, bf16[1,328,1024]{2,1,0:T(8,128)(2,1)S(1)}, u32[]{:S(2)}, u32[]{:S(2)}) collective-permute-start(bf16[1,328,1024]{2,1,0:T(8,128)(2,1)S(1)} %select_bitcast_fusion.refs_5_), channel_id=1, source_target_pairs={{0,16},{16,0},{1,17},{17,1},{2,18},{18,2},{3,19},{19,3},{4,20},{20... | collective-permute-start | bytes 2015240 | tf_op jit(solution)/shard_map/ppermute | solution.py:413
  136.7 16.2 %collective-permute-start.15 = (bf16[2,64,1024]{2,1,0:T(8,128)(2,1)S(1)}, bf16[2,64,1024]{2,1,0:T(8,128)(2,1)S(1)}, u32[]{:S(2)}, u32[]{:S(2)}) collective-permute-start(bf16[2,64,1024]{2,1,0:T(8,128)(2,1)S(1)} %reverse_select_fusion.1), channel_id=1, source_target_pairs={{0,4},{4,0},{8,12},{12,8},{1,5},{5,1},{9,13},{13,9},{2,6},{6,2},{1... | collective-permute-start | bytes 786440 | tf_op jit(solution)/shard_map/ppermute | solution.py:413
  136.8 17.9 %collective-permute-start.11 = (bf16[384,256]{1,0:T(8,128)(2,1)S(1)}, bf16[384,256]{1,0:T(8,128)(2,1)S(1)}, u32[]{:S(2)}, u32[]{:S(2)}) collective-permute-start(bf16[384,256]{1,0:T(8,128)(2,1)S(1)} %get-tuple-element.255), channel_id=1, source_target_pairs={{0,1},{1,0},{2,3},{3,2},{4,5},{5,4},{6,7},{7,6},{8,9},{9,8},{10,11... | collective-permute-start | bytes 589832 | tf_op jit(solution)/shard_map/ppermute | solution.py:413
  140.2 17.1 %collective-permute-start.12 = (bf16[384,256]{1,0:T(8,128)(2,1)S(1)}, bf16[384,256]{1,0:T(8,128)(2,1)S(1)}, u32[]{:S(2)}, u32[]{:S(2)}) collective-permute-start(bf16[384,256]{1,0:T(8,128)(2,1)S(1)} %get-tuple-element.254), channel_id=1, source_target_pairs={{0,2},{1,3},{2,0},{3,1},{4,6},{5,7},{6,4},{7,5},{8,10},{9,11},{10,... | collective-permute-start | bytes 589832 | tf_op jit(solution)/shard_map/ppermute | solution.py:413
  140.2 17.1 %collective-permute-start.13 = (bf16[384,256]{1,0:T(8,128)(2,1)S(1)}, bf16[384,256]{1,0:T(8,128)(2,1)S(1)}, u32[]{:S(2)}, u32[]{:S(2)}) collective-permute-start(bf16[384,256]{1,0:T(8,128)(2,1)S(1)} %get-tuple-element.253), channel_id=1, source_target_pairs={{0,3},{1,2},{2,1},{3,0},{4,7},{5,6},{6,5},{7,4},{8,11},{9,10},{10,... | collective-permute-start | bytes 589832 | tf_op jit(solution)/shard_map/ppermute | solution.py:413
  152.8 1.6 collective-permute-start.17
  159.6 2.3 collective-permute-start.18
  159.6 20.0 %collective-permute-start.20 = (bf16[384,1024]{1,0:T(8,128)(2,1)S(1)}, bf16[384,1024]{1,0:T(8,128)(2,1)S(1)}, u32[]{:S(2)}, u32[]{:S(2)}) collective-permute-start(bf16[384,1024]{1,0:T(8,128)(2,1)S(1)} %get-tuple-element.124), channel_id=1, source_target_pairs={{0,8},{4,12},{8,0},{12,4},{1,9},{5,13},{9,1},{13,5},{2,10},{6,14},... | collective-permute-start | bytes 2359304 | tf_op jit(solution)/shard_map/ppermute | solution.py:413
  179.6 2.3 collective-permute-start.21
  196.1 2.4 collective-permute-start.22
  196.3 22.2 %collective-permute-start.19 = (bf16[384,1024]{1,0:T(8,128)(2,1)}, bf16[384,1024]{1,0:T(8,128)(2,1)S(1)}, u32[]{:S(2)}, u32[]{:S(2)}) collective-permute-start(bf16[384,1024]{1,0:T(8,128)(2,1)} %get-tuple-element.126), channel_id=1, source_target_pairs={{0,4},{4,0},{8,12},{12,8},{1,5},{5,1},{9,13},{13,9},{2,6},{6,2},{1... | collective-permute-start | bytes 2359304 | tf_op jit(solution)/shard_map/ppermute | solution.py:413
  198.7 19.8 %collective-permute-start.23 = (bf16[384,1024]{1,0:T(8,128)(2,1)S(1)}, bf16[384,1024]{1,0:T(8,128)(2,1)}, u32[]{:S(2)}, u32[]{:S(2)}) collective-permute-start(bf16[384,1024]{1,0:T(8,128)(2,1)S(1)} %add_convert_fusion.3), channel_id=1, source_target_pairs={{0,8},{4,12},{8,0},{12,4},{1,9},{5,13},{9,1},{13,5},{2,10},{6,14},... | collective-permute-start | bytes 2359304 | tf_op jit(solution)/shard_map/ppermute | solution.py:413
  201.6 47.3 %collective-permute-start.25 = (bf16[2,384,1024]{2,1,0:T(8,128)(2,1)}, bf16[2,384,1024]{2,1,0:T(8,128)(2,1)}, u32[]{:S(2)}, u32[]{:S(2)}) collective-permute-start(bf16[2,384,1024]{2,1,0:T(8,128)(2,1)} %pad_maximum_fusion.1), channel_id=1, source_target_pairs={{0,4},{4,0},{8,12},{12,8},{1,5},{5,1},{9,13},{13,9},{2,6},{6,2},{1... | collective-permute-start | bytes 4718600 | tf_op jit(solution)/shard_map/ppermute | solution.py:413
  201.6 16.9 %copy-start.12 = (bf16[384,1024]{1,0:T(8,128)(2,1)S(1)}, bf16[384,1024]{1,0:T(8,128)(2,1)}, u32[]{:S(2)}) copy-start(bf16[384,1024]{1,0:T(8,128)(2,1)} %grad_ref.1) | copy-start | bytes 2359300
  201.6 16.9 %copy-start.20 = (bf16[384,1024]{1,0:T(8,128)(2,1)S(1)}, bf16[384,1024]{1,0:T(8,128)(2,1)}, u32[]{:S(2)}) copy-start(bf16[384,1024]{1,0:T(8,128)(2,1)} %copy-done.19) | copy-start | bytes 2359300
  213.8 48.4 %collective-permute-start.26 = (bf16[4,1,2,128,1024]{4,3,2,1,0:T(8,128)(2,1)}, bf16[4,1,2,128,1024]{4,3,2,1,0:T(8,128)(2,1)}, u32[]{:S(2)}, u32[]{:S(2)}) collective-permute-start(bf16[4,1,2,128,1024]{4,3,2,1,0:T(8,128)(2,1)} %get-tuple-element.144), channel_id=1, source_target_pairs={{0,16},{16,0},{1,17},{17,1},{2,18},{18,2},{3,19},{19,3},{4,20},{20... | collective-permute-start | bytes 6291464 | tf_op jit(solution)/shard_map/ppermute | solution.py:413
  227.6 21.3 %collective-permute-start.24 = (bf16[4,128,1024]{2,1,0:T(8,128)(2,1)}, bf16[4,128,1024]{2,1,0:T(8,128)(2,1)}, u32[]{:S(2)}, u32[]{:S(2)}) collective-permute-start(bf16[4,128,1024]{2,1,0:T(8,128)(2,1)} %get-tuple-element.143), channel_id=1, source_target_pairs={{0,4},{4,0},{8,12},{12,8},{1,5},{5,1},{9,13},{13,9},{2,6},{6,2},{1... | collective-permute-start | bytes 3145736 | tf_op jit(solution)/shard_map/ppermute | solution.py:413
  227.6 12.5 %collective-permute-start.27 = (bf16[384,256]{1,0:T(8,128)(2,1)S(1)}, bf16[384,256]{1,0:T(8,128)(2,1)S(1)}, u32[]{:S(2)}, u32[]{:S(2)}) collective-permute-start(bf16[384,256]{1,0:T(8,128)(2,1)S(1)} %get-tuple-element.147), channel_id=1, source_target_pairs={{0,1},{1,0},{2,3},{3,2},{4,5},{5,4},{6,7},{7,6},{8,9},{9,8},{10,11... | collective-permute-start | bytes 589832 | tf_op jit(solution)/shard_map/ppermute | solution.py:413
  231.7 13.0 %collective-permute-start.28 = (bf16[384,256]{1,0:T(8,128)(2,1)S(1)}, bf16[384,256]{1,0:T(8,128)(2,1)}, u32[]{:S(2)}, u32[]{:S(2)}) collective-permute-start(bf16[384,256]{1,0:T(8,128)(2,1)S(1)} %get-tuple-element.148), channel_id=1, source_target_pairs={{0,2},{1,3},{2,0},{3,1},{4,6},{5,7},{6,4},{7,5},{8,10},{9,11},{10,... | collective-permute-start | bytes 589832 | tf_op jit(solution)/shard_map/ppermute | solution.py:413
  240.1 8.7 %collective-permute-start.29 = (bf16[384,256]{1,0:T(8,128)(2,1)S(1)}, bf16[384,256]{1,0:T(8,128)(2,1)S(1)}, u32[]{:S(2)}, u32[]{:S(2)}) collective-permute-start(bf16[384,256]{1,0:T(8,128)(2,1)S(1)} %get-tuple-element.149), channel_id=1, source_target_pairs={{0,3},{1,2},{2,1},{3,0},{4,7},{5,6},{6,5},{7,4},{8,11},{9,10},{10,... | collective-permute-start | bytes 589832 | tf_op jit(solution)/shard_map/ppermute | solution.py:413
  248.9 15.2 %copy-start.48 = (bf16[384,256]{1,0:T(8,128)(2,1)}, bf16[384,256]{1,0:T(8,128)(2,1)S(1)}, u32[]{:S(2)}) copy-start(bf16[384,256]{1,0:T(8,128)(2,1)S(1)} %collective-permute-done.29) | copy-start | bytes 589828
  265.0 42.3 %collective-permute-start.30 = (bf16[4,2,32,1024]{3,2,0,1:T(8,128)(2,1)}, bf16[4,2,32,1024]{3,2,0,1:T(8,128)(2,1)}, u32[]{:S(2)}, u32[]{:S(2)}) collective-permute-start(bf16[4,2,32,1024]{3,2,0,1:T(8,128)(2,1)} %bitcast.125), channel_id=1, source_target_pairs={{0,8},{4,12},{8,0},{12,4},{1,9},{5,13},{9,1},{13,5},{2,10},{6,14},... | collective-permute-start | bytes 1572872 | tf_op jit(solution)/shard_map/ppermute | solution.py:413
  269.8 132.6 %reduce-scatter.5.cloned.1.call-start = ((), (), s32[]{:S(2)}) async-start(), calls=%async_computation.4 | async-start | bytes 3932160 | tf_op jit(solution)/shard_map/reduce_scatter | solution.py:1151
  271.6 35.8 %collective-permute-start.31 = (bf16[384,1024]{1,0:T(8,128)(2,1)S(1)}, bf16[384,1024]{1,0:T(8,128)(2,1)S(1)}, u32[]{:S(2)}, u32[]{:S(2)}) collective-permute-start(bf16[384,1024]{1,0:T(8,128)(2,1)S(1)} %fusion.20), channel_id=1, source_target_pairs={{0,8},{4,12},{8,0},{12,4},{1,9},{5,13},{9,1},{13,5},{2,10},{6,14},... | collective-permute-start | bytes 2359304 | tf_op jit(solution)/shard_map/ppermute | solution.py:413
  308.9 11.9 %collective-permute-start.32 = (bf16[4,1,32,1024]{3,2,0,1:T(8,128)(2,1)S(1)}, bf16[4,1,32,1024]{3,2,0,1:T(8,128)(2,1)S(1)}, u32[]{:S(2)}, u32[]{:S(2)}) collective-permute-start(bf16[4,1,32,1024]{3,2,0,1:T(8,128)(2,1)S(1)} %get-tuple-element.258), channel_id=1, source_target_pairs={{0,16},{16,0},{1,17},{17,1},{2,18},{18,2},{3,19},{19,3},{4,20},{20... | collective-permute-start | bytes 786440 | tf_op jit(solution)/shard_map/ppermute | solution.py:413
  320.9 16.9 %collective-permute-start.33 = (bf16[512,768]{1,0:T(8,128)(2,1)}, bf16[512,768]{1,0:T(8,128)(2,1)}, u32[]{:S(2)}, u32[]{:S(2)}) collective-permute-start(bf16[512,768]{1,0:T(8,128)(2,1)} %get-tuple-element.172), channel_id=1, source_target_pairs={{0,4},{4,0},{8,12},{12,8},{1,5},{5,1},{9,13},{13,9},{2,6},{6,2},{1... | collective-permute-start | bytes 2359304 | tf_op jit(solution)/shard_map/ppermute | solution.py:413
  332.8 16.7 %collective-permute-start.37 = (bf16[2,32,1024]{2,1,0:T(8,128)(2,1)S(1)}, bf16[2,32,1024]{2,1,0:T(8,128)(2,1)S(1)}, u32[]{:S(2)}, u32[]{:S(2)}) collective-permute-start(bf16[2,32,1024]{2,1,0:T(8,128)(2,1)S(1)} %slice.174), channel_id=1, source_target_pairs={{0,2},{1,3},{2,0},{3,1},{4,6},{5,7},{6,4},{7,5},{8,10},{9,11},{10,... | collective-permute-start | bytes 393224 | tf_op jit(solution)/shard_map/ppermute | solution.py:413
  338.2 9.6 %collective-permute-start.35 = (bf16[256,1024]{1,0:T(8,128)(2,1)}, bf16[256,1024]{1,0:T(8,128)(2,1)}, u32[]{:S(2)}, u32[]{:S(2)}) collective-permute-start(bf16[256,1024]{1,0:T(8,128)(2,1)} %bitcast.151), channel_id=1, source_target_pairs={{0,16},{4,12},{8,24},{12,4},{16,0},{20,28},{24,8},{28,20},{1,17},{... | collective-permute-start | bytes 1572872 | tf_op jit(solution)/shard_map/ppermute | solution.py:766
  340.1 12.1 %collective-permute-start.34 = (bf16[2,128,768]{2,1,0:T(8,128)(2,1)S(1)}, bf16[2,128,768]{2,1,0:T(8,128)(2,1)S(1)}, u32[]{:S(2)}, u32[]{:S(2)}) collective-permute-start(bf16[2,128,768]{2,1,0:T(8,128)(2,1)S(1)} %dynamic-slice_bitcast_fusion), channel_id=1, source_target_pairs={{0,8},{4,12},{8,0},{12,4},{1,9},{5,13},{9,1},{13,5},{2,10},{6,14},... | collective-permute-start | bytes 1179656 | tf_op jit(solution)/shard_map/ppermute | solution.py:413
  341.5 7.9 %collective-permute-start.36 = (f32[10,1024]{1,0:T(8,128)S(1)}, f32[10,1024]{1,0:T(8,128)S(1)}, u32[]{:S(2)}, u32[]{:S(2)}) collective-permute-start(f32[10,1024]{1,0:T(8,128)S(1)} %reshape.242), channel_id=1, source_target_pairs={{0,4},{4,0},{8,12},{12,8},{1,5},{5,1},{9,13},{13,9},{2,6},{6,2},{1... | collective-permute-start | bytes 122888 | tf_op jit(solution)/shard_map/ppermute | solution.py:413
  352.2 6.2 %collective-permute-start.41 = (f32[10,1024]{1,0:T(8,128)S(1)}, f32[10,1024]{1,0:T(8,128)S(1)}, u32[]{:S(2)}, u32[]{:S(2)}) collective-permute-start(f32[10,1024]{1,0:T(8,128)S(1)} %add.281), channel_id=1, source_target_pairs={{0,1},{1,0},{2,3},{3,2},{4,5},{5,4},{6,7},{7,6},{8,9},{9,8},{10,11... | collective-permute-start | bytes 122888 | tf_op jit(solution)/shard_map/ppermute | solution.py:413
  352.5 14.8 %collective-permute-start.40 = (bf16[2,256,1024]{2,1,0:T(8,128)(2,1)S(1)}, bf16[2,256,1024]{2,1,0:T(8,128)(2,1)S(1)}, u32[]{:S(2)}, u32[]{:S(2)}) collective-permute-start(bf16[2,256,1024]{2,1,0:T(8,128)(2,1)S(1)} %maximum_select_fusion.1), channel_id=1, source_target_pairs={{0,8},{4,20},{8,0},{12,28},{16,24},{20,4},{24,16},{28,12},{1,9},{5... | collective-permute-start | bytes 3145736 | tf_op jit(solution)/shard_map/ppermute | solution.py:766
  353.5 9.8 %collective-permute-start.39 = (bf16[1,32,1024]{2,1,0:T(8,128)(2,1)S(1)}, bf16[1,32,1024]{2,1,0:T(8,128)(2,1)S(1)}, u32[]{:S(2)}, u32[]{:S(2)}) collective-permute-start(bf16[1,32,1024]{2,1,0:T(8,128)(2,1)S(1)} %slice.218), channel_id=1, source_target_pairs={{0,1},{1,0},{2,3},{3,2},{4,5},{5,4},{6,7},{7,6},{8,9},{9,8},{10,11... | collective-permute-start | bytes 196616 | tf_op jit(solution)/shard_map/ppermute | solution.py:413
  355.4 8.0 %collective-permute-start.38 = (bf16[1,128,768]{2,1,0:T(8,128)(2,1)S(1)}, bf16[1,128,768]{2,1,0:T(8,128)(2,1)S(1)}, u32[]{:S(2)}, u32[]{:S(2)}) collective-permute-start(bf16[1,128,768]{2,1,0:T(8,128)(2,1)S(1)} %constant_dynamic-slice_fusion.2), channel_id=1, source_target_pairs={{0,16},{16,0},{1,17},{17,1},{2,18},{18,2},{3,19},{19,3},{4,20},{20... | collective-permute-start | bytes 589832 | tf_op jit(solution)/shard_map/ppermute | solution.py:413
  367.6 22.7 %copy-start.28 = (bf16[2,2,256,1024]{3,2,1,0:T(8,128)(2,1)}, bf16[2,2,256,1024]{3,2,1,0:T(8,128)(2,1)S(1)}, u32[]{:S(2)}) copy-start(bf16[2,2,256,1024]{3,2,1,0:T(8,128)(2,1)S(1)} %maximum_select_fusion) | copy-start | bytes 6291460
  367.6 19.3 %collective-permute-start.44 = (bf16[2,2,256,1024]{3,2,1,0:T(8,128)(2,1)S(1)}, bf16[2,2,256,1024]{3,2,1,0:T(8,128)(2,1)S(1)}, u32[]{:S(2)}, u32[]{:S(2)}) collective-permute-start(bf16[2,2,256,1024]{3,2,1,0:T(8,128)(2,1)S(1)} %maximum_select_fusion), channel_id=1, source_target_pairs={{0,4},{4,0},{8,12},{12,8},{1,5},{5,1},{9,13},{13,9},{2,6},{6,2},{1... | collective-permute-start | bytes 6291464 | tf_op jit(solution)/shard_map/ppermute | solution.py:413
  374.6 12.2 %collective-permute-start.42 = (bf16[512,256]{1,0:T(8,128)(2,1)S(1)}, bf16[512,256]{1,0:T(8,128)(2,1)S(1)}, u32[]{:S(2)}, u32[]{:S(2)}) collective-permute-start(bf16[512,256]{1,0:T(8,128)(2,1)S(1)} %constant_dynamic-update-slice_fusion.10), channel_id=1, source_target_pairs={{0,16},{4,12},{8,24},{12,4},{16,0},{20,28},{24,8},{28,20},{1,17},{... | collective-permute-start | bytes 786440 | tf_op jit(solution)/shard_map/ppermute | solution.py:766
  375.2 11.6 %collective-permute-start.43 = (f32[10,1024]{1,0:T(8,128)S(1)}, f32[10,1024]{1,0:T(8,128)S(1)}, u32[]{:S(2)}, u32[]{:S(2)}) collective-permute-start(f32[10,1024]{1,0:T(8,128)S(1)} %add.282), channel_id=1, source_target_pairs={{0,2},{1,3},{2,0},{3,1},{4,6},{5,7},{6,4},{7,5},{8,10},{9,11},{10,... | collective-permute-start | bytes 122888 | tf_op jit(solution)/shard_map/ppermute | solution.py:413
  388.3 11.5 %collective-permute-start.45 = (bf16[2,512,256]{2,1,0:T(8,128)(2,1)S(1)}, bf16[2,512,256]{2,1,0:T(8,128)(2,1)}, u32[]{:S(2)}, u32[]{:S(2)}) collective-permute-start(bf16[2,512,256]{2,1,0:T(8,128)(2,1)S(1)} %maximum_select_fusion.6), channel_id=1, source_target_pairs={{0,8},{4,20},{8,0},{12,28},{16,24},{20,4},{24,16},{28,12},{1,9},{5... | collective-permute-start | bytes 1572872 | tf_op jit(solution)/shard_map/ppermute | solution.py:766
  389.8 9.2 %collective-permute-start.46 = (f32[10,1024]{1,0:T(8,128)S(1)}, f32[10,1024]{1,0:T(8,128)}, u32[]{:S(2)}, u32[]{:S(2)}) collective-permute-start(f32[10,1024]{1,0:T(8,128)S(1)} %add.283), channel_id=1, source_target_pairs={{0,8},{4,12},{8,0},{12,4},{1,9},{5,13},{9,1},{13,5},{2,10},{6,14},... | collective-permute-start | bytes 122888 | tf_op jit(solution)/shard_map/ppermute | solution.py:413
  401.3 4.6 %collective-permute-start.47 = (bf16[2,2,512,256]{3,2,1,0:T(8,128)(2,1)S(1)}, bf16[2,2,512,256]{3,2,1,0:T(8,128)(2,1)S(1)}, u32[]{:S(2)}, u32[]{:S(2)}) collective-permute-start(bf16[2,2,512,256]{3,2,1,0:T(8,128)(2,1)S(1)} %maximum_select_fusion.2), channel_id=1, source_target_pairs={{0,4},{4,0},{8,12},{12,8},{1,5},{5,1},{9,13},{13,9},{2,6},{6,2},{1... | collective-permute-start | bytes 3145736 | tf_op jit(solution)/shard_map/ppermute | solution.py:413
  401.3 4.5 %collective-permute-start.48 = (f32[10,1024]{1,0:T(8,128)S(1)}, f32[10,1024]{1,0:T(8,128)S(1)}, u32[]{:S(2)}, u32[]{:S(2)}) collective-permute-start(f32[10,1024]{1,0:T(8,128)S(1)} %add.284), channel_id=1, source_target_pairs={{0,16},{16,0},{1,17},{17,1},{2,18},{18,2},{3,19},{19,3},{4,20},{20... | collective-permute-start | bytes 122888 | tf_op jit(solution)/shard_map/ppermute | solution.py:413
  (48 other events, 137.1 us)
Sparse Core Ops, SparseCore 0:
  11.6 84.5 all-gather.1
  269.9 45.2 reduce-scatter.2
  337.0 62.9 reduce-scatter.4
where the time goes:
time: 425 us; the launch traced here: 423 us
  waiting for transfers between devices  144 us (34%)
  Pallas kernels  126 us (30%)
  starting transfers between devices  61.1 us (14%)
  other arithmetic  41.1 us (10%)
  local copies, waits for them, and re-layouts  35.2 us (8%)
  between operations  15.1 us (4%)
    ppermute x39, waiting for transfers between devices, flip(): return lax.ppermute(value, axis, [(i, i ^ bit) for i in range(size)])  80.2 us
    ppermute x39, starting transfers between devices, flip(): return lax.ppermute(value, axis, [(i, i ^ bit) for i in range(size)])  46.7 us
    ppermute x3, waiting for transfers between devices, relay(): lax.ppermute(left, 'mp', to_left[:parts - step])  35.1 us
    pallas_call x1, Pallas kernels, attention_backward(): pl.pallas_call(attention_backward_kernel, grid_spec=pltpu.PrefetchScalarG...  31.4 us
    pallas_call x2, Pallas kernels, feed_forward(): pl.pallas_call(functools.partial(feed_kernel, unit=unit, count=len(weight...  26.1 us
    unnamed x141, local copies, waits for them, and re-layouts  24.6 us
    pallas_call x1, Pallas kernels, attention_forward(): pl.pallas_call(attention_forward_kernel, grid_spec=pltpu.PrefetchScalarGr...  24.5 us
    ppermute x3, waiting for transfers between devices, relay(): lax.ppermute(right, 'mp', to_right[step - 1:])  19.6 us
  transfers between devices with their start and end apart: 52, of which 24 were waited for; matrix products, arithmetic and copies ran while one was open for 11% of the time, Pallas kernels for 25%

commit v1 on v0

--- a/solution.py
+++ b/solution.py
@@ -12,9 +12,9 @@
 LIGHT = pl.CostEstimate(flops=1, bytes_accessed=1, transcendentals=0)
 MIDDLE = pl.CostEstimate(flops=2 * 10**10, bytes_accessed=1, transcendentals=0)
 SMALL = pl.CostEstimate(flops=1, bytes_accessed=1, transcendentals=0)
-COVER = pl.CostEstimate(flops=16 * 10**9, bytes_accessed=1, transcendentals=0)
+COVER = pl.CostEstimate(flops=1, bytes_accessed=1, transcendentals=0)
 HEAVY = pl.CostEstimate(flops=10**11, bytes_accessed=1, transcendentals=0)
-FEED_STEPS = 4
+FEED_STEPS = 2
 BLK = 256
 HEAD_LANES = 64
 NEAR = 128
@@ -186,9 +186,7 @@
         out_shape=[jax.ShapeDtypeStruct((length, 3 * width), jnp.bfloat16)] * 2
         + [jax.ShapeDtypeStruct((length, 2 * width), jnp.bfloat16)]
         + [jax.ShapeDtypeStruct((8, length), jnp.float32)] * 2,
-        compiler_params=pltpu.CompilerParams(
-            dimension_semantics=("arbitrary",), vmem_limit_bytes=48 * 1024 * 1024
-        ),
+        compiler_params=pltpu.CompilerParams(dimension_semantics=("arbitrary",)),
         cost_estimate=LIGHT,
         name="attention_forward",
     )(cut, normed, weights, near_bias)
@@ -353,9 +351,7 @@
             jax.ShapeDtypeStruct((length, 3 * width), jnp.bfloat16),
             jax.ShapeDtypeStruct((8, 2 * BLK), jnp.float32),
         ],
-        compiler_params=pltpu.CompilerParams(
-            dimension_semantics=("arbitrary",), vmem_limit_bytes=48 * 1024 * 1024
-        ),
+        compiler_params=pltpu.CompilerParams(dimension_semantics=("arbitrary",)),
         cost_estimate=MIDDLE,
         name="attention_backward",
     )(cut, *projected, grad_att, attended, *logs, near_bias)
@@ -558,7 +554,7 @@
             jax.ShapeDtypeStruct((head_width, depth), jnp.float32),
         ],
         compiler_params=pltpu.CompilerParams(dimension_semantics=("arbitrary",)),
-        cost_estimate=LIGHT,
+        cost_estimate=HEAVY,
         name="attention_grads_out",
     )(core, own, got)
 
@@ -596,12 +592,40 @@
             out_specs=[out, out],
         ),
         out_shape=[jax.ShapeDtypeStruct((half, 2 * width), jnp.bfloat16)] * 2,
-        compiler_params=pltpu.CompilerParams(
-            dimension_semantics=("arbitrary",), vmem_limit_bytes=40 * 1024 * 1024
-        ),
+        compiler_params=pltpu.CompilerParams(dimension_semantics=("arbitrary",)),
         cost_estimate=SMALL,
         name="qkv_weight_grad",
     )(core, rows, *grads)
+
+
+def first_norm_kernel(token_ref, line_ref, out_ref):
+    unit, _ = normalize(token_ref[...].astype(jnp.float32))
+    out_ref[...] = (unit * line_ref[0:1, :] + line_ref[1:2, :]).astype(jnp.bfloat16)
+
+
+def first_norm(tokens, lines):
+    return pl.pallas_call(
+        first_norm_kernel,
+        out_shape=jax.ShapeDtypeStruct(tokens.shape, jnp.bfloat16),
+        cost_estimate=LIGHT,
+        name="first_norm",
+    )(tokens, lines)
+
+
+def token_grads_kernel(grad_ref, hidden_ref, token_ref, line_ref, out_ref):
+    unit, inverse = normalize(token_ref[...].astype(jnp.float32))
+    grad = normalize_backward(grad_ref[...].astype(jnp.float32), line_ref[...], unit, inverse)
+    out_ref[...] = (hidden_ref[...] + grad).astype(jnp.bfloat16)
+
+
+def token_grads(grad, hidden, tokens, line):
+    return pl.pallas_call(
+        token_grads_kernel,
+        out_shape=jax.ShapeDtypeStruct(tokens.shape, jnp.bfloat16),
+        compiler_params=pltpu.CompilerParams(vmem_limit_bytes=32 * 1024 * 1024),
+        cost_estimate=LIGHT,
+        name="token_grads",
+    )(grad, hidden, tokens, line)
 
 
 def branch_kernel(*refs, count):
@@ -757,7 +781,15 @@
     return first, first[::-1] if copies == 2 else first
 
 
+def spread_end(value, got, mine):
+    return jnp.where(mine == 0, jnp.stack([value, got]), jnp.stack([got, value]))
+
+
 def spread_group(value, step, copies):
+    return spread_end(*spread_start(value, step, copies))
+
+
+def spread_start(value, step, copies):
     choices = [order[step] for order in orders(copies)]
     moves = []
     for place in range(copies * TEAM):
@@ -765,8 +797,7 @@
         moves.append((place, place ^ (bit if axis == "team" else bit * TEAM)))
     got = lax.ppermute(value, ("copy", "team"), moves)
     mine = [(lax.axis_index(axis) // bit) % 2 for axis, bit in choices]
-    mine = jnp.where(lax.axis_index("team") % 2 == 0, mine[0], mine[1])
-    return jnp.where(mine == 0, jnp.stack([value, got]), jnp.stack([got, value]))
+    return value, got, jnp.where(lax.axis_index("team") % 2 == 0, mine[0], mine[1])
 
 
 def place_in_group(step, copies):
@@ -1005,11 +1036,10 @@
             (part == 0) | (part == parts - 1), right3 + left3, jnp.where(part == 1, left1, right1)
         )
 
-    x_part = tokens.astype(wide)
-    unit1, inverse1 = normalize(x_part)
     normed = lax.all_gather(
-        (unit1 * ln1_gain + ln1_bias).astype(low), "mp", axis=0, tiled=True
-    )
+        first_norm(tokens, jnp.stack([ln1_gain, ln1_bias])), "mp", axis=0, tiled=True
+    )
+
     def own_units(place):
         first = member * team_units + (copy ^ place) * unit
         return jnp.concatenate(
@@ -1106,22 +1136,25 @@
     )
     row_sums = grad_rows.pop()
     received = exchange(grad_rows)
+    grad_branch, feed_beside, *received = sync(grad_branch, feed_beside, *received)
     wout_keep, wout_send = out_weight_grad(core.reshape(1), own_rows, grad_branch, parts)
-    received[0] = after(received[0], wout_keep)
     wout_got = flip(wout_send, "team", 1)
-    results = sync(wout_got, feed_beside, ff_got, *received)
-    wout_got, feed_beside, ff_got = results[:3]
-    received = results[3:]
-    wout_grad = halve_end((wout_keep, wout_got)).reshape(parts, 2, copies, -1, depth)
-    wout_pair = halve_start(wout_grad, 1, "team", 2)
-    ff_value = fold_copies(ff_grads, ff_got).reshape(parts, 2 * unit, depth)
-    ff_piece = lax.psum_scatter(ff_value, "mp", scatter_dimension=0, tiled=False)
     feed_sum = (feed_side.astype(wide) + feed_beside[0].astype(wide)).astype(low)
-    feed_across = flip(feed_sum, "team", 2)
     natural = jnp.zeros((parts, rows, head_width), low)
     for k in range(parts):
         natural = lax.dynamic_update_index_in_dim(natural, received[k], part ^ k, 0)
-    grad_att = after(natural.reshape(parts * rows, head_width), wout_pair[0], feed_sum, ff_value)
+    wout_grad = halve_end((wout_keep, wout_got)).reshape(parts, 2, copies, -1, depth)
+    side_bit = (member // 2) % 2
+    wout_keep = lax.dynamic_index_in_dim(wout_grad, side_bit, 1, keepdims=False)
+    wout_send = lax.dynamic_index_in_dim(wout_grad, 1 - side_bit, 1, keepdims=False)
+    ff_got, natural, feed_sum, wout_keep, wout_send = sync(
+        ff_got, natural, feed_sum, wout_keep, wout_send
+    )
+    ff_value = fold_copies(ff_grads, ff_got).reshape(parts, 2 * unit, depth)
+    ff_piece = lax.psum_scatter(ff_value, "mp", scatter_dimension=0, tiled=False)
+    wout_pair = (wout_keep, flip(wout_send, "team", 2))
+    feed_across = flip(feed_sum, "team", 2)
+    grad_att = natural.reshape(parts * rows, head_width)
     first_grads, last_grads, table_sums = attention_backward(
         cut, projected, grad_att, attended, logs, backward_bias
     )
@@ -1139,17 +1172,16 @@
     qkv_send, qkv_keep = qkv_weight_grad(
         core.reshape(1), normed, [after(dqkv[0], wout_keep), dqkv[1]]
     )
-    wout_last, qkv_keep, qkv_send = sync(wout_last, qkv_keep, qkv_send)
+    qkv_keep, qkv_send, dqkv[0] = sync(qkv_keep, qkv_send, dqkv[0])
     qkv_got = flip(qkv_send, "team", 1)
-    wout_grad = halve_end((wout_keep, wout_last)).reshape(parts, -1, depth)
-    dqkv[0], wout_grad = sync(dqkv[0], wout_grad)
-    wout_got = flip(wout_grad[2:], "mp", 2)
     running, line_sums = input_cotangent(
         dqkv, w_qkv, normed,
         jnp.stack([after(ln1_bias, dqkv[0]), 1.0 / ln1_gain]),
     )
-    grad_first = lax.psum_scatter(running, "mp", scatter_dimension=0, tiled=True).astype(wide)
-    qkv_got, running, ff_piece = sync(qkv_got, running, ff_piece)
+    grad_first = lax.psum_scatter(running, "mp", scatter_dimension=0, tiled=True)
+    qkv_got, running, ff_piece, wout_last = sync(qkv_got, running, ff_piece, wout_last)
+    wout_grad = halve_end((wout_keep, wout_last)).reshape(parts, -1, depth)
+    wout_blocks = exchange([wout_grad[k] for k in range(parts)])
     qkv_grad = halve_end((qkv_keep, qkv_got))
     table_sums = after(table_sums, running)
     table_line = table_gradient(
@@ -1175,24 +1207,32 @@
 
     qkv_pair = halve_start(qkv_grad.reshape(2, copies, -1, qkv_grad.shape[1]), 0, "team", 2)
     ff_all = spread_group(ff_piece, 0, copies)
-    small_got = flip(small, "team", 1)
+    small = small + flip(small, "team", 1)
+    small_got = flip(small, "team", 2)
     feed_own = feed_own.astype(wide) + feed_beside[1].astype(wide) + feed_across.astype(wide)
     layer_out = (hidden_in + feed_own + down_bias).astype(low)
-    qkv_last, ff_all, small_got, layer_out, wout_got = sync(
-        qkv_pair[1], ff_all, small_got, layer_out, wout_got
-    )
-    wout_grad = (wout_grad[:2].astype(wide) + wout_got.astype(wide)).astype(low)
+    qkv_last, ff_all, small_got, layer_out = sync(qkv_pair[1], ff_all, small_got, layer_out)
     qkv_grad = halve_end((qkv_pair[0], qkv_last))
     small = small + small_got
 
     for bit in reversed(bits_of(copies)):
-        qkv_grad = halve(qkv_grad.reshape((2, -1) + qkv_grad.shape[1:]), 0, "copy", bit)
-    for step in range(1, len(orders(copies)[0])):
+        qkv_pair = halve_start(qkv_grad.reshape((2, -1) + qkv_grad.shape[1:]), 0, "copy", bit)
+        if bit > 1:
+            qkv_grad = halve_end(qkv_pair)
+    if copies == 1:
+        qkv_pair = (qkv_grad, jnp.zeros_like(qkv_grad))
+    for step in range(1, len(orders(copies)[0]) - 1):
         ff_all = spread_group(ff_all, step, copies)
-    wout_got = flip(wout_grad[1:], "mp", 1)
-    small = small + flip(small, "mp", 1)
-    wout_grad = (wout_grad[:1].astype(wide) + wout_got.astype(wide)).astype(low)
-    wout_grad = wout_grad.reshape(-1, depth)
+    ff_own, ff_got, ff_mine = spread_start(ff_all, len(orders(copies)[0]) - 1, copies)
+    for bit in bits_of(copies)[1:]:
+        small = small + flip(small, "copy", bit)
+    small_got = flip(small, "copy", 1) if copies > 1 else jnp.zeros_like(small)
+    results = sync(qkv_pair[1], small_got, small, ff_got, *wout_blocks)
+    qkv_last, small_got, small, ff_got = results[:4]
+    ff_all = spread_end(ff_own, ff_got, ff_mine)
+    small = small + small_got
+    qkv_grad = halve_end((qkv_pair[0], qkv_last))
+    wout_grad = sum(one.astype(wide) for one in results[4:]).astype(low)
     qkv_grad = qkv_grad.reshape(-1, 3 * head_width)
     columns = [
         jnp.concatenate(
@@ -1204,31 +1244,35 @@
         )
         for slot in range(3)
     ] + [wout_grad[:, start : start + head_width] for start in range(0, depth, head_width)]
-    flat, ff_all, small = sync(jnp.concatenate(columns), ff_all, small)
-
+    flat = jnp.concatenate(columns)
     ff_got = flip(ff_all, "team", 1)
     flat = spread_group(flat, 0, copies)
-    small = small + flip(small, "mp", 2)
-    flat, small, ff_got = sync(flat, small, ff_got)
+    flat, ff_got = sync(flat, ff_got)
 
     for step in range(1, len(orders(copies)[0])):
         flat = spread_group(flat, step, copies)
-    small = small + flip(small, "team", 2)
     grad_up, grad_down = feed_grads_out(
         core.reshape(1), ff_all.reshape(2 * copies, 2, unit, depth),
         ff_got.reshape(2 * copies, 2, unit, depth), copies,
     )
-    flat, small, grad_up, grad_down = sync(flat, small, grad_up, grad_down)
-
+    flat, grad_up, grad_down = sync(flat, grad_up, grad_down)
+
+    flat, small, grad_first = sync(flat, small, grad_first)
     flat_got = flip(flat, "team", 1)
-    for bit in bits_of(copies):
-        small = small + flip(small, "copy", bit)
-    flat_got, small, grad_first = sync(flat_got, small, grad_first)
+    small_got = flip(small, "mp", 1)
+    flat_got, small_got = sync(flat_got, small_got)
+    small = small + small_got
+    small_got = flip(small, "mp", 2)
     grad_qkv, grad_wout = attention_grads_out(
         core.reshape(1), flat.reshape(2 * copies, -1, head_width),
         flat_got.reshape(2 * copies, -1, head_width), depth, head_width,
     )
 
+    grad_tokens = token_grads(grad_first, grad_hidden, tokens, ln1_gain[None])
+    small_got, grad_qkv, grad_wout, grad_tokens = sync(
+        small_got, grad_qkv, grad_wout, grad_tokens
+    )
+    small = small + small_got
     small = small.reshape(-1)
     lines = [small[index * depth : (index + 1) * depth] for index in range(5)]
     start = 5 * depth
@@ -1242,10 +1286,6 @@
         rel_table.shape
     )
 
-    grad_first = after(grad_first, grad_qkv, grad_wout)
-    unit1, inverse1 = normalize(after(tokens, grad_first).astype(wide))
-    grad_first_norm = normalize_backward(grad_first, ln1_gain, unit1, inverse1)
-    grad_tokens = (grad_hidden + grad_first_norm).astype(low)
     return (
         layer_out, grad_tokens, lines[0], lines[1], grad_qkv, grad_table, grad_wout,
         lines[2], lines[3], grad_up, grad_up_bias, grad_down, lines[4],

time: 425 us -> 415 us (0.976)
  other arithmetic: 41.1 us -> 29.9 us
  local copies, waits for them, and re-layouts: 35.2 us -> 26.3 us
  Pallas kernels: 126 us -> 133 us
    unnamed x141 -> x111, local copies, waits for them, and re-layouts: 24.6 us -> 16.1 us
    convert_element_type x4 -> x1, other arithmetic: 6.6 us -> 0.04 us  [body(): wout_grad = sum((one.astype(wide) for one in results[4:])).astype(low)]
    pallas_call x0 -> x2, Pallas kernels: none -> 4.58 us  [the longest x1 2.58 us: first_norm(): pl.pallas_call(first_norm_kernel, out_shape=jax.ShapeDtypeStruct(tokens.s...]
    convert_element_type x5 -> x6, other arithmetic: 8.72 us -> 5.98 us  [halve_end(): (pair[0].astype(jnp.float32) + pair[1].astype(jnp.float32)).astype(jnp.bf...]
    ppermute x39 -> x40, waiting for transfers between devices: 80.2 us -> 78.3 us  [flip(): return lax.ppermute(value, axis, [(i, i ^ bit) for i in range(size)])]
    ppermute x39 -> x40, starting transfers between devices: 46.7 us -> 44.9 us  [flip(): return lax.ppermute(value, axis, [(i, i ^ bit) for i in range(size)])]
  transfers between devices with their start and end apart: 52 -> 53, of which waited for: 24 -> 25; matrix products, arithmetic and copies ran while one was open for 11% -> 9% of each run, Pallas kernels for 25% -> 29%
where the time goes in v1:
time: 415 us; the launch traced here: 410 us
  waiting for transfers between devices  144 us (35%)
  Pallas kernels  133 us (32%)
  starting transfers between devices  61.7 us (15%)
  other arithmetic  29.9 us (7%)
  local copies, waits for them, and re-layouts  26.3 us (6%)
  between operations  15.3 us (4%)
    ppermute x40, waiting for transfers between devices, flip(): return lax.ppermute(value, axis, [(i, i ^ bit) for i in range(size)])  78.3 us
    ppermute x40, starting transfers between devices, flip(): return lax.ppermute(value, axis, [(i, i ^ bit) for i in range(size)])  44.9 us
    ppermute x3, waiting for transfers between devices, relay(): lax.ppermute(left, 'mp', to_left[:parts - step])  36.1 us
    pallas_call x1, Pallas kernels, attention_backward(): pl.pallas_call(attention_backward_kernel, grid_spec=pltpu.PrefetchScalarG...  33.5 us
    pallas_call x1, Pallas kernels, attention_forward(): pl.pallas_call(attention_forward_kernel, grid_spec=pltpu.PrefetchScalarGr...  26.2 us
    pallas_call x2, Pallas kernels, feed_forward(): pl.pallas_call(functools.partial(feed_kernel, unit=unit, count=len(weight...  23.3 us
    ppermute x3, waiting for transfers between devices, relay(): lax.ppermute(right, 'mp', to_right[step - 1:])  19.2 us
    unnamed x111, local copies, waits for them, and re-layouts  16.1 us
  transfers between devices with their start and end apart: 53, of which 25 were waited for; matrix products, arithmetic and copies ran while one was open for 9% of the time, Pallas kernels for 29%

profile of v1, /device:TPU:0, one launch (start us, length us, event | category | flops | bytes accessed | tf_op | source)
XLA Modules:
  0.0 410.4 jit_solution(6979659595621697918)
XLA Ops:
  8.6 2.6 first_norm.1
  14.3 1.8 constant_dynamic-slice_fusion.8
  16.9 5.0 %collective-permute-start.3 = (bf16[328,1024]{1,0:T(8,128)(2,1)}, bf16[328,1024]{1,0:T(8,128)(2,1)S(1)}, u32[]{:S(2)}, u32[]{:S(2)}) collective-permute-start(bf16[328,1024]{1,0:T(8,128)(2,1)} %pad_maximum_fusion.3), channel_id=1, source_target_pairs={{0,1},{1,2},{2,3},{4,5},{5,6},{6,7},{8,9},{9,10},{10,11},{12,13},{... | collective-permute-start | bytes 2015240 | tf_op jit(solution)/shard_map/ppermute | solution.py:1030
  23.2 1.6 collective-permute-start.1
  29.8 2.0 maximum_bitcast_fusion
  31.8 19.2 %collective-permute-done.3 = bf16[328,1024]{1,0:T(8,128)(2,1)S(1)} collective-permute-done((bf16[328,1024]{1,0:T(8,128)(2,1)}, bf16[328,1024]{1,0:T(8,128)(2,1)S(1)}, u32[]{:S(2)}, u32[]{:S(2)}) %collective-permute-start.3) | collective-permute-done | bytes 671776 | tf_op jit(solution)/shard_map/ppermute | solution.py:1030
  51.0 19.8 %collective-permute-done.5 = bf16[328,1024]{1,0:T(8,128)(2,1)S(1)} collective-permute-done((bf16[328,1024]{1,0:T(8,128)(2,1)}, bf16[328,1024]{1,0:T(8,128)(2,1)S(1)}, u32[]{:S(2)}, u32[]{:S(2)}) %collective-permute-start.5) | collective-permute-done | bytes 671776 | tf_op jit(solution)/shard_map/ppermute | solution.py:1031
  71.7 1.7 collective-permute-start.7
  74.2 2.3 pad_maximum_fusion.2.refs_0_
  76.6 1.5 collective-permute-start.4
  79.4 2.1 constant_dynamic-update-slice_fusion.3
  82.7 4.0 collective-permute-done.7.refs_2_
  87.8 16.3 %collective-permute-done.6 = bf16[328,1024]{1,0:T(8,128)(2,1)} collective-permute-done((bf16[328,1024]{1,0:T(8,128)(2,1)S(1)}, bf16[328,1024]{1,0:T(8,128)(2,1)}, u32[]{:S(2)}, u32[]{:S(2)}) %collective-permute-start.6) | collective-permute-done | bytes 671776 | tf_op jit(solution)/shard_map/ppermute | solution.py:1031
  106.8 2.1 collective-permute-start.8
  108.9 1.5 collective-permute-start.10
  111.7 26.2 %attention_forward.1 = (bf16[1536,384]{1,0:T(8,128)(2,1)}, bf16[1536,384]{1,0:T(8,128)(2,1)}, bf16[1536,256]{1,0:T(8,128)(2,1)}, f32[8,1536]{1,0:T(8,128)}, f32[8,1536]{1,0:T(8,128)}) custom-call(s32[1]{0:T(128)} %bitcast.9.cut_ref, bf16[1536,1024]{1,0:T(8,128)(2,1)} %all-gather.2.cloned.1.call-done.rows_ref.normed_ref, bf16[3,1024,256]{2,1,0:T(8,128)(2,1)} %weight_b.1, ...), custom_call_target="tpu_custom_call" | custom-call | flops 1 | bytes 1 | tf_op jit(solution)/shard_map/attention_forward/pallas_call | solution.py:167
  137.9 1.7 select_bitcast_fusion.refs_5_
  140.9 3.8 collective-permute-start.12
  144.9 2.2 collective-permute-start.14
  147.1 9.4 %collective-permute-done.11.refs_6_ = bf16[1,328,1024]{2,1,0:T(8,128)(2,1)S(1)} collective-permute-done((bf16[1,328,1024]{2,1,0:T(8,128)(2,1)S(1)}, bf16[1,328,1024]{2,1,0:T(8,128)(2,1)S(1)}, u32[]{:S(2)}, u32[]{:S(2)}) %collective-permute-start.11) | collective-permute-done | bytes 671776 | tf_op jit(solution)/shard_map/ppermute | solution.py:409
  158.6 3.1 collective-permute-done.13.refs_2_
  161.7 1.4 branch_and_norm.1
  163.3 1.5 collective-permute-start.19
  166.7 11.7 %feed_forward.2 = (bf16[768,1024]{1,0:T(8,128)(2,1)}, bf16[768,1024]{1,0:T(8,128)(2,1)}, bf16[384,1024]{1,0:T(8,128)(2,1)S(1)}, bf16[384,1024]{1,0:T(8,128)(2,1)...) custom-call(bf16[2,256,1024]{2,1,0:T(8,128)(2,1)} %pad_maximum_fusion.2.refs_0_, ...), custom_call_target="tpu_custom_call" | custom-call | flops 1 | bytes 1 | tf_op jit(solution)/shard_map/feed_forward/pallas_call | solution.py:930
  178.4 4.8 %collective-permute-done.19 = bf16[384,1024]{1,0:T(8,128)(2,1)S(1)} collective-permute-done((bf16[384,1024]{1,0:T(8,128)(2,1)S(1)}, bf16[384,1024]{1,0:T(8,128)(2,1)S(1)}, u32[]{:S(2)}, u32[]{:S(2)}) %collective-permute-start.19) | collective-permute-done | bytes 786464 | tf_op jit(solution)/shard_map/ppermute | solution.py:409
  183.3 2.2 collective-permute-done.20
  186.8 11.6 %feed_forward.3 = (bf16[768,1024]{1,0:T(8,128)(2,1)}, bf16[768,1024]{1,0:T(8,128)(2,1)}, bf16[384,1024]{1,0:T(8,128)(2,1)S(1)}, bf16[384,1024]{1,0:T(8,128)(2,1)...) custom-call(bf16[2,256,1024]{2,1,0:T(8,128)(2,1)} %pad_maximum_fusion.2.refs_0_, ...), custom_call_target="tpu_custom_call" | custom-call | flops 1 | bytes 1 | tf_op jit(solution)/shard_map/feed_forward/pallas_call | solution.py:930
  198.9 1.8 collective-permute-done.21
  201.0 1.5 collective-permute-start.24
  203.9 11.9 %weight_grads.1 = (bf16[4,1,2,128,1024]{4,3,2,1,0:T(8,128)(2,1)}, bf16[4,1,2,128,1024]{4,3,2,1,0:T(8,128)(2,1)}) custom-call(s32[1]{0:T(128)} %bitcast.15.part_ref, bf16[768,1024]{1,0:T(8,128)(2,1)} %get-tuple-element.133.act_a, bf16[768,1024]{1,0:T(8,128)(2,1)} %get-tuple-element.142.act_b, bf16[768,1024]{1,0:T(8,128)(2,1)} %get-tuple-element.143.pre_a, ...), custom_call_target="tpu_custom_call" | custom-call | flops 99999997952 | bytes 1 | tf_op jit(solution)/shard_map/weight_grads/pallas_call | solution.py:974
  217.0 3.7 collective-permute-done.24.across_ref
  220.7 2.2 row_grads.1
  224.9 3.8 collective-permute-start.26
  228.9 2.2 collective-permute-start.28
  231.1 4.9 %collective-permute-done.26 = bf16[384,256]{1,0:T(8,128)(2,1)S(1)} collective-permute-done((bf16[384,256]{1,0:T(8,128)(2,1)S(1)}, bf16[384,256]{1,0:T(8,128)(2,1)S(1)}, u32[]{:S(2)}, u32[]{:S(2)}) %collective-permute-start.26) | collective-permute-done | bytes 196640 | tf_op jit(solution)/shard_map/ppermute | solution.py:409
  236.0 9.8 %collective-permute-done.27 = bf16[384,256]{1,0:T(8,128)(2,1)S(1)} collective-permute-done((bf16[384,256]{1,0:T(8,128)(2,1)S(1)}, bf16[384,256]{1,0:T(8,128)(2,1)S(1)}, u32[]{:S(2)}, u32[]{:S(2)}) %collective-permute-start.27) | collective-permute-done | bytes 196640 | tf_op jit(solution)/shard_map/ppermute | solution.py:409
  245.8 3.7 out_weight_grad.1
  250.6 2.3 fusion.4
  254.3 9.9 %collective-permute-done.22 = bf16[4,1,2,128,1024]{4,3,2,1,0:T(8,128)(2,1)} collective-permute-done((bf16[4,1,2,128,1024]{4,3,2,1,0:T(8,128)(2,1)}, bf16[4,1,2,128,1024]{4,3,2,1,0:T(8,128)(2,1)}, u32[]{:S(2)}, u32[]{:S(2)}) %collective-permute-start.22) | collective-permute-done | bytes 2097184 | tf_op jit(solution)/shard_map/ppermute | solution.py:409
  264.1 3.9 add_convert_fusion
  269.7 1.5 collective-permute-start.30
  271.2 33.5 %attention_backward.1 = (bf16[1536,384]{1,0:T(8,128)(2,1)}, bf16[1536,384]{1,0:T(8,128)(2,1)}, f32[8,512]{1,0:T(8,128)}) custom-call(s32[1]{0:T(128)} %bitcast.9.cut_ref, bf16[1536,384]{1,0:T(8,128)(2,1)} %get-tuple-element.125.qkv_a, bf16[1536,384]{1,0:T(8,128)(2,1)} %get-tuple-element.126.qkv_b, bf16[1536,256]{1,0:T(8,128)(2,1)} %bitcast.152, ...), custom_call_target="tpu_custom_call" | custom-call | flops 20000000000 | bytes 1 | tf_op jit(solution)/shard_map/attention_backward/pallas_call | solution.py:327
  305.0 7.1 %qkv_weight_grad.1 = (bf16[512,768]{1,0:T(8,128)(2,1)}, bf16[512,768]{1,0:T(8,128)(2,1)}) custom-call(s32[1]{0:T(128)} %bitcast.core_ref, bf16[1536,1024]{1,0:T(8,128)(2,1)} %all-gather.2.cloned.1.call-done.rows_ref.normed_ref, bf16[1536,384]{1,0:T(8,128)(2,1)} %get-tuple-element.181.grad_a, bf16[1536,384]{1,0:T(8,128)(2,1)} %get-tuple-element.176.grad_b), custom_call_target="tpu_custom_call" | custom-call | flops 1 | bytes 1 | tf_op jit(solution)/shard_map/qkv_weight_grad/pallas_call | solution.py:583
  312.8 8.6 %input_cotangent.1 = (bf16[1536,1024]{1,0:T(8,128)(2,1)}, f32[16,1024]{1,0:T(8,128)}) custom-call(bf16[1536,384]{1,0:T(8,128)(2,1)} %get-tuple-element.181.grad_a, bf16[1536,384]{1,0:T(8,128)(2,1)} %get-tuple-element.176.grad_b, bf16[3,1024,256]{2,1,0:T(8,128)(2,1)} %weight_b.1, bf16[3,1024,256]{2,1,0:T(8,128)(2,1)} %weight_b.1, ...), custom_call_target="tpu_custom_call" | custom-call | flops 1 | bytes 1 | tf_op jit(solution)/shard_map/input_cotangent/pallas_call | solution.py:846
  323.5 6.6 %collective-permute-done.33 = bf16[4,1,32,1024]{3,2,1,0:T(8,128)(2,1)S(1)} collective-permute-done((bf16[4,1,32,1024]{3,2,1,0:T(8,128)(2,1)S(1)}, bf16[4,1,32,1024]{3,2,1,0:T(8,128)(2,1)S(1)}, u32[]{:S(2)}, u32[]{:S(2)}) %collective-permute-start.33) | collective-permute-done | bytes 262176 | tf_op jit(solution)/shard_map/ppermute | solution.py:409
  334.5 2.8 fusion.3
  337.3 1.5 collective-permute-start.37
  338.8 1.8 collective-permute-done.35
  340.8 6.5 %collective-permute-done.37 = f32[10,1024]{1,0:T(8,128)S(1)} collective-permute-done((f32[10,1024]{1,0:T(8,128)S(1)}, f32[10,1024]{1,0:T(8,128)S(1)}, u32[]{:S(2)}, u32[]{:S(2)}) %collective-permute-start.37) | collective-permute-done | bytes 40992 | tf_op jit(solution)/shard_map/ppermute | solution.py:409
  349.0 4.1 collective-permute-start.41
  353.1 2.4 collective-permute-start.43
  355.5 4.7 %collective-permute-done.41 = bf16[32,1024]{1,0:T(8,128)(2,1)S(1)} collective-permute-done((bf16[32,1024]{1,0:T(8,128)(2,1)S(1)}, bf16[32,1024]{1,0:T(8,128)(2,1)S(1)}, u32[]{:S(2)}, u32[]{:S(2)}) %collective-permute-start.41) | collective-permute-done | bytes 65568 | tf_op jit(solution)/shard_map/ppermute | solution.py:409
  360.2 1.4 collective-permute-start.39
  361.7 2.1 collective-permute-done.43
  363.8 1.4 collective-permute-done.39
  365.6 3.6 collective-permute-start.45
  370.4 5.6 %collective-permute-done.44 = bf16[512,256]{1,0:T(8,128)(2,1)S(1)} collective-permute-done((bf16[512,256]{1,0:T(8,128)(2,1)S(1)}, bf16[512,256]{1,0:T(8,128)(2,1)S(1)}, u32[]{:S(2)}, u32[]{:S(2)}) %collective-permute-start.44) | collective-permute-done | bytes 262176 | tf_op jit(solution)/shard_map/ppermute | solution.py:798
  376.1 1.5 collective-permute-start.46
  377.6 6.6 %feed_grads_out.1 = (f32[1024,1024]{1,0:T(8,128)}, f32[1024,1024]{1,0:T(8,128)}) custom-call(s32[1]{0:T(128)} %bitcast.core_ref, bf16[4,2,128,1024]{3,2,1,0:T(8,128)(2,1)} %bitcast.136, bf16[4,2,128,1024]{3,2,1,0:T(8,128)(2,1)} %bitcast.144), custom_call_target="tpu_custom_call" | custom-call | flops 1 | bytes 1 | tf_op jit(solution)/shard_map/feed_grads_out/pallas_call | solution.py:486
  386.5 1.9 reduce-scatter.5.cloned.1.call-done.grad_ref
  388.3 2.5 collective-permute-start.48
  392.0 2.0 token_grads.1
  395.0 1.5 collective-permute-start.49
  396.5 3.7 attention_grads_out.1
  (294 shorter events, 55.6 us)
Async XLA Ops:
  7.2 17.6 %copy-start = (f32[32,4]{0,1:T(4,128)S(1)}, f32[32,4]{0,1:T(4,128)}, u32[]{:S(2)}) copy-start(f32[32,4]{0,1:T(4,128)} %param.21) | copy-start | bytes 1540
  7.2 97.0 %all-gather.2.cloned.1.call-start = ((), (), s32[]{:S(2)}) async-start(), calls=%async_computation.2 | async-start | bytes 3932160 | tf_op jit(solution)/shard_map/all_gather | solution.py:1039
  11.2 318.9 %reduce-scatter.3.cloned.1.call-start = ((), (), s32[]{:S(2)}) async-start(), calls=%async_computation.3 | async-start | bytes 2621440 | tf_op jit(solution)/shard_map/reduce_scatter | solution.py:1154
  12.3 10.9 %copy-start.8 = (bf16[384,1024]{1,0:T(8,128)(2,1)S(1)}, bf16[384,1024]{1,0:T(8,128)(2,1)}, u32[]{:S(2)}) copy-start(bf16[384,1024]{1,0:T(8,128)(2,1)} %grad_ref.1) | copy-start | bytes 2359300
  12.3 12.4 %copy-start.43 = (s32[128]{0:T(128)S(1)}, s32[128]{0:T(128)}, u32[]{:S(2)}) copy-start(s32[128]{0:T(128)} %param.17) | copy-start | bytes 1540
  12.4 12.7 %copy-start.39 = (s32[1,1536]{1,0:T(1,128)S(1)}, s32[1,1536]{1,0:T(1,128)}, u32[]{:S(2)}) copy-start(s32[1,1536]{1,0:T(1,128)} %param.16) | copy-start | bytes 18436
  16.1 12.9 %copy-start.16 = (f32[1024]{0:T(1024)S(1)}, f32[1024]{0:T(1024)}, u32[]{:S(2)}) copy-start(f32[1024]{0:T(1024)} %param.23) | copy-start | bytes 12292
  16.1 12.9 %copy-start.40 = (f32[1024]{0:T(1024)S(1)}, f32[1024]{0:T(1024)}, u32[]{:S(2)}) copy-start(f32[1024]{0:T(1024)} %param.24) | copy-start | bytes 12292
  16.9 34.0 %collective-permute-start.3 = (bf16[328,1024]{1,0:T(8,128)(2,1)}, bf16[328,1024]{1,0:T(8,128)(2,1)S(1)}, u32[]{:S(2)}, u32[]{:S(2)}) collective-permute-start(bf16[328,1024]{1,0:T(8,128)(2,1)} %pad_maximum_fusion.3), channel_id=1, source_target_pairs={{0,1},{1,2},{2,3},{4,5},{5,6},{6,7},{8,9},{9,10},{10,11},{12,13},{... | collective-permute-start | bytes 2015240 | tf_op jit(solution)/shard_map/ppermute | solution.py:1030
  21.9 48.9 %collective-permute-start.5 = (bf16[328,1024]{1,0:T(8,128)(2,1)}, bf16[328,1024]{1,0:T(8,128)(2,1)S(1)}, u32[]{:S(2)}, u32[]{:S(2)}) collective-permute-start(bf16[328,1024]{1,0:T(8,128)(2,1)} %pad_maximum_fusion.3), channel_id=1, source_target_pairs={{1,0},{2,1},{3,2},{5,4},{6,5},{7,6},{9,8},{10,9},{11,10},{13,12},{... | collective-permute-start | bytes 2015240 | tf_op jit(solution)/shard_map/ppermute | solution.py:1031
  23.2 53.2 %collective-permute-start.1 = (bf16[384,1024]{1,0:T(8,128)(2,1)S(1)}, bf16[384,1024]{1,0:T(8,128)(2,1)}, u32[]{:S(2)}, u32[]{:S(2)}) collective-permute-start(bf16[384,1024]{1,0:T(8,128)(2,1)S(1)} %copy-done.8), channel_id=1, source_target_pairs={{0,8},{4,12},{8,0},{12,4},{1,9},{5,13},{9,1},{13,5},{2,10},{6,14},... | collective-permute-start | bytes 2359304 | tf_op jit(solution)/shard_map/ppermute | solution.py:409
  24.8 56.7 %collective-permute-start = (bf16[384,1024]{1,0:T(8,128)(2,1)S(1)}, bf16[384,1024]{1,0:T(8,128)(2,1)}, u32[]{:S(2)}, u32[]{:S(2)}) collective-permute-start(bf16[384,1024]{1,0:T(8,128)(2,1)S(1)} %copy-done.8), channel_id=1, source_target_pairs={{0,4},{4,0},{8,12},{12,8},{1,5},{5,1},{9,13},{13,9},{2,6},{6,2},{1... | collective-permute-start | bytes 2359304 | tf_op jit(solution)/shard_map/ppermute | solution.py:409
  71.7 15.0 %collective-permute-start.7 = (bf16[1,328,1024]{2,1,0:T(8,128)(2,1)S(1)}, bf16[1,328,1024]{2,1,0:T(8,128)(2,1)S(1)}, u32[]{:S(2)}, u32[]{:S(2)}) collective-permute-start(bf16[1,328,1024]{2,1,0:T(8,128)(2,1)S(1)} %select_bitcast_fusion.1.refs_1_), channel_id=1, source_target_pairs={{0,16},{16,0},{1,17},{17,1},{2,18},{18,2},{3,19},{19,3},{4,20},{20... | collective-permute-start | bytes 2015240 | tf_op jit(solution)/shard_map/ppermute | solution.py:409
  76.5 10.4 %collective-permute-start.2 = (bf16[384,1024]{1,0:T(8,128)(2,1)}, bf16[384,1024]{1,0:T(8,128)(2,1)S(1)}, u32[]{:S(2)}, u32[]{:S(2)}) collective-permute-start(bf16[384,1024]{1,0:T(8,128)(2,1)} %collective-permute-done.1), channel_id=1, source_target_pairs={{0,4},{4,0},{8,12},{12,8},{1,5},{5,1},{9,13},{13,9},{2,6},{6,2},{1... | collective-permute-start | bytes 2359304 | tf_op jit(solution)/shard_map/ppermute | solution.py:409
  76.6 11.3 %collective-permute-start.4 = (bf16[328,1024]{1,0:T(8,128)(2,1)S(1)}, bf16[328,1024]{1,0:T(8,128)(2,1)}, u32[]{:S(2)}, u32[]{:S(2)}) collective-permute-start(bf16[328,1024]{1,0:T(8,128)(2,1)S(1)} %collective-permute-done.3), channel_id=1, source_target_pairs={{1,2},{2,3},{5,6},{6,7},{9,10},{10,11},{13,14},{14,15},{17,18},{18... | collective-permute-start | bytes 2015240 | tf_op jit(solution)/shard_map/ppermute | solution.py:1030
  78.1 26.1 %collective-permute-start.6 = (bf16[328,1024]{1,0:T(8,128)(2,1)S(1)}, bf16[328,1024]{1,0:T(8,128)(2,1)}, u32[]{:S(2)}, u32[]{:S(2)}) collective-permute-start(bf16[328,1024]{1,0:T(8,128)(2,1)S(1)} %copy-done.23), channel_id=1, source_target_pairs={{1,0},{2,1},{5,4},{6,5},{9,8},{10,9},{13,12},{14,13},{17,16},{18,1... | collective-permute-start | bytes 2015240 | tf_op jit(solution)/shard_map/ppermute | solution.py:1031
  86.7 17.5 %copy-start.4 = (bf16[1,328,1024]{2,1,0:T(8,128)(2,1)}, bf16[1,328,1024]{2,1,0:T(8,128)(2,1)S(1)}, u32[]{:S(2)}) copy-start(bf16[1,328,1024]{2,1,0:T(8,128)(2,1)S(1)} %collective-permute-done.7.refs_2_) | copy-start | bytes 2015236
  86.8 23.7 %collective-permute-start.15 = (bf16[2,64,1024]{2,1,0:T(8,128)(2,1)S(1)}, bf16[2,64,1024]{2,1,0:T(8,128)(2,1)}, u32[]{:S(2)}, u32[]{:S(2)}) collective-permute-start(bf16[2,64,1024]{2,1,0:T(8,128)(2,1)S(1)} %reverse_select_fusion.2), channel_id=1, source_target_pairs={{0,4},{4,0},{8,12},{12,8},{1,5},{5,1},{9,13},{13,9},{2,6},{6,2},{1... | collective-permute-start | bytes 786440 | tf_op jit(solution)/shard_map/ppermute | solution.py:409
  104.2 33.8 %collective-permute-start.9 = (bf16[328,1024]{1,0:T(8,128)(2,1)}, bf16[328,1024]{1,0:T(8,128)(2,1)}, u32[]{:S(2)}, u32[]{:S(2)}) collective-permute-start(bf16[328,1024]{1,0:T(8,128)(2,1)} %collective-permute-done.6), channel_id=1, source_target_pairs={{1,0},{5,4},{9,8},{13,12},{17,16},{21,20},{25,24},{29,28}} | collective-permute-start | bytes 2015240 | tf_op jit(solution)/shard_map/ppermute | solution.py:1031
  106.8 31.1 %collective-permute-start.8 = (bf16[328,1024]{1,0:T(8,128)(2,1)}, bf16[328,1024]{1,0:T(8,128)(2,1)}, u32[]{:S(2)}, u32[]{:S(2)}) collective-permute-start(bf16[328,1024]{1,0:T(8,128)(2,1)} %collective-permute-done.4), channel_id=1, source_target_pairs={{2,3},{6,7},{10,11},{14,15},{18,19},{22,23},{26,27},{30,31}} | collective-permute-start | bytes 2015240 | tf_op jit(solution)/shard_map/ppermute | solution.py:1030
  108.9 29.0 %collective-permute-start.10 = (bf16[1,328,1024]{2,1,0:T(8,128)(2,1)S(1)}, bf16[1,328,1024]{2,1,0:T(8,128)(2,1)S(1)}, u32[]{:S(2)}, u32[]{:S(2)}) collective-permute-start(bf16[1,328,1024]{2,1,0:T(8,128)(2,1)S(1)} %add_bitcast_fusion.refs_3_), channel_id=1, source_target_pairs={{0,16},{16,0},{1,17},{17,1},{2,18},{18,2},{3,19},{19,3},{4,20},{20... | collective-permute-start | bytes 2015240 | tf_op jit(solution)/shard_map/ppermute | solution.py:409
  139.7 16.9 %collective-permute-start.11 = (bf16[1,328,1024]{2,1,0:T(8,128)(2,1)S(1)}, bf16[1,328,1024]{2,1,0:T(8,128)(2,1)S(1)}, u32[]{:S(2)}, u32[]{:S(2)}) collective-permute-start(bf16[1,328,1024]{2,1,0:T(8,128)(2,1)S(1)} %select_bitcast_fusion.refs_5_), channel_id=1, source_target_pairs={{0,16},{16,0},{1,17},{17,1},{2,18},{18,2},{3,19},{19,3},{4,20},{20... | collective-permute-start | bytes 2015240 | tf_op jit(solution)/shard_map/ppermute | solution.py:409
  140.4 16.3 %collective-permute-start.16 = (bf16[2,64,1024]{2,1,0:T(8,128)(2,1)S(1)}, bf16[2,64,1024]{2,1,0:T(8,128)(2,1)S(1)}, u32[]{:S(2)}, u32[]{:S(2)}) collective-permute-start(bf16[2,64,1024]{2,1,0:T(8,128)(2,1)S(1)} %reverse_select_fusion.1), channel_id=1, source_target_pairs={{0,4},{4,0},{8,12},{12,8},{1,5},{5,1},{9,13},{13,9},{2,6},{6,2},{1... | collective-permute-start | bytes 786440 | tf_op jit(solution)/shard_map/ppermute | solution.py:409
  140.9 17.7 %collective-permute-start.12 = (bf16[384,256]{1,0:T(8,128)(2,1)S(1)}, bf16[384,256]{1,0:T(8,128)(2,1)S(1)}, u32[]{:S(2)}, u32[]{:S(2)}) collective-permute-start(bf16[384,256]{1,0:T(8,128)(2,1)S(1)} %get-tuple-element.267), channel_id=1, source_target_pairs={{0,1},{1,0},{2,3},{3,2},{4,5},{5,4},{6,7},{7,6},{8,9},{9,8},{10,11... | collective-permute-start | bytes 589832 | tf_op jit(solution)/shard_map/ppermute | solution.py:409
  144.6 17.1 %collective-permute-start.13 = (bf16[384,256]{1,0:T(8,128)(2,1)S(1)}, bf16[384,256]{1,0:T(8,128)(2,1)S(1)}, u32[]{:S(2)}, u32[]{:S(2)}) collective-permute-start(bf16[384,256]{1,0:T(8,128)(2,1)S(1)} %get-tuple-element.266), channel_id=1, source_target_pairs={{0,2},{1,3},{2,0},{3,1},{4,6},{5,7},{6,4},{7,5},{8,10},{9,11},{10,... | collective-permute-start | bytes 589832 | tf_op jit(solution)/shard_map/ppermute | solution.py:409
  144.9 16.8 %collective-permute-start.14 = (bf16[384,256]{1,0:T(8,128)(2,1)S(1)}, bf16[384,256]{1,0:T(8,128)(2,1)S(1)}, u32[]{:S(2)}, u32[]{:S(2)}) collective-permute-start(bf16[384,256]{1,0:T(8,128)(2,1)S(1)} %get-tuple-element.265), channel_id=1, source_target_pairs={{0,3},{1,2},{2,1},{3,0},{4,7},{5,6},{6,5},{7,4},{8,11},{9,10},{10,... | collective-permute-start | bytes 589832 | tf_op jit(solution)/shard_map/ppermute | solution.py:409
  156.7 1.6 collective-permute-start.17
  163.2 2.4 collective-permute-start.18
  163.3 20.0 %collective-permute-start.19 = (bf16[384,1024]{1,0:T(8,128)(2,1)S(1)}, bf16[384,1024]{1,0:T(8,128)(2,1)S(1)}, u32[]{:S(2)}, u32[]{:S(2)}) collective-permute-start(bf16[384,1024]{1,0:T(8,128)(2,1)S(1)} %get-tuple-element.132), channel_id=1, source_target_pairs={{0,8},{4,12},{8,0},{12,4},{1,9},{5,13},{9,1},{13,5},{2,10},{6,14},... | collective-permute-start | bytes 2359304 | tf_op jit(solution)/shard_map/ppermute | solution.py:409
  183.3 2.3 collective-permute-start.20
  198.4 2.4 collective-permute-start.21
  198.6 22.1 %collective-permute-start.23 = (bf16[384,1024]{1,0:T(8,128)(2,1)}, bf16[384,1024]{1,0:T(8,128)(2,1)S(1)}, u32[]{:S(2)}, u32[]{:S(2)}) collective-permute-start(bf16[384,1024]{1,0:T(8,128)(2,1)} %get-tuple-element.146), channel_id=1, source_target_pairs={{0,4},{4,0},{8,12},{12,8},{1,5},{5,1},{9,13},{13,9},{2,6},{6,2},{1... | collective-permute-start | bytes 2359304 | tf_op jit(solution)/shard_map/ppermute | solution.py:409
  201.0 19.7 %collective-permute-start.24 = (bf16[384,1024]{1,0:T(8,128)(2,1)S(1)}, bf16[384,1024]{1,0:T(8,128)(2,1)S(1)}, u32[]{:S(2)}, u32[]{:S(2)}) collective-permute-start(bf16[384,1024]{1,0:T(8,128)(2,1)S(1)} %add_convert_fusion.3), channel_id=1, source_target_pairs={{0,8},{4,12},{8,0},{12,4},{1,9},{5,13},{9,1},{13,5},{2,10},{6,14},... | collective-permute-start | bytes 2359304 | tf_op jit(solution)/shard_map/ppermute | solution.py:409
  203.8 41.9 %collective-permute-start.25 = (bf16[2,384,1024]{2,1,0:T(8,128)(2,1)}, bf16[2,384,1024]{2,1,0:T(8,128)(2,1)}, u32[]{:S(2)}, u32[]{:S(2)}) collective-permute-start(bf16[2,384,1024]{2,1,0:T(8,128)(2,1)} %pad_maximum_fusion.1), channel_id=1, source_target_pairs={{0,4},{4,0},{8,12},{12,8},{1,5},{5,1},{9,13},{13,9},{2,6},{6,2},{1... | collective-permute-start | bytes 4718600 | tf_op jit(solution)/shard_map/ppermute | solution.py:409
  203.8 16.8 %copy-start.9 = (bf16[384,1024]{1,0:T(8,128)(2,1)S(1)}, bf16[384,1024]{1,0:T(8,128)(2,1)}, u32[]{:S(2)}) copy-start(bf16[384,1024]{1,0:T(8,128)(2,1)} %grad_ref.1) | copy-start | bytes 2359300
  215.8 48.4 %collective-permute-start.22 = (bf16[4,1,2,128,1024]{4,3,2,1,0:T(8,128)(2,1)}, bf16[4,1,2,128,1024]{4,3,2,1,0:T(8,128)(2,1)}, u32[]{:S(2)}, u32[]{:S(2)}) collective-permute-start(bf16[4,1,2,128,1024]{4,3,2,1,0:T(8,128)(2,1)} %get-tuple-element.145), channel_id=1, source_target_pairs={{0,16},{16,0},{1,17},{17,1},{2,18},{18,2},{3,19},{19,3},{4,20},{20... | collective-permute-start | bytes 6291464 | tf_op jit(solution)/shard_map/ppermute | solution.py:409
  224.9 11.0 %collective-permute-start.26 = (bf16[384,256]{1,0:T(8,128)(2,1)S(1)}, bf16[384,256]{1,0:T(8,128)(2,1)S(1)}, u32[]{:S(2)}, u32[]{:S(2)}) collective-permute-start(bf16[384,256]{1,0:T(8,128)(2,1)S(1)} %get-tuple-element.152), channel_id=1, source_target_pairs={{0,1},{1,0},{2,3},{3,2},{4,5},{5,4},{6,7},{7,6},{8,9},{9,8},{10,11... | collective-permute-start | bytes 589832 | tf_op jit(solution)/shard_map/ppermute | solution.py:409
  228.7 17.0 %collective-permute-start.27 = (bf16[384,256]{1,0:T(8,128)(2,1)S(1)}, bf16[384,256]{1,0:T(8,128)(2,1)S(1)}, u32[]{:S(2)}, u32[]{:S(2)}) collective-permute-start(bf16[384,256]{1,0:T(8,128)(2,1)S(1)} %get-tuple-element.153), channel_id=1, source_target_pairs={{0,2},{1,3},{2,0},{3,1},{4,6},{5,7},{6,4},{7,5},{8,10},{9,11},{10,... | collective-permute-start | bytes 589832 | tf_op jit(solution)/shard_map/ppermute | solution.py:409
  228.9 16.9 %collective-permute-start.28 = (bf16[384,256]{1,0:T(8,128)(2,1)S(1)}, bf16[384,256]{1,0:T(8,128)(2,1)S(1)}, u32[]{:S(2)}, u32[]{:S(2)}) collective-permute-start(bf16[384,256]{1,0:T(8,128)(2,1)S(1)} %get-tuple-element.154), channel_id=1, source_target_pairs={{0,3},{1,2},{2,1},{3,0},{4,7},{5,6},{6,5},{7,4},{8,11},{9,10},{10,... | collective-permute-start | bytes 589832 | tf_op jit(solution)/shard_map/ppermute | solution.py:409
  249.4 3.5 collective-permute-start.29
  253.4 10.8 %copy-start.24 = (bf16[4,1,2,128,1024]{4,3,2,1,0:T(8,128)(2,1)S(1)}, bf16[4,1,2,128,1024]{4,3,2,1,0:T(8,128)(2,1)}, u32[]{:S(2)}) copy-start(bf16[4,1,2,128,1024]{4,3,2,1,0:T(8,128)(2,1)} %get-tuple-element.147) | copy-start | bytes 6291460
  268.1 120.3 %reduce-scatter.5.cloned.1.call-start = ((), (), s32[]{:S(2)}) async-start(), calls=%async_computation.4 | async-start | bytes 3932160 | tf_op jit(solution)/shard_map/reduce_scatter | solution.py:1181
  269.2 35.6 %collective-permute-start.31 = (bf16[384,1024]{1,0:T(8,128)(2,1)S(1)}, bf16[384,1024]{1,0:T(8,128)(2,1)}, u32[]{:S(2)}, u32[]{:S(2)}) collective-permute-start(bf16[384,1024]{1,0:T(8,128)(2,1)S(1)} %copy-done.31), channel_id=1, source_target_pairs={{0,8},{4,12},{8,0},{12,4},{1,9},{5,13},{9,1},{13,5},{2,10},{6,14},... | collective-permute-start | bytes 2359304 | tf_op jit(solution)/shard_map/ppermute | solution.py:409
  269.7 35.0 %collective-permute-start.30 = (bf16[4,2,32,1024]{3,2,1,0:T(8,128)(2,1)}, bf16[4,2,32,1024]{3,2,1,0:T(8,128)(2,1)S(1)}, u32[]{:S(2)}, u32[]{:S(2)}) collective-permute-start(bf16[4,2,32,1024]{3,2,1,0:T(8,128)(2,1)} %get-tuple-element.170), channel_id=1, source_target_pairs={{0,8},{4,12},{8,0},{12,4},{1,9},{5,13},{9,1},{13,5},{2,10},{6,14},... | collective-permute-start | bytes 1572872 | tf_op jit(solution)/shard_map/ppermute | solution.py:409
  312.1 18.0 %collective-permute-start.32 = (bf16[512,768]{1,0:T(8,128)(2,1)}, bf16[512,768]{1,0:T(8,128)(2,1)}, u32[]{:S(2)}, u32[]{:S(2)}) collective-permute-start(bf16[512,768]{1,0:T(8,128)(2,1)} %get-tuple-element.180), channel_id=1, source_target_pairs={{0,4},{4,0},{8,12},{12,8},{1,5},{5,1},{9,13},{13,9},{2,6},{6,2},{1... | collective-permute-start | bytes 2359304 | tf_op jit(solution)/shard_map/ppermute | solution.py:409
  321.3 8.7 %collective-permute-start.33 = (bf16[4,1,32,1024]{3,2,1,0:T(8,128)(2,1)S(1)}, bf16[4,1,32,1024]{3,2,1,0:T(8,128)(2,1)S(1)}, u32[]{:S(2)}, u32[]{:S(2)}) collective-permute-start(bf16[4,1,32,1024]{3,2,1,0:T(8,128)(2,1)S(1)} %get-tuple-element.269), channel_id=1, source_target_pairs={{0,16},{16,0},{1,17},{17,1},{2,18},{18,2},{3,19},{19,3},{4,20},{20... | collective-permute-start | bytes 786440 | tf_op jit(solution)/shard_map/ppermute | solution.py:409
  331.1 6.2 %collective-permute-start.36 = (f32[10,1024]{1,0:T(8,128)S(1)}, f32[10,1024]{1,0:T(8,128)S(1)}, u32[]{:S(2)}, u32[]{:S(2)}) collective-permute-start(f32[10,1024]{1,0:T(8,128)S(1)} %reshape.212), channel_id=1, source_target_pairs={{0,4},{4,0},{8,12},{12,8},{1,5},{5,1},{9,13},{13,9},{2,6},{6,2},{1... | collective-permute-start | bytes 122888 | tf_op jit(solution)/shard_map/ppermute | solution.py:409
  331.2 9.5 %collective-permute-start.35 = (bf16[256,1024]{1,0:T(8,128)(2,1)}, bf16[256,1024]{1,0:T(8,128)(2,1)S(1)}, u32[]{:S(2)}, u32[]{:S(2)}) collective-permute-start(bf16[256,1024]{1,0:T(8,128)(2,1)} %bitcast.155), channel_id=1, source_target_pairs={{0,16},{4,12},{8,24},{12,4},{16,0},{20,28},{24,8},{28,20},{1,17},{... | collective-permute-start | bytes 1572872 | tf_op jit(solution)/shard_map/ppermute | solution.py:798
  333.8 13.5 %collective-permute-start.34 = (bf16[2,128,768]{2,1,0:T(8,128)(2,1)S(1)}, bf16[2,128,768]{2,1,0:T(8,128)(2,1)S(1)}, u32[]{:S(2)}, u32[]{:S(2)}) collective-permute-start(bf16[2,128,768]{2,1,0:T(8,128)(2,1)S(1)} %dynamic-slice_bitcast_fusion.2), channel_id=1, source_target_pairs={{0,8},{4,12},{8,0},{12,4},{1,9},{5,13},{9,1},{13,5},{2,10},{6,14},... | collective-permute-start | bytes 1179656 | tf_op jit(solution)/shard_map/ppermute | solution.py:409
  337.3 10.0 %collective-permute-start.37 = (f32[10,1024]{1,0:T(8,128)S(1)}, f32[10,1024]{1,0:T(8,128)S(1)}, u32[]{:S(2)}, u32[]{:S(2)}) collective-permute-start(f32[10,1024]{1,0:T(8,128)S(1)} %add.244), channel_id=1, source_target_pairs={{0,8},{4,12},{8,0},{12,4},{1,9},{5,13},{9,1},{13,5},{2,10},{6,14},... | collective-permute-start | bytes 122888 | tf_op jit(solution)/shard_map/ppermute | solution.py:409
  347.3 18.0 %collective-permute-start.40 = (bf16[2,256,1024]{2,1,0:T(8,128)(2,1)S(1)}, bf16[2,256,1024]{2,1,0:T(8,128)(2,1)S(1)}, u32[]{:S(2)}, u32[]{:S(2)}) collective-permute-start(bf16[2,256,1024]{2,1,0:T(8,128)(2,1)S(1)} %maximum_select_fusion.1), channel_id=1, source_target_pairs={{0,8},{4,20},{8,0},{12,28},{16,24},{20,4},{24,16},{28,12},{1,9},{5... | collective-permute-start | bytes 3145736 | tf_op jit(solution)/shard_map/ppermute | solution.py:798
  348.1 17.1 %collective-permute-start.38 = (bf16[1,128,768]{2,1,0:T(8,128)(2,1)S(1)}, bf16[1,128,768]{2,1,0:T(8,128)(2,1)S(1)}, u32[]{:S(2)}, u32[]{:S(2)}) collective-permute-start(bf16[1,128,768]{2,1,0:T(8,128)(2,1)S(1)} %constant_dynamic-slice_fusion.2), channel_id=1, source_target_pairs={{0,16},{16,0},{1,17},{17,1},{2,18},{18,2},{3,19},{19,3},{4,20},{20... | collective-permute-start | bytes 589832 | tf_op jit(solution)/shard_map/ppermute | solution.py:409
  349.0 11.2 %collective-permute-start.41 = (bf16[32,1024]{1,0:T(8,128)(2,1)S(1)}, bf16[32,1024]{1,0:T(8,128)(2,1)S(1)}, u32[]{:S(2)}, u32[]{:S(2)}) collective-permute-start(bf16[32,1024]{1,0:T(8,128)(2,1)S(1)} %get-tuple-element.273), channel_id=1, source_target_pairs={{0,1},{1,0},{2,3},{3,2},{4,5},{5,4},{6,7},{7,6},{8,9},{9,8},{10,11... | collective-permute-start | bytes 196616 | tf_op jit(solution)/shard_map/ppermute | solution.py:409
  353.1 8.6 %collective-permute-start.42 = (bf16[32,1024]{1,0:T(8,128)(2,1)S(1)}, bf16[32,1024]{1,0:T(8,128)(2,1)S(1)}, u32[]{:S(2)}, u32[]{:S(2)}) collective-permute-start(bf16[32,1024]{1,0:T(8,128)(2,1)S(1)} %get-tuple-element.272), channel_id=1, source_target_pairs={{0,2},{1,3},{2,0},{3,1},{4,6},{5,7},{6,4},{7,5},{8,10},{9,11},{10,... | collective-permute-start | bytes 196616 | tf_op jit(solution)/shard_map/ppermute | solution.py:409
  353.1 10.7 %collective-permute-start.43 = (bf16[32,1024]{1,0:T(8,128)(2,1)S(1)}, bf16[32,1024]{1,0:T(8,128)(2,1)S(1)}, u32[]{:S(2)}, u32[]{:S(2)}) collective-permute-start(bf16[32,1024]{1,0:T(8,128)(2,1)S(1)} %get-tuple-element.271), channel_id=1, source_target_pairs={{0,3},{1,2},{2,1},{3,0},{4,7},{5,6},{6,5},{7,4},{8,11},{9,10},{10,... | collective-permute-start | bytes 196616 | tf_op jit(solution)/shard_map/ppermute | solution.py:409
  360.2 5.0 %collective-permute-start.39 = (f32[10,1024]{1,0:T(8,128)S(1)}, f32[10,1024]{1,0:T(8,128)S(1)}, u32[]{:S(2)}, u32[]{:S(2)}) collective-permute-start(f32[10,1024]{1,0:T(8,128)S(1)} %add.251), channel_id=1, source_target_pairs={{0,16},{16,0},{1,17},{17,1},{2,18},{18,2},{3,19},{19,3},{4,20},{20... | collective-permute-start | bytes 122888 | tf_op jit(solution)/shard_map/ppermute | solution.py:409
  365.6 11.9 %copy-start.17 = (bf16[2,2,256,1024]{3,2,1,0:T(8,128)(2,1)}, bf16[2,2,256,1024]{3,2,1,0:T(8,128)(2,1)S(1)}, u32[]{:S(2)}) copy-start(bf16[2,2,256,1024]{3,2,1,0:T(8,128)(2,1)S(1)} %maximum_select_fusion) | copy-start | bytes 6291460
  365.6 10.4 %collective-permute-start.45 = (bf16[2,2,256,1024]{3,2,1,0:T(8,128)(2,1)S(1)}, bf16[2,2,256,1024]{3,2,1,0:T(8,128)(2,1)S(1)}, u32[]{:S(2)}, u32[]{:S(2)}) collective-permute-start(bf16[2,2,256,1024]{3,2,1,0:T(8,128)(2,1)S(1)} %maximum_select_fusion), channel_id=1, source_target_pairs={{0,4},{4,0},{8,12},{12,8},{1,5},{5,1},{9,13},{13,9},{2,6},{6,2},{1... | collective-permute-start | bytes 6291464 | tf_op jit(solution)/shard_map/ppermute | solution.py:409
  369.5 6.4 %collective-permute-start.44 = (bf16[512,256]{1,0:T(8,128)(2,1)S(1)}, bf16[512,256]{1,0:T(8,128)(2,1)S(1)}, u32[]{:S(2)}, u32[]{:S(2)}) collective-permute-start(bf16[512,256]{1,0:T(8,128)(2,1)S(1)} %constant_dynamic-update-slice_fusion.10), channel_id=1, source_target_pairs={{0,16},{4,12},{8,24},{12,4},{16,0},{20,28},{24,8},{28,20},{1,17},{... | collective-permute-start | bytes 786440 | tf_op jit(solution)/shard_map/ppermute | solution.py:798
  376.1 9.2 %collective-permute-start.46 = (bf16[2,512,256]{2,1,0:T(8,128)(2,1)S(1)}, bf16[2,512,256]{2,1,0:T(8,128)(2,1)S(1)}, u32[]{:S(2)}, u32[]{:S(2)}) collective-permute-start(bf16[2,512,256]{2,1,0:T(8,128)(2,1)S(1)} %maximum_select_fusion.6), channel_id=1, source_target_pairs={{0,8},{4,20},{8,0},{12,28},{16,24},{20,4},{24,16},{28,12},{1,9},{5... | collective-permute-start | bytes 1572872 | tf_op jit(solution)/shard_map/ppermute | solution.py:798
  377.6 13.3 %copy-start.11 = (f32[384,1024]{1,0:T(8,128)S(1)}, f32[384,1024]{1,0:T(8,128)}, u32[]{:S(2)}) copy-start(f32[384,1024]{1,0:T(8,128)} %copy-done.10) | copy-start | bytes 4718596
  388.3 5.7 %collective-permute-start.47 = (bf16[2,2,512,256]{3,2,1,0:T(8,128)(2,1)}, bf16[2,2,512,256]{3,2,1,0:T(8,128)(2,1)S(1)}, u32[]{:S(2)}, u32[]{:S(2)}) collective-permute-start(bf16[2,2,512,256]{3,2,1,0:T(8,128)(2,1)} %maximum_select_fusion.2), channel_id=1, source_target_pairs={{0,4},{4,0},{8,12},{12,8},{1,5},{5,1},{9,13},{13,9},{2,6},{6,2},{1... | collective-permute-start | bytes 3145736 | tf_op jit(solution)/shard_map/ppermute | solution.py:409
  388.3 5.6 %collective-permute-start.48 = (f32[10,1024]{1,0:T(8,128)S(1)}, f32[10,1024]{1,0:T(8,128)S(1)}, u32[]{:S(2)}, u32[]{:S(2)}) collective-permute-start(f32[10,1024]{1,0:T(8,128)S(1)} %add.257), channel_id=1, source_target_pairs={{0,1},{1,0},{2,3},{3,2},{4,5},{5,4},{6,7},{7,6},{8,9},{9,8},{10,11... | collective-permute-start | bytes 122888 | tf_op jit(solution)/shard_map/ppermute | solution.py:409
  395.0 6.5 %collective-permute-start.49 = (f32[10,1024]{1,0:T(8,128)S(1)}, f32[10,1024]{1,0:T(8,128)S(1)}, u32[]{:S(2)}, u32[]{:S(2)}) collective-permute-start(f32[10,1024]{1,0:T(8,128)S(1)} %add.258), channel_id=1, source_target_pairs={{0,2},{1,3},{2,0},{3,1},{4,6},{5,7},{6,4},{7,5},{8,10},{9,11},{10,... | collective-permute-start | bytes 122888 | tf_op jit(solution)/shard_map/ppermute | solution.py:409
  (34 other events, 120.0 us)
Sparse Core Ops, SparseCore 0:
  11.3 84.3 all-gather.1
  268.2 44.5 reduce-scatter.2
  323.6 64.7 reduce-scatter.4

commit v2 on v1

--- a/solution.py
+++ b/solution.py
@@ -77,7 +77,10 @@
         lax.fori_loop(0, rows_ref.shape[0] // BLK, one_chunk, 0)
         for head in range(heads):
             wide = jnp.broadcast_to(bias_ref[head : head + 1, :], (BLK, 2 * BLK))
-            tile_ref[head] = pltpu.roll(wide, 0, 1, stride=1, stride_axis=0)
+            tile_ref[head, :, 0 : 2 * BLK] = pltpu.roll(wide, 0, 1, stride=1, stride_axis=0)
+            tile_ref[head, :, 2 * BLK :] = wide[:, 2 * BLK - 1 :] + jnp.zeros(
+                (BLK, BLK), jnp.float32
+            )
             masked_v[head] = one_head(qkv_refs[head // 2][:, 2 * width :], head % 2)
 
     row_start = block * BLK
@@ -95,13 +98,12 @@
         keys = [ref[pl.ds(key_start, BLK), width : 2 * width] for ref in qkv_refs]
         places = key_start + columns
         allowed = (places <= rows) & (places >= seg_start)
-        offset = pl.multiple_of(jnp.maximum(key_block - block + 1, 0) * BLK, BLK)
-        near = key_block - block + 1 >= 0
+        order = key_block - block + 1
+        offset = pl.multiple_of(jnp.where(order >= 0, order, 2) * BLK, BLK)
         new_tops = []
         for head in range(heads):
             raw = dot_nt(q_heads[head], keys[head // 2])
-            far = bias_ref[head : head + 1, 2 * BLK - 1 : 2 * BLK]
-            bias = jnp.where(near, tile_ref[head, :, pl.ds(offset, BLK)], far)
+            bias = tile_ref[head, :, pl.ds(offset, BLK)]
             scores = jnp.where(allowed, raw + bias, -1e30)
             score_ref[head, :, pl.ds(key_start, BLK)] = scores
             top = tops[head]
@@ -178,7 +180,7 @@
             ],
             out_specs=[full, full, row, line, line],
             scratch_shapes=[
-                pltpu.VMEM((heads, BLK, 2 * BLK), jnp.float32),
+                pltpu.VMEM((heads, BLK, 3 * BLK), jnp.float32),
                 pltpu.VMEM((heads, length, width), jnp.bfloat16),
                 pltpu.VMEM((heads, BLK, length), jnp.float32),
             ],
@@ -195,7 +197,7 @@
 def attention_backward_kernel(
     cut_ref, qkv_a, qkv_b, grad_ref, att_ref, lse_a, lse_b, bias_ref,
     dqkv_a, dqkv_b, table_ref,
-    tile_ref, q_masked, grad_masked, delta_ref, dq_sum, near_sum, far_sum,
+    tile_ref, q_masked, grad_masked, delta_ref, dq_sum, near_sum,
 ):
     heads = q_masked.shape[0]
     block = pl.program_id(0)
@@ -224,10 +226,12 @@
                 grad_masked[head] = one_head(grad_pair, place)
         for head in range(heads):
             wide = jnp.broadcast_to(bias_ref[head : head + 1, :], (BLK, 2 * BLK))
-            tile_ref[head] = pltpu.roll(wide, 0, 1, stride=1, stride_axis=0)
+            tile_ref[head, :, 0 : 2 * BLK] = pltpu.roll(wide, 0, 1, stride=1, stride_axis=0)
+            tile_ref[head, :, 2 * BLK :] = wide[:, BLK - 1 : BLK] + jnp.zeros(
+                (BLK, BLK), jnp.float32
+            )
         dq_sum[...] = jnp.zeros_like(dq_sum)
         near_sum[...] = jnp.zeros_like(near_sum)
-        far_sum[...] = jnp.zeros_like(far_sum)
 
     key_start = pl.multiple_of(block * BLK, BLK)
     keys = [ref[pl.ds(key_start, BLK), width : 2 * width] for ref in qkv_refs]
@@ -242,8 +246,7 @@
         rows = row_start + columns
         allowed = (places <= rows) & (places >= jnp.where(rows >= cut, cut, 0))
         distance = query_block - block
-        near = distance <= 1
-        offset = pl.multiple_of(jnp.minimum(distance, 1) * BLK, BLK)
+        offset = pl.multiple_of(jnp.minimum(distance, 2) * BLK, BLK)
         results = []
         for pair in range(2):
             soft_pieces, grad_pieces, q_pieces, out_pieces = [], [], [], []
@@ -251,8 +254,7 @@
                 head = 2 * pair + place
                 q_head = q_masked[head, pl.ds(row_start, BLK), :]
                 grad_head = grad_masked[head, pl.ds(row_start, BLK), :]
-                far = bias_ref[head : head + 1, BLK - 1 : BLK]
-                bias = jnp.where(near, tile_ref[head, :, pl.ds(offset, BLK)], far)
+                bias = tile_ref[head, :, pl.ds(offset, BLK)]
                 scores = dot_nt(keys[pair], q_head) + bias
                 log_total = lse_refs[pair][place : place + 1, pl.ds(row_start, BLK)]
                 soft = jnp.exp(jnp.where(allowed, scores - log_total, -1e30))
@@ -261,16 +263,7 @@
                 grad_scores = soft * (grad_soft - delta)
                 grad_low = grad_scores.astype(jnp.bfloat16)
 
-                @pl.when(near)
-                def _():
-                    near_sum[head, :, pl.ds(offset, BLK)] += grad_scores
-
-                @pl.when(jnp.logical_not(near))
-                def _():
-                    far_sum[head] += jnp.sum(
-                        grad_scores.reshape(BLK // 8, 8, BLK), axis=0
-                    )
-
+                near_sum[head, :, pl.ds(offset, BLK)] += grad_scores
                 own = slice(place * HEAD_LANES, (place + 1) * HEAD_LANES)
                 spot = slice(head * HEAD_LANES, (head + 1) * HEAD_LANES)
                 dq_sum[spot, pl.ds(row_start, BLK)] += dot_nn(keys_t[pair][own, :], grad_low)
@@ -305,14 +298,14 @@
         for head in range(heads):
             lined = jnp.zeros((8, 2 * BLK), jnp.float32)
             for group in range(BLK // 8):
-                piece = near_sum[head, group * 8 : group * 8 + 8, :]
+                piece = near_sum[head, group * 8 : group * 8 + 8, 0 : 2 * BLK]
                 shift = (2 * BLK - group * 8) % (2 * BLK)
                 lined = lined + (pltpu.roll(piece, shift, 1) if shift else piece)
             total = lined[0:1, :]
             for row in range(1, 8):
                 total = total + pltpu.roll(lined, 2 * BLK - row, 1)[row : row + 1, :]
             table_ref[head : head + 1, :] = total
-            rest = jnp.sum(far_sum[head], axis=0, keepdims=True)
+            rest = jnp.sum(near_sum[head, :, 2 * BLK :], axis=0, keepdims=True)
             table_ref[heads + head : heads + head + 1, :] = jnp.concatenate(
                 [rest, jnp.zeros_like(rest)], axis=1
             )
@@ -337,13 +330,12 @@
                 full(3 * width), full(3 * width), pl.BlockSpec((8, 2 * BLK), whole),
             ],
             scratch_shapes=[
-                pltpu.VMEM((heads, BLK, 2 * BLK), jnp.float32),
+                pltpu.VMEM((heads, BLK, 3 * BLK), jnp.float32),
                 pltpu.VMEM((heads, length, width), jnp.bfloat16),
                 pltpu.VMEM((heads, length, width), jnp.bfloat16),
                 pltpu.VMEM((2, 8, length), jnp.float32),
                 pltpu.VMEM((2 * width, length), jnp.float32),
-                pltpu.VMEM((heads, BLK, 2 * BLK), jnp.float32),
-                pltpu.VMEM((heads, 8, BLK), jnp.float32),
+                pltpu.VMEM((heads, BLK, 3 * BLK), jnp.float32),
             ],
         ),
         out_shape=[

time: 415 us -> 411 us (level)
  transfers between devices with their start and end apart: 53 -> 53, of which waited for: 25 -> 25; matrix products, arithmetic and copies ran while one was open for 9% -> 9% of each run, Pallas kernels for 29% -> 28%
where the time goes in v2:
time: 411 us; the launch traced here: 407 us
  waiting for transfers between devices  144 us (35%)
  Pallas kernels  129 us (31%)
  starting transfers between devices  61.7 us (15%)
  other arithmetic  29.9 us (7%)
  local copies, waits for them, and re-layouts  26.3 us (6%)
  between operations  15.3 us (4%)
    ppermute x40, waiting for transfers between devices, flip(): return lax.ppermute(value, axis, [(i, i ^ bit) for i in range(size)])  78.2 us
    ppermute x40, starting transfers between devices, flip(): return lax.ppermute(value, axis, [(i, i ^ bit) for i in range(size)])  45 us
    ppermute x3, waiting for transfers between devices, relay(): lax.ppermute(left, 'mp', to_left[:parts - step])  36.1 us
    pallas_call x1, Pallas kernels, attention_backward(): pl.pallas_call(attention_backward_kernel, grid_spec=pltpu.PrefetchScalarG...  30.2 us
    pallas_call x1, Pallas kernels, attention_forward(): pl.pallas_call(attention_forward_kernel, grid_spec=pltpu.PrefetchScalarGr...  25.9 us
    pallas_call x2, Pallas kernels, feed_forward(): pl.pallas_call(functools.partial(feed_kernel, unit=unit, count=len(weight...  23.3 us
    ppermute x3, waiting for transfers between devices, relay(): lax.ppermute(right, 'mp', to_right[step - 1:])  19.2 us
    unnamed x111, local copies, waits for them, and re-layouts  16.1 us
  transfers between devices with their start and end apart: 53, of which 25 were waited for; matrix products, arithmetic and copies ran while one was open for 9% of the time, Pallas kernels for 28%

profile of v2, /device:TPU:0, one launch (start us, length us, event | category | flops | bytes accessed | tf_op | source)
XLA Modules:
  0.0 406.8 jit_solution(13517388473421462573)
XLA Ops:
  8.6 2.6 first_norm.1
  14.3 1.8 constant_dynamic-slice_fusion.8
  16.9 5.0 %collective-permute-start.3 = (bf16[328,1024]{1,0:T(8,128)(2,1)}, bf16[328,1024]{1,0:T(8,128)(2,1)S(1)}, u32[]{:S(2)}, u32[]{:S(2)}) collective-permute-start(bf16[328,1024]{1,0:T(8,128)(2,1)} %pad_maximum_fusion.3), channel_id=1, source_target_pairs={{0,1},{1,2},{2,3},{4,5},{5,6},{6,7},{8,9},{9,10},{10,11},{12,13},{... | collective-permute-start | bytes 2015240 | tf_op jit(solution)/shard_map/ppermute | solution.py:1022
  23.2 1.6 collective-permute-start.1
  29.8 2.0 maximum_bitcast_fusion
  31.8 19.2 %collective-permute-done.3 = bf16[328,1024]{1,0:T(8,128)(2,1)S(1)} collective-permute-done((bf16[328,1024]{1,0:T(8,128)(2,1)}, bf16[328,1024]{1,0:T(8,128)(2,1)S(1)}, u32[]{:S(2)}, u32[]{:S(2)}) %collective-permute-start.3) | collective-permute-done | bytes 671776 | tf_op jit(solution)/shard_map/ppermute | solution.py:1022
  51.0 19.8 %collective-permute-done.5 = bf16[328,1024]{1,0:T(8,128)(2,1)S(1)} collective-permute-done((bf16[328,1024]{1,0:T(8,128)(2,1)}, bf16[328,1024]{1,0:T(8,128)(2,1)S(1)}, u32[]{:S(2)}, u32[]{:S(2)}) %collective-permute-start.5) | collective-permute-done | bytes 671776 | tf_op jit(solution)/shard_map/ppermute | solution.py:1023
  71.7 1.7 collective-permute-start.7
  74.2 2.3 pad_maximum_fusion.2.refs_0_
  76.6 1.5 collective-permute-start.4
  79.4 2.1 constant_dynamic-update-slice_fusion.3
  82.7 4.0 collective-permute-done.7.refs_2_
  87.8 16.3 %collective-permute-done.6 = bf16[328,1024]{1,0:T(8,128)(2,1)} collective-permute-done((bf16[328,1024]{1,0:T(8,128)(2,1)S(1)}, bf16[328,1024]{1,0:T(8,128)(2,1)}, u32[]{:S(2)}, u32[]{:S(2)}) %collective-permute-start.6) | collective-permute-done | bytes 671776 | tf_op jit(solution)/shard_map/ppermute | solution.py:1023
  105.5 1.4 add_bitcast_fusion.refs_3_
  106.8 2.1 collective-permute-start.8
  108.9 1.5 collective-permute-start.10
  111.7 25.9 %attention_forward.1 = (bf16[1536,384]{1,0:T(8,128)(2,1)}, bf16[1536,384]{1,0:T(8,128)(2,1)}, bf16[1536,256]{1,0:T(8,128)(2,1)}, f32[8,1536]{1,0:T(8,128)}, f32[8,1536]{1,0:T(8,128)}) custom-call(s32[1]{0:T(128)} %bitcast.9.cut_ref, bf16[1536,1024]{1,0:T(8,128)(2,1)} %all-gather.2.cloned.1.call-done.rows_ref.normed_ref, bf16[3,1024,256]{2,1,0:T(8,128)(2,1)} %weight_b.1, ...), custom_call_target="tpu_custom_call" | custom-call | flops 1 | bytes 1 | tf_op jit(solution)/shard_map/attention_forward/pallas_call | solution.py:169
  137.7 1.7 select_bitcast_fusion.refs_5_
  140.6 3.8 collective-permute-start.12
  144.6 2.2 collective-permute-start.14
  146.8 9.4 %collective-permute-done.11.refs_6_ = bf16[1,328,1024]{2,1,0:T(8,128)(2,1)S(1)} collective-permute-done((bf16[1,328,1024]{2,1,0:T(8,128)(2,1)S(1)}, bf16[1,328,1024]{2,1,0:T(8,128)(2,1)S(1)}, u32[]{:S(2)}, u32[]{:S(2)}) %collective-permute-start.11) | collective-permute-done | bytes 671776 | tf_op jit(solution)/shard_map/ppermute | solution.py:401
  158.3 3.2 collective-permute-done.13.refs_2_
  161.5 1.4 branch_and_norm.1
  163.0 1.5 collective-permute-start.19
  166.5 11.7 %feed_forward.2 = (bf16[768,1024]{1,0:T(8,128)(2,1)}, bf16[768,1024]{1,0:T(8,128)(2,1)}, bf16[384,1024]{1,0:T(8,128)(2,1)S(1)}, bf16[384,1024]{1,0:T(8,128)(2,1)...) custom-call(bf16[2,256,1024]{2,1,0:T(8,128)(2,1)} %pad_maximum_fusion.2.refs_0_, ...), custom_call_target="tpu_custom_call" | custom-call | flops 1 | bytes 1 | tf_op jit(solution)/shard_map/feed_forward/pallas_call | solution.py:922
  178.1 4.8 %collective-permute-done.19 = bf16[384,1024]{1,0:T(8,128)(2,1)S(1)} collective-permute-done((bf16[384,1024]{1,0:T(8,128)(2,1)S(1)}, bf16[384,1024]{1,0:T(8,128)(2,1)S(1)}, u32[]{:S(2)}, u32[]{:S(2)}) %collective-permute-start.19) | collective-permute-done | bytes 786464 | tf_op jit(solution)/shard_map/ppermute | solution.py:401
  183.0 2.2 collective-permute-done.20
  186.5 11.6 %feed_forward.3 = (bf16[768,1024]{1,0:T(8,128)(2,1)}, bf16[768,1024]{1,0:T(8,128)(2,1)}, bf16[384,1024]{1,0:T(8,128)(2,1)S(1)}, bf16[384,1024]{1,0:T(8,128)(2,1)...) custom-call(bf16[2,256,1024]{2,1,0:T(8,128)(2,1)} %pad_maximum_fusion.2.refs_0_, ...), custom_call_target="tpu_custom_call" | custom-call | flops 1 | bytes 1 | tf_op jit(solution)/shard_map/feed_forward/pallas_call | solution.py:922
  198.6 1.8 collective-permute-done.21
  200.7 1.5 collective-permute-start.24
  203.5 11.9 %weight_grads.1 = (bf16[4,1,2,128,1024]{4,3,2,1,0:T(8,128)(2,1)}, bf16[4,1,2,128,1024]{4,3,2,1,0:T(8,128)(2,1)}) custom-call(s32[1]{0:T(128)} %bitcast.15.part_ref, bf16[768,1024]{1,0:T(8,128)(2,1)} %get-tuple-element.133.act_a, bf16[768,1024]{1,0:T(8,128)(2,1)} %get-tuple-element.142.act_b, bf16[768,1024]{1,0:T(8,128)(2,1)} %get-tuple-element.143.pre_a, ...), custom_call_target="tpu_custom_call" | custom-call | flops 99999997952 | bytes 1 | tf_op jit(solution)/shard_map/weight_grads/pallas_call | solution.py:966
  216.7 3.7 collective-permute-done.24.across_ref
  220.4 2.2 row_grads.1
  224.7 3.8 collective-permute-start.26
  228.6 2.2 collective-permute-start.28
  230.8 4.9 %collective-permute-done.26 = bf16[384,256]{1,0:T(8,128)(2,1)S(1)} collective-permute-done((bf16[384,256]{1,0:T(8,128)(2,1)S(1)}, bf16[384,256]{1,0:T(8,128)(2,1)S(1)}, u32[]{:S(2)}, u32[]{:S(2)}) %collective-permute-start.26) | collective-permute-done | bytes 196640 | tf_op jit(solution)/shard_map/ppermute | solution.py:401
  235.7 9.8 %collective-permute-done.27 = bf16[384,256]{1,0:T(8,128)(2,1)S(1)} collective-permute-done((bf16[384,256]{1,0:T(8,128)(2,1)S(1)}, bf16[384,256]{1,0:T(8,128)(2,1)S(1)}, u32[]{:S(2)}, u32[]{:S(2)}) %collective-permute-start.27) | collective-permute-done | bytes 196640 | tf_op jit(solution)/shard_map/ppermute | solution.py:401
  245.5 3.7 out_weight_grad.1
  250.3 2.3 fusion.4
  254.0 9.8 %collective-permute-done.22 = bf16[4,1,2,128,1024]{4,3,2,1,0:T(8,128)(2,1)} collective-permute-done((bf16[4,1,2,128,1024]{4,3,2,1,0:T(8,128)(2,1)}, bf16[4,1,2,128,1024]{4,3,2,1,0:T(8,128)(2,1)}, u32[]{:S(2)}, u32[]{:S(2)}) %collective-permute-start.22) | collective-permute-done | bytes 2097184 | tf_op jit(solution)/shard_map/ppermute | solution.py:401
  263.8 3.9 add_convert_fusion
  269.4 1.5 collective-permute-start.30
  270.9 30.2 %attention_backward.1 = (bf16[1536,384]{1,0:T(8,128)(2,1)}, bf16[1536,384]{1,0:T(8,128)(2,1)}, f32[8,512]{1,0:T(8,128)}) custom-call(s32[1]{0:T(128)} %bitcast.9.cut_ref, bf16[1536,384]{1,0:T(8,128)(2,1)} %get-tuple-element.125.qkv_a, bf16[1536,384]{1,0:T(8,128)(2,1)} %get-tuple-element.126.qkv_b, bf16[1536,256]{1,0:T(8,128)(2,1)} %bitcast.152, ...), custom_call_target="tpu_custom_call" | custom-call | flops 20000000000 | bytes 1 | tf_op jit(solution)/shard_map/attention_backward/pallas_call | solution.py:320
  301.4 7.1 %qkv_weight_grad.1 = (bf16[512,768]{1,0:T(8,128)(2,1)}, bf16[512,768]{1,0:T(8,128)(2,1)}) custom-call(s32[1]{0:T(128)} %bitcast.core_ref, bf16[1536,1024]{1,0:T(8,128)(2,1)} %all-gather.2.cloned.1.call-done.rows_ref.normed_ref, bf16[1536,384]{1,0:T(8,128)(2,1)} %get-tuple-element.181.grad_a, bf16[1536,384]{1,0:T(8,128)(2,1)} %get-tuple-element.176.grad_b), custom_call_target="tpu_custom_call" | custom-call | flops 1 | bytes 1 | tf_op jit(solution)/shard_map/qkv_weight_grad/pallas_call | solution.py:575
  309.2 8.6 %input_cotangent.1 = (bf16[1536,1024]{1,0:T(8,128)(2,1)}, f32[16,1024]{1,0:T(8,128)}) custom-call(bf16[1536,384]{1,0:T(8,128)(2,1)} %get-tuple-element.181.grad_a, bf16[1536,384]{1,0:T(8,128)(2,1)} %get-tuple-element.176.grad_b, bf16[3,1024,256]{2,1,0:T(8,128)(2,1)} %weight_b.1, bf16[3,1024,256]{2,1,0:T(8,128)(2,1)} %weight_b.1, ...), custom_call_target="tpu_custom_call" | custom-call | flops 1 | bytes 1 | tf_op jit(solution)/shard_map/input_cotangent/pallas_call | solution.py:838
  319.9 6.6 %collective-permute-done.33 = bf16[4,1,32,1024]{3,2,1,0:T(8,128)(2,1)S(1)} collective-permute-done((bf16[4,1,32,1024]{3,2,1,0:T(8,128)(2,1)S(1)}, bf16[4,1,32,1024]{3,2,1,0:T(8,128)(2,1)S(1)}, u32[]{:S(2)}, u32[]{:S(2)}) %collective-permute-start.33) | collective-permute-done | bytes 262176 | tf_op jit(solution)/shard_map/ppermute | solution.py:401
  330.9 2.8 fusion.3
  333.7 1.5 collective-permute-start.37
  335.2 1.8 collective-permute-done.35
  337.2 6.5 %collective-permute-done.37 = f32[10,1024]{1,0:T(8,128)S(1)} collective-permute-done((f32[10,1024]{1,0:T(8,128)S(1)}, f32[10,1024]{1,0:T(8,128)S(1)}, u32[]{:S(2)}, u32[]{:S(2)}) %collective-permute-start.37) | collective-permute-done | bytes 40992 | tf_op jit(solution)/shard_map/ppermute | solution.py:401
  345.4 4.1 collective-permute-start.41
  349.5 2.4 collective-permute-start.43
  351.9 4.7 %collective-permute-done.41 = bf16[32,1024]{1,0:T(8,128)(2,1)S(1)} collective-permute-done((bf16[32,1024]{1,0:T(8,128)(2,1)S(1)}, bf16[32,1024]{1,0:T(8,128)(2,1)S(1)}, u32[]{:S(2)}, u32[]{:S(2)}) %collective-permute-start.41) | collective-permute-done | bytes 65568 | tf_op jit(solution)/shard_map/ppermute | solution.py:401
  356.6 1.5 collective-permute-start.39
  358.2 2.1 collective-permute-done.43
  362.0 3.7 collective-permute-start.45
  366.8 5.6 %collective-permute-done.44 = bf16[512,256]{1,0:T(8,128)(2,1)S(1)} collective-permute-done((bf16[512,256]{1,0:T(8,128)(2,1)S(1)}, bf16[512,256]{1,0:T(8,128)(2,1)S(1)}, u32[]{:S(2)}, u32[]{:S(2)}) %collective-permute-start.44) | collective-permute-done | bytes 262176 | tf_op jit(solution)/shard_map/ppermute | solution.py:790
  372.5 1.5 collective-permute-start.46
  374.0 6.6 %feed_grads_out.1 = (f32[1024,1024]{1,0:T(8,128)}, f32[1024,1024]{1,0:T(8,128)}) custom-call(s32[1]{0:T(128)} %bitcast.core_ref, bf16[4,2,128,1024]{3,2,1,0:T(8,128)(2,1)} %bitcast.136, bf16[4,2,128,1024]{3,2,1,0:T(8,128)(2,1)} %bitcast.144), custom_call_target="tpu_custom_call" | custom-call | flops 1 | bytes 1 | tf_op jit(solution)/shard_map/feed_grads_out/pallas_call | solution.py:478
  382.9 1.9 reduce-scatter.5.cloned.1.call-done.grad_ref
  384.8 2.5 collective-permute-start.48
  388.4 2.0 token_grads.1
  391.4 1.5 collective-permute-start.49
  392.9 3.7 attention_grads_out.1
  (294 shorter events, 55.8 us)
Async XLA Ops:
  7.2 17.6 %copy-start = (f32[32,4]{0,1:T(4,128)S(1)}, f32[32,4]{0,1:T(4,128)}, u32[]{:S(2)}) copy-start(f32[32,4]{0,1:T(4,128)} %param.21) | copy-start | bytes 1540
  7.2 97.0 %all-gather.2.cloned.1.call-start = ((), (), s32[]{:S(2)}) async-start(), calls=%async_computation.2 | async-start | bytes 3932160 | tf_op jit(solution)/shard_map/all_gather | solution.py:1031
  11.2 315.3 %reduce-scatter.3.cloned.1.call-start = ((), (), s32[]{:S(2)}) async-start(), calls=%async_computation.3 | async-start | bytes 2621440 | tf_op jit(solution)/shard_map/reduce_scatter | solution.py:1146
  12.3 10.9 %copy-start.8 = (bf16[384,1024]{1,0:T(8,128)(2,1)S(1)}, bf16[384,1024]{1,0:T(8,128)(2,1)}, u32[]{:S(2)}) copy-start(bf16[384,1024]{1,0:T(8,128)(2,1)} %grad_ref.1) | copy-start | bytes 2359300
  12.3 12.4 %copy-start.43 = (s32[128]{0:T(128)S(1)}, s32[128]{0:T(128)}, u32[]{:S(2)}) copy-start(s32[128]{0:T(128)} %param.17) | copy-start | bytes 1540
  12.4 12.7 %copy-start.39 = (s32[1,1536]{1,0:T(1,128)S(1)}, s32[1,1536]{1,0:T(1,128)}, u32[]{:S(2)}) copy-start(s32[1,1536]{1,0:T(1,128)} %param.16) | copy-start | bytes 18436
  16.1 12.9 %copy-start.16 = (f32[1024]{0:T(1024)S(1)}, f32[1024]{0:T(1024)}, u32[]{:S(2)}) copy-start(f32[1024]{0:T(1024)} %param.23) | copy-start | bytes 12292
  16.1 12.9 %copy-start.40 = (f32[1024]{0:T(1024)S(1)}, f32[1024]{0:T(1024)}, u32[]{:S(2)}) copy-start(f32[1024]{0:T(1024)} %param.24) | copy-start | bytes 12292
  16.9 34.0 %collective-permute-start.3 = (bf16[328,1024]{1,0:T(8,128)(2,1)}, bf16[328,1024]{1,0:T(8,128)(2,1)S(1)}, u32[]{:S(2)}, u32[]{:S(2)}) collective-permute-start(bf16[328,1024]{1,0:T(8,128)(2,1)} %pad_maximum_fusion.3), channel_id=1, source_target_pairs={{0,1},{1,2},{2,3},{4,5},{5,6},{6,7},{8,9},{9,10},{10,11},{12,13},{... | collective-permute-start | bytes 2015240 | tf_op jit(solution)/shard_map/ppermute | solution.py:1022
  21.9 48.9 %collective-permute-start.5 = (bf16[328,1024]{1,0:T(8,128)(2,1)}, bf16[328,1024]{1,0:T(8,128)(2,1)S(1)}, u32[]{:S(2)}, u32[]{:S(2)}) collective-permute-start(bf16[328,1024]{1,0:T(8,128)(2,1)} %pad_maximum_fusion.3), channel_id=1, source_target_pairs={{1,0},{2,1},{3,2},{5,4},{6,5},{7,6},{9,8},{10,9},{11,10},{13,12},{... | collective-permute-start | bytes 2015240 | tf_op jit(solution)/shard_map/ppermute | solution.py:1023
  23.2 53.2 %collective-permute-start.1 = (bf16[384,1024]{1,0:T(8,128)(2,1)S(1)}, bf16[384,1024]{1,0:T(8,128)(2,1)}, u32[]{:S(2)}, u32[]{:S(2)}) collective-permute-start(bf16[384,1024]{1,0:T(8,128)(2,1)S(1)} %copy-done.8), channel_id=1, source_target_pairs={{0,8},{4,12},{8,0},{12,4},{1,9},{5,13},{9,1},{13,5},{2,10},{6,14},... | collective-permute-start | bytes 2359304 | tf_op jit(solution)/shard_map/ppermute | solution.py:401
  24.8 56.7 %collective-permute-start = (bf16[384,1024]{1,0:T(8,128)(2,1)S(1)}, bf16[384,1024]{1,0:T(8,128)(2,1)}, u32[]{:S(2)}, u32[]{:S(2)}) collective-permute-start(bf16[384,1024]{1,0:T(8,128)(2,1)S(1)} %copy-done.8), channel_id=1, source_target_pairs={{0,4},{4,0},{8,12},{12,8},{1,5},{5,1},{9,13},{13,9},{2,6},{6,2},{1... | collective-permute-start | bytes 2359304 | tf_op jit(solution)/shard_map/ppermute | solution.py:401
  71.7 15.0 %collective-permute-start.7 = (bf16[1,328,1024]{2,1,0:T(8,128)(2,1)S(1)}, bf16[1,328,1024]{2,1,0:T(8,128)(2,1)S(1)}, u32[]{:S(2)}, u32[]{:S(2)}) collective-permute-start(bf16[1,328,1024]{2,1,0:T(8,128)(2,1)S(1)} %select_bitcast_fusion.1.refs_1_), channel_id=1, source_target_pairs={{0,16},{16,0},{1,17},{17,1},{2,18},{18,2},{3,19},{19,3},{4,20},{20... | collective-permute-start | bytes 2015240 | tf_op jit(solution)/shard_map/ppermute | solution.py:401
  76.5 10.4 %collective-permute-start.2 = (bf16[384,1024]{1,0:T(8,128)(2,1)}, bf16[384,1024]{1,0:T(8,128)(2,1)S(1)}, u32[]{:S(2)}, u32[]{:S(2)}) collective-permute-start(bf16[384,1024]{1,0:T(8,128)(2,1)} %collective-permute-done.1), channel_id=1, source_target_pairs={{0,4},{4,0},{8,12},{12,8},{1,5},{5,1},{9,13},{13,9},{2,6},{6,2},{1... | collective-permute-start | bytes 2359304 | tf_op jit(solution)/shard_map/ppermute | solution.py:401
  76.6 11.3 %collective-permute-start.4 = (bf16[328,1024]{1,0:T(8,128)(2,1)S(1)}, bf16[328,1024]{1,0:T(8,128)(2,1)}, u32[]{:S(2)}, u32[]{:S(2)}) collective-permute-start(bf16[328,1024]{1,0:T(8,128)(2,1)S(1)} %collective-permute-done.3), channel_id=1, source_target_pairs={{1,2},{2,3},{5,6},{6,7},{9,10},{10,11},{13,14},{14,15},{17,18},{18... | collective-permute-start | bytes 2015240 | tf_op jit(solution)/shard_map/ppermute | solution.py:1022
  78.1 26.1 %collective-permute-start.6 = (bf16[328,1024]{1,0:T(8,128)(2,1)S(1)}, bf16[328,1024]{1,0:T(8,128)(2,1)}, u32[]{:S(2)}, u32[]{:S(2)}) collective-permute-start(bf16[328,1024]{1,0:T(8,128)(2,1)S(1)} %copy-done.23), channel_id=1, source_target_pairs={{1,0},{2,1},{5,4},{6,5},{9,8},{10,9},{13,12},{14,13},{17,16},{18,1... | collective-permute-start | bytes 2015240 | tf_op jit(solution)/shard_map/ppermute | solution.py:1023
  86.7 17.5 %copy-start.4 = (bf16[1,328,1024]{2,1,0:T(8,128)(2,1)}, bf16[1,328,1024]{2,1,0:T(8,128)(2,1)S(1)}, u32[]{:S(2)}) copy-start(bf16[1,328,1024]{2,1,0:T(8,128)(2,1)S(1)} %collective-permute-done.7.refs_2_) | copy-start | bytes 2015236
  86.8 23.7 %collective-permute-start.15 = (bf16[2,64,1024]{2,1,0:T(8,128)(2,1)S(1)}, bf16[2,64,1024]{2,1,0:T(8,128)(2,1)}, u32[]{:S(2)}, u32[]{:S(2)}) collective-permute-start(bf16[2,64,1024]{2,1,0:T(8,128)(2,1)S(1)} %reverse_select_fusion.2), channel_id=1, source_target_pairs={{0,4},{4,0},{8,12},{12,8},{1,5},{5,1},{9,13},{13,9},{2,6},{6,2},{1... | collective-permute-start | bytes 786440 | tf_op jit(solution)/shard_map/ppermute | solution.py:401
  104.2 33.5 %collective-permute-start.9 = (bf16[328,1024]{1,0:T(8,128)(2,1)}, bf16[328,1024]{1,0:T(8,128)(2,1)}, u32[]{:S(2)}, u32[]{:S(2)}) collective-permute-start(bf16[328,1024]{1,0:T(8,128)(2,1)} %collective-permute-done.6), channel_id=1, source_target_pairs={{1,0},{5,4},{9,8},{13,12},{17,16},{21,20},{25,24},{29,28}} | collective-permute-start | bytes 2015240 | tf_op jit(solution)/shard_map/ppermute | solution.py:1023
  106.8 30.8 %collective-permute-start.8 = (bf16[328,1024]{1,0:T(8,128)(2,1)}, bf16[328,1024]{1,0:T(8,128)(2,1)}, u32[]{:S(2)}, u32[]{:S(2)}) collective-permute-start(bf16[328,1024]{1,0:T(8,128)(2,1)} %collective-permute-done.4), channel_id=1, source_target_pairs={{2,3},{6,7},{10,11},{14,15},{18,19},{22,23},{26,27},{30,31}} | collective-permute-start | bytes 2015240 | tf_op jit(solution)/shard_map/ppermute | solution.py:1022
  108.9 28.7 %collective-permute-start.10 = (bf16[1,328,1024]{2,1,0:T(8,128)(2,1)S(1)}, bf16[1,328,1024]{2,1,0:T(8,128)(2,1)S(1)}, u32[]{:S(2)}, u32[]{:S(2)}) collective-permute-start(bf16[1,328,1024]{2,1,0:T(8,128)(2,1)S(1)} %add_bitcast_fusion.refs_3_), channel_id=1, source_target_pairs={{0,16},{16,0},{1,17},{17,1},{2,18},{18,2},{3,19},{19,3},{4,20},{20... | collective-permute-start | bytes 2015240 | tf_op jit(solution)/shard_map/ppermute | solution.py:401
  139.4 16.9 %collective-permute-start.11 = (bf16[1,328,1024]{2,1,0:T(8,128)(2,1)S(1)}, bf16[1,328,1024]{2,1,0:T(8,128)(2,1)S(1)}, u32[]{:S(2)}, u32[]{:S(2)}) collective-permute-start(bf16[1,328,1024]{2,1,0:T(8,128)(2,1)S(1)} %select_bitcast_fusion.refs_5_), channel_id=1, source_target_pairs={{0,16},{16,0},{1,17},{17,1},{2,18},{18,2},{3,19},{19,3},{4,20},{20... | collective-permute-start | bytes 2015240 | tf_op jit(solution)/shard_map/ppermute | solution.py:401
  140.2 16.3 %collective-permute-start.16 = (bf16[2,64,1024]{2,1,0:T(8,128)(2,1)S(1)}, bf16[2,64,1024]{2,1,0:T(8,128)(2,1)S(1)}, u32[]{:S(2)}, u32[]{:S(2)}) collective-permute-start(bf16[2,64,1024]{2,1,0:T(8,128)(2,1)S(1)} %reverse_select_fusion.1), channel_id=1, source_target_pairs={{0,4},{4,0},{8,12},{12,8},{1,5},{5,1},{9,13},{13,9},{2,6},{6,2},{1... | collective-permute-start | bytes 786440 | tf_op jit(solution)/shard_map/ppermute | solution.py:401
  140.6 17.7 %collective-permute-start.12 = (bf16[384,256]{1,0:T(8,128)(2,1)S(1)}, bf16[384,256]{1,0:T(8,128)(2,1)S(1)}, u32[]{:S(2)}, u32[]{:S(2)}) collective-permute-start(bf16[384,256]{1,0:T(8,128)(2,1)S(1)} %get-tuple-element.267), channel_id=1, source_target_pairs={{0,1},{1,0},{2,3},{3,2},{4,5},{5,4},{6,7},{7,6},{8,9},{9,8},{10,11... | collective-permute-start | bytes 589832 | tf_op jit(solution)/shard_map/ppermute | solution.py:401
  144.3 17.1 %collective-permute-start.13 = (bf16[384,256]{1,0:T(8,128)(2,1)S(1)}, bf16[384,256]{1,0:T(8,128)(2,1)S(1)}, u32[]{:S(2)}, u32[]{:S(2)}) collective-permute-start(bf16[384,256]{1,0:T(8,128)(2,1)S(1)} %get-tuple-element.266), channel_id=1, source_target_pairs={{0,2},{1,3},{2,0},{3,1},{4,6},{5,7},{6,4},{7,5},{8,10},{9,11},{10,... | collective-permute-start | bytes 589832 | tf_op jit(solution)/shard_map/ppermute | solution.py:401
  144.6 16.8 %collective-permute-start.14 = (bf16[384,256]{1,0:T(8,128)(2,1)S(1)}, bf16[384,256]{1,0:T(8,128)(2,1)S(1)}, u32[]{:S(2)}, u32[]{:S(2)}) collective-permute-start(bf16[384,256]{1,0:T(8,128)(2,1)S(1)} %get-tuple-element.265), channel_id=1, source_target_pairs={{0,3},{1,2},{2,1},{3,0},{4,7},{5,6},{6,5},{7,4},{8,11},{9,10},{10,... | collective-permute-start | bytes 589832 | tf_op jit(solution)/shard_map/ppermute | solution.py:401
  156.4 1.6 collective-permute-start.17
  162.9 2.4 collective-permute-start.18
  163.0 20.0 %collective-permute-start.19 = (bf16[384,1024]{1,0:T(8,128)(2,1)S(1)}, bf16[384,1024]{1,0:T(8,128)(2,1)S(1)}, u32[]{:S(2)}, u32[]{:S(2)}) collective-permute-start(bf16[384,1024]{1,0:T(8,128)(2,1)S(1)} %get-tuple-element.132), channel_id=1, source_target_pairs={{0,8},{4,12},{8,0},{12,4},{1,9},{5,13},{9,1},{13,5},{2,10},{6,14},... | collective-permute-start | bytes 2359304 | tf_op jit(solution)/shard_map/ppermute | solution.py:401
  183.0 2.3 collective-permute-start.20
  198.1 2.4 collective-permute-start.21
  198.3 22.1 %collective-permute-start.23 = (bf16[384,1024]{1,0:T(8,128)(2,1)}, bf16[384,1024]{1,0:T(8,128)(2,1)S(1)}, u32[]{:S(2)}, u32[]{:S(2)}) collective-permute-start(bf16[384,1024]{1,0:T(8,128)(2,1)} %get-tuple-element.146), channel_id=1, source_target_pairs={{0,4},{4,0},{8,12},{12,8},{1,5},{5,1},{9,13},{13,9},{2,6},{6,2},{1... | collective-permute-start | bytes 2359304 | tf_op jit(solution)/shard_map/ppermute | solution.py:401
  200.7 19.7 %collective-permute-start.24 = (bf16[384,1024]{1,0:T(8,128)(2,1)S(1)}, bf16[384,1024]{1,0:T(8,128)(2,1)S(1)}, u32[]{:S(2)}, u32[]{:S(2)}) collective-permute-start(bf16[384,1024]{1,0:T(8,128)(2,1)S(1)} %add_convert_fusion.3), channel_id=1, source_target_pairs={{0,8},{4,12},{8,0},{12,4},{1,9},{5,13},{9,1},{13,5},{2,10},{6,14},... | collective-permute-start | bytes 2359304 | tf_op jit(solution)/shard_map/ppermute | solution.py:401
  203.5 41.9 %collective-permute-start.25 = (bf16[2,384,1024]{2,1,0:T(8,128)(2,1)}, bf16[2,384,1024]{2,1,0:T(8,128)(2,1)}, u32[]{:S(2)}, u32[]{:S(2)}) collective-permute-start(bf16[2,384,1024]{2,1,0:T(8,128)(2,1)} %pad_maximum_fusion.1), channel_id=1, source_target_pairs={{0,4},{4,0},{8,12},{12,8},{1,5},{5,1},{9,13},{13,9},{2,6},{6,2},{1... | collective-permute-start | bytes 4718600 | tf_op jit(solution)/shard_map/ppermute | solution.py:401
  203.5 16.9 %copy-start.9 = (bf16[384,1024]{1,0:T(8,128)(2,1)S(1)}, bf16[384,1024]{1,0:T(8,128)(2,1)}, u32[]{:S(2)}) copy-start(bf16[384,1024]{1,0:T(8,128)(2,1)} %grad_ref.1) | copy-start | bytes 2359300
  215.5 48.4 %collective-permute-start.22 = (bf16[4,1,2,128,1024]{4,3,2,1,0:T(8,128)(2,1)}, bf16[4,1,2,128,1024]{4,3,2,1,0:T(8,128)(2,1)}, u32[]{:S(2)}, u32[]{:S(2)}) collective-permute-start(bf16[4,1,2,128,1024]{4,3,2,1,0:T(8,128)(2,1)} %get-tuple-element.145), channel_id=1, source_target_pairs={{0,16},{16,0},{1,17},{17,1},{2,18},{18,2},{3,19},{19,3},{4,20},{20... | collective-permute-start | bytes 6291464 | tf_op jit(solution)/shard_map/ppermute | solution.py:401
  224.7 11.0 %collective-permute-start.26 = (bf16[384,256]{1,0:T(8,128)(2,1)S(1)}, bf16[384,256]{1,0:T(8,128)(2,1)S(1)}, u32[]{:S(2)}, u32[]{:S(2)}) collective-permute-start(bf16[384,256]{1,0:T(8,128)(2,1)S(1)} %get-tuple-element.152), channel_id=1, source_target_pairs={{0,1},{1,0},{2,3},{3,2},{4,5},{5,4},{6,7},{7,6},{8,9},{9,8},{10,11... | collective-permute-start | bytes 589832 | tf_op jit(solution)/shard_map/ppermute | solution.py:401
  228.4 17.0 %collective-permute-start.27 = (bf16[384,256]{1,0:T(8,128)(2,1)S(1)}, bf16[384,256]{1,0:T(8,128)(2,1)S(1)}, u32[]{:S(2)}, u32[]{:S(2)}) collective-permute-start(bf16[384,256]{1,0:T(8,128)(2,1)S(1)} %get-tuple-element.153), channel_id=1, source_target_pairs={{0,2},{1,3},{2,0},{3,1},{4,6},{5,7},{6,4},{7,5},{8,10},{9,11},{10,... | collective-permute-start | bytes 589832 | tf_op jit(solution)/shard_map/ppermute | solution.py:401
  228.6 16.9 %collective-permute-start.28 = (bf16[384,256]{1,0:T(8,128)(2,1)S(1)}, bf16[384,256]{1,0:T(8,128)(2,1)S(1)}, u32[]{:S(2)}, u32[]{:S(2)}) collective-permute-start(bf16[384,256]{1,0:T(8,128)(2,1)S(1)} %get-tuple-element.154), channel_id=1, source_target_pairs={{0,3},{1,2},{2,1},{3,0},{4,7},{5,6},{6,5},{7,4},{8,11},{9,10},{10,... | collective-permute-start | bytes 589832 | tf_op jit(solution)/shard_map/ppermute | solution.py:401
  249.1 3.5 collective-permute-start.29
  253.1 10.8 %copy-start.24 = (bf16[4,1,2,128,1024]{4,3,2,1,0:T(8,128)(2,1)S(1)}, bf16[4,1,2,128,1024]{4,3,2,1,0:T(8,128)(2,1)}, u32[]{:S(2)}) copy-start(bf16[4,1,2,128,1024]{4,3,2,1,0:T(8,128)(2,1)} %get-tuple-element.147) | copy-start | bytes 6291460
  267.7 117.1 %reduce-scatter.5.cloned.1.call-start = ((), (), s32[]{:S(2)}) async-start(), calls=%async_computation.4 | async-start | bytes 3932160 | tf_op jit(solution)/shard_map/reduce_scatter | solution.py:1173
  268.9 32.3 %collective-permute-start.31 = (bf16[384,1024]{1,0:T(8,128)(2,1)S(1)}, bf16[384,1024]{1,0:T(8,128)(2,1)}, u32[]{:S(2)}, u32[]{:S(2)}) collective-permute-start(bf16[384,1024]{1,0:T(8,128)(2,1)S(1)} %copy-done.31), channel_id=1, source_target_pairs={{0,8},{4,12},{8,0},{12,4},{1,9},{5,13},{9,1},{13,5},{2,10},{6,14},... | collective-permute-start | bytes 2359304 | tf_op jit(solution)/shard_map/ppermute | solution.py:401
  269.4 31.7 %collective-permute-start.30 = (bf16[4,2,32,1024]{3,2,1,0:T(8,128)(2,1)}, bf16[4,2,32,1024]{3,2,1,0:T(8,128)(2,1)S(1)}, u32[]{:S(2)}, u32[]{:S(2)}) collective-permute-start(bf16[4,2,32,1024]{3,2,1,0:T(8,128)(2,1)} %get-tuple-element.170), channel_id=1, source_target_pairs={{0,8},{4,12},{8,0},{12,4},{1,9},{5,13},{9,1},{13,5},{2,10},{6,14},... | collective-permute-start | bytes 1572872 | tf_op jit(solution)/shard_map/ppermute | solution.py:401
  308.5 18.0 %collective-permute-start.32 = (bf16[512,768]{1,0:T(8,128)(2,1)}, bf16[512,768]{1,0:T(8,128)(2,1)}, u32[]{:S(2)}, u32[]{:S(2)}) collective-permute-start(bf16[512,768]{1,0:T(8,128)(2,1)} %get-tuple-element.180), channel_id=1, source_target_pairs={{0,4},{4,0},{8,12},{12,8},{1,5},{5,1},{9,13},{13,9},{2,6},{6,2},{1... | collective-permute-start | bytes 2359304 | tf_op jit(solution)/shard_map/ppermute | solution.py:401
  317.8 8.7 %collective-permute-start.33 = (bf16[4,1,32,1024]{3,2,1,0:T(8,128)(2,1)S(1)}, bf16[4,1,32,1024]{3,2,1,0:T(8,128)(2,1)S(1)}, u32[]{:S(2)}, u32[]{:S(2)}) collective-permute-start(bf16[4,1,32,1024]{3,2,1,0:T(8,128)(2,1)S(1)} %get-tuple-element.269), channel_id=1, source_target_pairs={{0,16},{16,0},{1,17},{17,1},{2,18},{18,2},{3,19},{19,3},{4,20},{20... | collective-permute-start | bytes 786440 | tf_op jit(solution)/shard_map/ppermute | solution.py:401
  327.5 6.2 %collective-permute-start.36 = (f32[10,1024]{1,0:T(8,128)S(1)}, f32[10,1024]{1,0:T(8,128)S(1)}, u32[]{:S(2)}, u32[]{:S(2)}) collective-permute-start(f32[10,1024]{1,0:T(8,128)S(1)} %reshape.212), channel_id=1, source_target_pairs={{0,4},{4,0},{8,12},{12,8},{1,5},{5,1},{9,13},{13,9},{2,6},{6,2},{1... | collective-permute-start | bytes 122888 | tf_op jit(solution)/shard_map/ppermute | solution.py:401
  327.6 9.5 %collective-permute-start.35 = (bf16[256,1024]{1,0:T(8,128)(2,1)}, bf16[256,1024]{1,0:T(8,128)(2,1)S(1)}, u32[]{:S(2)}, u32[]{:S(2)}) collective-permute-start(bf16[256,1024]{1,0:T(8,128)(2,1)} %bitcast.155), channel_id=1, source_target_pairs={{0,16},{4,12},{8,24},{12,4},{16,0},{20,28},{24,8},{28,20},{1,17},{... | collective-permute-start | bytes 1572872 | tf_op jit(solution)/shard_map/ppermute | solution.py:790
  330.2 13.5 %collective-permute-start.34 = (bf16[2,128,768]{2,1,0:T(8,128)(2,1)S(1)}, bf16[2,128,768]{2,1,0:T(8,128)(2,1)S(1)}, u32[]{:S(2)}, u32[]{:S(2)}) collective-permute-start(bf16[2,128,768]{2,1,0:T(8,128)(2,1)S(1)} %dynamic-slice_bitcast_fusion.2), channel_id=1, source_target_pairs={{0,8},{4,12},{8,0},{12,4},{1,9},{5,13},{9,1},{13,5},{2,10},{6,14},... | collective-permute-start | bytes 1179656 | tf_op jit(solution)/shard_map/ppermute | solution.py:401
  333.7 10.0 %collective-permute-start.37 = (f32[10,1024]{1,0:T(8,128)S(1)}, f32[10,1024]{1,0:T(8,128)S(1)}, u32[]{:S(2)}, u32[]{:S(2)}) collective-permute-start(f32[10,1024]{1,0:T(8,128)S(1)} %add.244), channel_id=1, source_target_pairs={{0,8},{4,12},{8,0},{12,4},{1,9},{5,13},{9,1},{13,5},{2,10},{6,14},... | collective-permute-start | bytes 122888 | tf_op jit(solution)/shard_map/ppermute | solution.py:401
  343.7 17.9 %collective-permute-start.40 = (bf16[2,256,1024]{2,1,0:T(8,128)(2,1)S(1)}, bf16[2,256,1024]{2,1,0:T(8,128)(2,1)S(1)}, u32[]{:S(2)}, u32[]{:S(2)}) collective-permute-start(bf16[2,256,1024]{2,1,0:T(8,128)(2,1)S(1)} %maximum_select_fusion.1), channel_id=1, source_target_pairs={{0,8},{4,20},{8,0},{12,28},{16,24},{20,4},{24,16},{28,12},{1,9},{5... | collective-permute-start | bytes 3145736 | tf_op jit(solution)/shard_map/ppermute | solution.py:790
  344.6 17.1 %collective-permute-start.38 = (bf16[1,128,768]{2,1,0:T(8,128)(2,1)S(1)}, bf16[1,128,768]{2,1,0:T(8,128)(2,1)S(1)}, u32[]{:S(2)}, u32[]{:S(2)}) collective-permute-start(bf16[1,128,768]{2,1,0:T(8,128)(2,1)S(1)} %constant_dynamic-slice_fusion.2), channel_id=1, source_target_pairs={{0,16},{16,0},{1,17},{17,1},{2,18},{18,2},{3,19},{19,3},{4,20},{20... | collective-permute-start | bytes 589832 | tf_op jit(solution)/shard_map/ppermute | solution.py:401
  345.4 11.2 %collective-permute-start.41 = (bf16[32,1024]{1,0:T(8,128)(2,1)S(1)}, bf16[32,1024]{1,0:T(8,128)(2,1)S(1)}, u32[]{:S(2)}, u32[]{:S(2)}) collective-permute-start(bf16[32,1024]{1,0:T(8,128)(2,1)S(1)} %get-tuple-element.273), channel_id=1, source_target_pairs={{0,1},{1,0},{2,3},{3,2},{4,5},{5,4},{6,7},{7,6},{8,9},{9,8},{10,11... | collective-permute-start | bytes 196616 | tf_op jit(solution)/shard_map/ppermute | solution.py:401
  349.5 8.7 %collective-permute-start.42 = (bf16[32,1024]{1,0:T(8,128)(2,1)S(1)}, bf16[32,1024]{1,0:T(8,128)(2,1)S(1)}, u32[]{:S(2)}, u32[]{:S(2)}) collective-permute-start(bf16[32,1024]{1,0:T(8,128)(2,1)S(1)} %get-tuple-element.272), channel_id=1, source_target_pairs={{0,2},{1,3},{2,0},{3,1},{4,6},{5,7},{6,4},{7,5},{8,10},{9,11},{10,... | collective-permute-start | bytes 196616 | tf_op jit(solution)/shard_map/ppermute | solution.py:401
  349.5 10.8 %collective-permute-start.43 = (bf16[32,1024]{1,0:T(8,128)(2,1)S(1)}, bf16[32,1024]{1,0:T(8,128)(2,1)S(1)}, u32[]{:S(2)}, u32[]{:S(2)}) collective-permute-start(bf16[32,1024]{1,0:T(8,128)(2,1)S(1)} %get-tuple-element.271), channel_id=1, source_target_pairs={{0,3},{1,2},{2,1},{3,0},{4,7},{5,6},{6,5},{7,4},{8,11},{9,10},{10,... | collective-permute-start | bytes 196616 | tf_op jit(solution)/shard_map/ppermute | solution.py:401
  356.6 5.0 %collective-permute-start.39 = (f32[10,1024]{1,0:T(8,128)S(1)}, f32[10,1024]{1,0:T(8,128)S(1)}, u32[]{:S(2)}, u32[]{:S(2)}) collective-permute-start(f32[10,1024]{1,0:T(8,128)S(1)} %add.251), channel_id=1, source_target_pairs={{0,16},{16,0},{1,17},{17,1},{2,18},{18,2},{3,19},{19,3},{4,20},{20... | collective-permute-start | bytes 122888 | tf_op jit(solution)/shard_map/ppermute | solution.py:401
  362.0 11.9 %copy-start.17 = (bf16[2,2,256,1024]{3,2,1,0:T(8,128)(2,1)}, bf16[2,2,256,1024]{3,2,1,0:T(8,128)(2,1)S(1)}, u32[]{:S(2)}) copy-start(bf16[2,2,256,1024]{3,2,1,0:T(8,128)(2,1)S(1)} %maximum_select_fusion) | copy-start | bytes 6291460
  362.0 10.4 %collective-permute-start.45 = (bf16[2,2,256,1024]{3,2,1,0:T(8,128)(2,1)S(1)}, bf16[2,2,256,1024]{3,2,1,0:T(8,128)(2,1)S(1)}, u32[]{:S(2)}, u32[]{:S(2)}) collective-permute-start(bf16[2,2,256,1024]{3,2,1,0:T(8,128)(2,1)S(1)} %maximum_select_fusion), channel_id=1, source_target_pairs={{0,4},{4,0},{8,12},{12,8},{1,5},{5,1},{9,13},{13,9},{2,6},{6,2},{1... | collective-permute-start | bytes 6291464 | tf_op jit(solution)/shard_map/ppermute | solution.py:401
  365.9 6.4 %collective-permute-start.44 = (bf16[512,256]{1,0:T(8,128)(2,1)S(1)}, bf16[512,256]{1,0:T(8,128)(2,1)S(1)}, u32[]{:S(2)}, u32[]{:S(2)}) collective-permute-start(bf16[512,256]{1,0:T(8,128)(2,1)S(1)} %constant_dynamic-update-slice_fusion.10), channel_id=1, source_target_pairs={{0,16},{4,12},{8,24},{12,4},{16,0},{20,28},{24,8},{28,20},{1,17},{... | collective-permute-start | bytes 786440 | tf_op jit(solution)/shard_map/ppermute | solution.py:790
  372.5 9.2 %collective-permute-start.46 = (bf16[2,512,256]{2,1,0:T(8,128)(2,1)S(1)}, bf16[2,512,256]{2,1,0:T(8,128)(2,1)S(1)}, u32[]{:S(2)}, u32[]{:S(2)}) collective-permute-start(bf16[2,512,256]{2,1,0:T(8,128)(2,1)S(1)} %maximum_select_fusion.6), channel_id=1, source_target_pairs={{0,8},{4,20},{8,0},{12,28},{16,24},{20,4},{24,16},{28,12},{1,9},{5... | collective-permute-start | bytes 1572872 | tf_op jit(solution)/shard_map/ppermute | solution.py:790
  374.0 13.3 %copy-start.11 = (f32[384,1024]{1,0:T(8,128)S(1)}, f32[384,1024]{1,0:T(8,128)}, u32[]{:S(2)}) copy-start(f32[384,1024]{1,0:T(8,128)} %copy-done.10) | copy-start | bytes 4718596
  384.8 5.6 %collective-permute-start.47 = (bf16[2,2,512,256]{3,2,1,0:T(8,128)(2,1)}, bf16[2,2,512,256]{3,2,1,0:T(8,128)(2,1)S(1)}, u32[]{:S(2)}, u32[]{:S(2)}) collective-permute-start(bf16[2,2,512,256]{3,2,1,0:T(8,128)(2,1)} %maximum_select_fusion.2), channel_id=1, source_target_pairs={{0,4},{4,0},{8,12},{12,8},{1,5},{5,1},{9,13},{13,9},{2,6},{6,2},{1... | collective-permute-start | bytes 3145736 | tf_op jit(solution)/shard_map/ppermute | solution.py:401
  384.8 5.6 %collective-permute-start.48 = (f32[10,1024]{1,0:T(8,128)S(1)}, f32[10,1024]{1,0:T(8,128)S(1)}, u32[]{:S(2)}, u32[]{:S(2)}) collective-permute-start(f32[10,1024]{1,0:T(8,128)S(1)} %add.257), channel_id=1, source_target_pairs={{0,1},{1,0},{2,3},{3,2},{4,5},{5,4},{6,7},{7,6},{8,9},{9,8},{10,11... | collective-permute-start | bytes 122888 | tf_op jit(solution)/shard_map/ppermute | solution.py:401
  391.4 6.5 %collective-permute-start.49 = (f32[10,1024]{1,0:T(8,128)S(1)}, f32[10,1024]{1,0:T(8,128)S(1)}, u32[]{:S(2)}, u32[]{:S(2)}) collective-permute-start(f32[10,1024]{1,0:T(8,128)S(1)} %add.258), channel_id=1, source_target_pairs={{0,2},{1,3},{2,0},{3,1},{4,6},{5,7},{6,4},{7,5},{8,10},{9,11},{10,... | collective-permute-start | bytes 122888 | tf_op jit(solution)/shard_map/ppermute | solution.py:401
  (34 other events, 119.9 us)
Sparse Core Ops, SparseCore 0:
  11.3 84.3 all-gather.1
  267.9 44.5 reduce-scatter.2
  320.0 64.7 reduce-scatter.4

commit v3 on v2

--- a/solution.py
+++ b/solution.py
@@ -188,7 +188,9 @@
         out_shape=[jax.ShapeDtypeStruct((length, 3 * width), jnp.bfloat16)] * 2
         + [jax.ShapeDtypeStruct((length, 2 * width), jnp.bfloat16)]
         + [jax.ShapeDtypeStruct((8, length), jnp.float32)] * 2,
-        compiler_params=pltpu.CompilerParams(dimension_semantics=("arbitrary",)),
+        compiler_params=pltpu.CompilerParams(
+            dimension_semantics=("arbitrary",), vmem_limit_bytes=54 * 1024 * 1024
+        ),
         cost_estimate=LIGHT,
         name="attention_forward",
     )(cut, normed, weights, near_bias)

time: 411 us -> 407 us (level)
    unnamed x111 -> x109, local copies, waits for them, and re-layouts: 16.1 us -> 15 us
  transfers between devices with their start and end apart: 53 -> 53, of which waited for: 25 -> 25; matrix products, arithmetic and copies ran while one was open for 9% -> 11% of each run, Pallas kernels for 28% -> 28%
where the time goes in v3:
time: 407 us; the launch traced here: 403 us
  waiting for transfers between devices  141 us (35%)
  Pallas kernels  128 us (31%)
  starting transfers between devices  60.5 us (15%)
  other arithmetic  29.3 us (7%)
  local copies, waits for them, and re-layouts  28.6 us (7%)
  between operations  15.2 us (4%)
    ppermute x40, waiting for transfers between devices, flip(): return lax.ppermute(value, axis, [(i, i ^ bit) for i in range(size)])  76.5 us
    ppermute x40, starting transfers between devices, flip(): return lax.ppermute(value, axis, [(i, i ^ bit) for i in range(size)])  45.4 us
    ppermute x3, waiting for transfers between devices, relay(): lax.ppermute(left, 'mp', to_left[:parts - step])  35.3 us
    pallas_call x1, Pallas kernels, attention_backward(): pl.pallas_call(attention_backward_kernel, grid_spec=pltpu.PrefetchScalarG...  29.9 us
    pallas_call x1, Pallas kernels, attention_forward(): pl.pallas_call(attention_forward_kernel, grid_spec=pltpu.PrefetchScalarGr...  25.7 us
    pallas_call x2, Pallas kernels, feed_forward(): pl.pallas_call(functools.partial(feed_kernel, unit=unit, count=len(weight...  23 us
    ppermute x3, waiting for transfers between devices, relay(): lax.ppermute(right, 'mp', to_right[step - 1:])  19.2 us
    unnamed x109, local copies, waits for them, and re-layouts  15 us
  transfers between devices with their start and end apart: 53, of which 25 were waited for; matrix products, arithmetic and copies ran while one was open for 11% of the time, Pallas kernels for 28%

profile of v3, /device:TPU:0, one launch (start us, length us, event | category | flops | bytes accessed | tf_op | source)
XLA Modules:
  0.0 402.9 jit_solution(8412670208968959121)
XLA Ops:
  7.2 1.3 pad_maximum_fusion.7.line_ref
  8.6 2.6 first_norm.1
  14.3 1.8 constant_dynamic-slice_fusion.8
  16.9 5.0 %collective-permute-start.3 = (bf16[328,1024]{1,0:T(8,128)(2,1)}, bf16[328,1024]{1,0:T(8,128)(2,1)S(1)}, u32[]{:S(2)}, u32[]{:S(2)}) collective-permute-start(bf16[328,1024]{1,0:T(8,128)(2,1)} %pad_maximum_fusion.3), channel_id=1, source_target_pairs={{0,1},{1,2},{2,3},{4,5},{5,6},{6,7},{8,9},{9,10},{10,11},{12,13},{... | collective-permute-start | bytes 2015240 | tf_op jit(solution)/shard_map/ppermute | solution.py:1024
  23.2 1.6 collective-permute-start.1
  29.8 1.9 maximum_bitcast_fusion
  31.8 19.2 %collective-permute-done.3 = bf16[328,1024]{1,0:T(8,128)(2,1)S(1)} collective-permute-done((bf16[328,1024]{1,0:T(8,128)(2,1)}, bf16[328,1024]{1,0:T(8,128)(2,1)S(1)}, u32[]{:S(2)}, u32[]{:S(2)}) %collective-permute-start.3) | collective-permute-done | bytes 671776 | tf_op jit(solution)/shard_map/ppermute | solution.py:1024
  51.0 19.8 %collective-permute-done.5 = bf16[328,1024]{1,0:T(8,128)(2,1)S(1)} collective-permute-done((bf16[328,1024]{1,0:T(8,128)(2,1)}, bf16[328,1024]{1,0:T(8,128)(2,1)S(1)}, u32[]{:S(2)}, u32[]{:S(2)}) %collective-permute-start.5) | collective-permute-done | bytes 671776 | tf_op jit(solution)/shard_map/ppermute | solution.py:1025
  71.7 1.7 collective-permute-start.7
  74.2 2.3 pad_maximum_fusion.2.refs_0_
  78.6 2.1 constant_dynamic-update-slice_fusion.3
  81.9 4.8 %collective-permute-done.7.refs_2_ = bf16[1,328,1024]{2,1,0:T(8,128)(2,1)S(1)} collective-permute-done((bf16[1,328,1024]{2,1,0:T(8,128)(2,1)S(1)}, bf16[1,328,1024]{2,1,0:T(8,128)(2,1)S(1)}, u32[]{:S(2)}, u32[]{:S(2)}) %collective-permute-start.7) | collective-permute-done | bytes 671776 | tf_op jit(solution)/shard_map/ppermute | solution.py:403
  88.7 15.5 %collective-permute-done.6 = bf16[328,1024]{1,0:T(8,128)(2,1)} collective-permute-done((bf16[328,1024]{1,0:T(8,128)(2,1)S(1)}, bf16[328,1024]{1,0:T(8,128)(2,1)}, u32[]{:S(2)}, u32[]{:S(2)}) %collective-permute-start.6) | collective-permute-done | bytes 671776 | tf_op jit(solution)/shard_map/ppermute | solution.py:1025
  104.2 1.4 collective-permute-start.9
  105.6 1.4 add_bitcast_fusion.refs_3_
  108.2 1.5 collective-permute-start.10
  110.0 25.7 %attention_forward.1 = (bf16[1536,384]{1,0:T(8,128)(2,1)}, bf16[1536,384]{1,0:T(8,128)(2,1)}, bf16[1536,256]{1,0:T(8,128)(2,1)}, f32[8,1536]{1,0:T(8,128)}, f32[8,1536]{1,0:T(8,128)}) custom-call(s32[1]{0:T(128)} %bitcast.9.cut_ref, bf16[1536,1024]{1,0:T(8,128)(2,1)} %all-gather.2.cloned.1.call-done.rows_ref.normed_ref, bf16[3,1024,256]{2,1,0:T(8,128)(2,1)} %weight_b.1, ...), custom_call_target="tpu_custom_call" | custom-call | flops 1 | bytes 1 | tf_op jit(solution)/shard_map/attention_forward/pallas_call | solution.py:169
  137.0 2.7 collective-permute-start.12
  141.0 1.4 collective-permute-start.14
  142.4 10.2 %collective-permute-done.11.refs_6_ = bf16[1,328,1024]{2,1,0:T(8,128)(2,1)S(1)} collective-permute-done((bf16[1,328,1024]{2,1,0:T(8,128)(2,1)S(1)}, bf16[1,328,1024]{2,1,0:T(8,128)(2,1)S(1)}, u32[]{:S(2)}, u32[]{:S(2)}) %collective-permute-start.11) | collective-permute-done | bytes 671776 | tf_op jit(solution)/shard_map/ppermute | solution.py:403
  154.7 2.2 collective-permute-done.13.refs_2_
  156.9 1.4 branch_and_norm.1
  158.4 1.6 collective-permute-start.19
  161.9 11.5 %feed_forward.2 = (bf16[768,1024]{1,0:T(8,128)(2,1)}, bf16[768,1024]{1,0:T(8,128)(2,1)}, bf16[384,1024]{1,0:T(8,128)(2,1)S(1)}, bf16[384,1024]{1,0:T(8,128)(2,1)...) custom-call(bf16[2,256,1024]{2,1,0:T(8,128)(2,1)} %pad_maximum_fusion.2.refs_0_, ...), custom_call_target="tpu_custom_call" | custom-call | flops 1 | bytes 1 | tf_op jit(solution)/shard_map/feed_forward/pallas_call | solution.py:924
  173.4 5.0 %collective-permute-done.19 = bf16[384,1024]{1,0:T(8,128)(2,1)S(1)} collective-permute-done((bf16[384,1024]{1,0:T(8,128)(2,1)S(1)}, bf16[384,1024]{1,0:T(8,128)(2,1)S(1)}, u32[]{:S(2)}, u32[]{:S(2)}) %collective-permute-start.19) | collective-permute-done | bytes 786464 | tf_op jit(solution)/shard_map/ppermute | solution.py:403
  178.4 2.2 collective-permute-done.20
  181.9 11.4 %feed_forward.3 = (bf16[768,1024]{1,0:T(8,128)(2,1)}, bf16[768,1024]{1,0:T(8,128)(2,1)}, bf16[384,1024]{1,0:T(8,128)(2,1)S(1)}, bf16[384,1024]{1,0:T(8,128)(2,1)...) custom-call(bf16[2,256,1024]{2,1,0:T(8,128)(2,1)} %pad_maximum_fusion.2.refs_0_, ...), custom_call_target="tpu_custom_call" | custom-call | flops 1 | bytes 1 | tf_op jit(solution)/shard_map/feed_forward/pallas_call | solution.py:924
  193.9 1.8 collective-permute-done.21
  196.9 1.5 collective-permute-start.24
  199.7 11.9 %weight_grads.1 = (bf16[4,1,2,128,1024]{4,3,2,1,0:T(8,128)(2,1)}, bf16[4,1,2,128,1024]{4,3,2,1,0:T(8,128)(2,1)}) custom-call(s32[1]{0:T(128)} %bitcast.15.part_ref, bf16[768,1024]{1,0:T(8,128)(2,1)} %get-tuple-element.133.act_a, bf16[768,1024]{1,0:T(8,128)(2,1)} %get-tuple-element.142.act_b, bf16[768,1024]{1,0:T(8,128)(2,1)} %get-tuple-element.143.pre_a, ...), custom_call_target="tpu_custom_call" | custom-call | flops 99999997952 | bytes 1 | tf_op jit(solution)/shard_map/weight_grads/pallas_call | solution.py:968
  212.8 3.9 collective-permute-done.24.across_ref
  216.7 2.2 row_grads.1
  220.9 3.8 collective-permute-start.26
  225.7 1.5 collective-permute-start.28
  227.2 4.9 %collective-permute-done.26 = bf16[384,256]{1,0:T(8,128)(2,1)S(1)} collective-permute-done((bf16[384,256]{1,0:T(8,128)(2,1)S(1)}, bf16[384,256]{1,0:T(8,128)(2,1)S(1)}, u32[]{:S(2)}, u32[]{:S(2)}) %collective-permute-start.26) | collective-permute-done | bytes 196640 | tf_op jit(solution)/shard_map/ppermute | solution.py:403
  232.1 9.7 %collective-permute-done.27 = bf16[384,256]{1,0:T(8,128)(2,1)S(1)} collective-permute-done((bf16[384,256]{1,0:T(8,128)(2,1)S(1)}, bf16[384,256]{1,0:T(8,128)(2,1)S(1)}, u32[]{:S(2)}, u32[]{:S(2)}) %collective-permute-start.27) | collective-permute-done | bytes 196640 | tf_op jit(solution)/shard_map/ppermute | solution.py:403
  241.8 3.6 out_weight_grad.1
  249.2 2.3 fusion.4
  252.0 7.9 %collective-permute-done.22 = bf16[4,1,2,128,1024]{4,3,2,1,0:T(8,128)(2,1)} collective-permute-done((bf16[4,1,2,128,1024]{4,3,2,1,0:T(8,128)(2,1)}, bf16[4,1,2,128,1024]{4,3,2,1,0:T(8,128)(2,1)}, u32[]{:S(2)}, u32[]{:S(2)}) %collective-permute-start.22) | collective-permute-done | bytes 2097184 | tf_op jit(solution)/shard_map/ppermute | solution.py:403
  259.9 3.9 add_convert_fusion
  264.5 1.5 collective-permute-start.30
  266.0 29.9 %attention_backward.1 = (bf16[1536,384]{1,0:T(8,128)(2,1)}, bf16[1536,384]{1,0:T(8,128)(2,1)}, f32[8,512]{1,0:T(8,128)}) custom-call(s32[1]{0:T(128)} %bitcast.9.cut_ref, bf16[1536,384]{1,0:T(8,128)(2,1)} %get-tuple-element.125.qkv_a, bf16[1536,384]{1,0:T(8,128)(2,1)} %get-tuple-element.126.qkv_b, bf16[1536,256]{1,0:T(8,128)(2,1)} %bitcast.44.grad_ref, ...), custom_call_target="tpu_custom_call" | custom-call | flops 20000000000 | bytes 1 | tf_op jit(solution)/shard_map/attention_backward/pallas_call | solution.py:322
  296.9 7.1 %qkv_weight_grad.1 = (bf16[512,768]{1,0:T(8,128)(2,1)}, bf16[512,768]{1,0:T(8,128)(2,1)}) custom-call(s32[1]{0:T(128)} %bitcast.core_ref, bf16[1536,1024]{1,0:T(8,128)(2,1)} %all-gather.2.cloned.1.call-done.rows_ref.normed_ref, bf16[1536,384]{1,0:T(8,128)(2,1)} %get-tuple-element.181.grad_a, bf16[1536,384]{1,0:T(8,128)(2,1)} %get-tuple-element.176.grad_b), custom_call_target="tpu_custom_call" | custom-call | flops 1 | bytes 1 | tf_op jit(solution)/shard_map/qkv_weight_grad/pallas_call | solution.py:577
  304.7 8.6 %input_cotangent.1 = (bf16[1536,1024]{1,0:T(8,128)(2,1)}, f32[16,1024]{1,0:T(8,128)}) custom-call(bf16[1536,384]{1,0:T(8,128)(2,1)} %get-tuple-element.181.grad_a, bf16[1536,384]{1,0:T(8,128)(2,1)} %get-tuple-element.176.grad_b, bf16[3,1024,256]{2,1,0:T(8,128)(2,1)} %weight_b.1, bf16[3,1024,256]{2,1,0:T(8,128)(2,1)} %weight_b.1, ...), custom_call_target="tpu_custom_call" | custom-call | flops 1 | bytes 1 | tf_op jit(solution)/shard_map/input_cotangent/pallas_call | solution.py:840
  315.3 6.7 %collective-permute-done.33 = bf16[4,1,32,1024]{3,2,1,0:T(8,128)(2,1)S(1)} collective-permute-done((bf16[4,1,32,1024]{3,2,1,0:T(8,128)(2,1)S(1)}, bf16[4,1,32,1024]{3,2,1,0:T(8,128)(2,1)S(1)}, u32[]{:S(2)}, u32[]{:S(2)}) %collective-permute-start.33) | collective-permute-done | bytes 262176 | tf_op jit(solution)/shard_map/ppermute | solution.py:403
  324.4 1.6 add_convert_fusion.2
  326.6 2.9 fusion.3
  329.4 1.6 collective-permute-start.37
  331.0 1.5 collective-permute-done.35
  332.7 6.7 %collective-permute-done.37 = f32[10,1024]{1,0:T(8,128)S(1)} collective-permute-done((f32[10,1024]{1,0:T(8,128)S(1)}, f32[10,1024]{1,0:T(8,128)S(1)}, u32[]{:S(2)}, u32[]{:S(2)}) %collective-permute-start.37) | collective-permute-done | bytes 40992 | tf_op jit(solution)/shard_map/ppermute | solution.py:403
  341.3 3.7 collective-permute-start.41
  346.1 1.4 collective-permute-start.43
  347.5 4.6 %collective-permute-done.41 = bf16[32,1024]{1,0:T(8,128)(2,1)S(1)} collective-permute-done((bf16[32,1024]{1,0:T(8,128)(2,1)S(1)}, bf16[32,1024]{1,0:T(8,128)(2,1)S(1)}, u32[]{:S(2)}, u32[]{:S(2)}) %collective-permute-start.41) | collective-permute-done | bytes 65568 | tf_op jit(solution)/shard_map/ppermute | solution.py:403
  352.2 1.4 collective-permute-start.39
  353.6 3.5 collective-permute-done.43
  357.6 3.8 collective-permute-start.45
  363.6 5.4 %collective-permute-done.44 = bf16[512,256]{1,0:T(8,128)(2,1)S(1)} collective-permute-done((bf16[512,256]{1,0:T(8,128)(2,1)S(1)}, bf16[512,256]{1,0:T(8,128)(2,1)S(1)}, u32[]{:S(2)}, u32[]{:S(2)}) %collective-permute-start.44) | collective-permute-done | bytes 262176 | tf_op jit(solution)/shard_map/ppermute | solution.py:792
  369.1 1.4 collective-permute-start.46
  370.5 6.6 %feed_grads_out.1 = (f32[1024,1024]{1,0:T(8,128)}, f32[1024,1024]{1,0:T(8,128)}) custom-call(s32[1]{0:T(128)} %bitcast.core_ref, bf16[4,2,128,1024]{3,2,1,0:T(8,128)(2,1)} %bitcast.136, bf16[4,2,128,1024]{3,2,1,0:T(8,128)(2,1)} %bitcast.144), custom_call_target="tpu_custom_call" | custom-call | flops 1 | bytes 1 | tf_op jit(solution)/shard_map/feed_grads_out/pallas_call | solution.py:480
  379.5 1.5 reduce-scatter.5.cloned.1.call-done.grad_ref
  380.9 2.6 collective-permute-start.48
  384.6 1.9 token_grads.1
  387.5 2.6 collective-permute-start.49
  390.1 3.7 attention_grads_out.1
  (292 shorter events, 57.7 us)
Async XLA Ops:
  7.2 17.6 %copy-start = (f32[32,4]{0,1:T(4,128)S(1)}, f32[32,4]{0,1:T(4,128)}, u32[]{:S(2)}) copy-start(f32[32,4]{0,1:T(4,128)} %param.21) | copy-start | bytes 1540
  7.2 97.0 %all-gather.2.cloned.1.call-start = ((), (), s32[]{:S(2)}) async-start(), calls=%async_computation.2 | async-start | bytes 3932160 | tf_op jit(solution)/shard_map/all_gather | solution.py:1033
  11.2 310.9 %reduce-scatter.3.cloned.1.call-start = ((), (), s32[]{:S(2)}) async-start(), calls=%async_computation.3 | async-start | bytes 2621440 | tf_op jit(solution)/shard_map/reduce_scatter | solution.py:1148
  12.3 10.9 %copy-start.4 = (bf16[384,1024]{1,0:T(8,128)(2,1)S(1)}, bf16[384,1024]{1,0:T(8,128)(2,1)}, u32[]{:S(2)}) copy-start(bf16[384,1024]{1,0:T(8,128)(2,1)} %grad_ref.1) | copy-start | bytes 2359300
  12.3 12.4 %copy-start.42 = (s32[128]{0:T(128)S(1)}, s32[128]{0:T(128)}, u32[]{:S(2)}) copy-start(s32[128]{0:T(128)} %param.17) | copy-start | bytes 1540
  12.4 12.7 %copy-start.38 = (s32[1,1536]{1,0:T(1,128)S(1)}, s32[1,1536]{1,0:T(1,128)}, u32[]{:S(2)}) copy-start(s32[1,1536]{1,0:T(1,128)} %param.16) | copy-start | bytes 18436
  16.1 12.9 %copy-start.12 = (f32[1024]{0:T(1024)S(1)}, f32[1024]{0:T(1024)}, u32[]{:S(2)}) copy-start(f32[1024]{0:T(1024)} %param.23) | copy-start | bytes 12292
  16.1 12.9 %copy-start.39 = (f32[1024]{0:T(1024)S(1)}, f32[1024]{0:T(1024)}, u32[]{:S(2)}) copy-start(f32[1024]{0:T(1024)} %param.24) | copy-start | bytes 12292
  16.9 34.0 %collective-permute-start.3 = (bf16[328,1024]{1,0:T(8,128)(2,1)}, bf16[328,1024]{1,0:T(8,128)(2,1)S(1)}, u32[]{:S(2)}, u32[]{:S(2)}) collective-permute-start(bf16[328,1024]{1,0:T(8,128)(2,1)} %pad_maximum_fusion.3), channel_id=1, source_target_pairs={{0,1},{1,2},{2,3},{4,5},{5,6},{6,7},{8,9},{9,10},{10,11},{12,13},{... | collective-permute-start | bytes 2015240 | tf_op jit(solution)/shard_map/ppermute | solution.py:1024
  21.9 48.9 %collective-permute-start.5 = (bf16[328,1024]{1,0:T(8,128)(2,1)}, bf16[328,1024]{1,0:T(8,128)(2,1)S(1)}, u32[]{:S(2)}, u32[]{:S(2)}) collective-permute-start(bf16[328,1024]{1,0:T(8,128)(2,1)} %pad_maximum_fusion.3), channel_id=1, source_target_pairs={{1,0},{2,1},{3,2},{5,4},{6,5},{7,6},{9,8},{10,9},{11,10},{13,12},{... | collective-permute-start | bytes 2015240 | tf_op jit(solution)/shard_map/ppermute | solution.py:1025
  23.2 53.2 %collective-permute-start.1 = (bf16[384,1024]{1,0:T(8,128)(2,1)S(1)}, bf16[384,1024]{1,0:T(8,128)(2,1)}, u32[]{:S(2)}, u32[]{:S(2)}) collective-permute-start(bf16[384,1024]{1,0:T(8,128)(2,1)S(1)} %copy-done.4), channel_id=1, source_target_pairs={{0,8},{4,12},{8,0},{12,4},{1,9},{5,13},{9,1},{13,5},{2,10},{6,14},... | collective-permute-start | bytes 2359304 | tf_op jit(solution)/shard_map/ppermute | solution.py:403
  24.8 55.9 %collective-permute-start = (bf16[384,1024]{1,0:T(8,128)(2,1)S(1)}, bf16[384,1024]{1,0:T(8,128)(2,1)}, u32[]{:S(2)}, u32[]{:S(2)}) collective-permute-start(bf16[384,1024]{1,0:T(8,128)(2,1)S(1)} %copy-done.4), channel_id=1, source_target_pairs={{0,4},{4,0},{8,12},{12,8},{1,5},{5,1},{9,13},{13,9},{2,6},{6,2},{1... | collective-permute-start | bytes 2359304 | tf_op jit(solution)/shard_map/ppermute | solution.py:403
  71.7 15.0 %collective-permute-start.7 = (bf16[1,328,1024]{2,1,0:T(8,128)(2,1)S(1)}, bf16[1,328,1024]{2,1,0:T(8,128)(2,1)S(1)}, u32[]{:S(2)}, u32[]{:S(2)}) collective-permute-start(bf16[1,328,1024]{2,1,0:T(8,128)(2,1)S(1)} %select_bitcast_fusion.1.refs_1_), channel_id=1, source_target_pairs={{0,16},{16,0},{1,17},{17,1},{2,18},{18,2},{3,19},{19,3},{4,20},{20... | collective-permute-start | bytes 2015240 | tf_op jit(solution)/shard_map/ppermute | solution.py:403
  76.5 10.4 %collective-permute-start.2 = (bf16[384,1024]{1,0:T(8,128)(2,1)}, bf16[384,1024]{1,0:T(8,128)(2,1)S(1)}, u32[]{:S(2)}, u32[]{:S(2)}) collective-permute-start(bf16[384,1024]{1,0:T(8,128)(2,1)} %collective-permute-done.1), channel_id=1, source_target_pairs={{0,4},{4,0},{8,12},{12,8},{1,5},{5,1},{9,13},{13,9},{2,6},{6,2},{1... | collective-permute-start | bytes 2359304 | tf_op jit(solution)/shard_map/ppermute | solution.py:403
  76.6 11.3 %collective-permute-start.4 = (bf16[328,1024]{1,0:T(8,128)(2,1)S(1)}, bf16[328,1024]{1,0:T(8,128)(2,1)S(1)}, u32[]{:S(2)}, u32[]{:S(2)}) collective-permute-start(bf16[328,1024]{1,0:T(8,128)(2,1)S(1)} %collective-permute-done.3), channel_id=1, source_target_pairs={{1,2},{2,3},{5,6},{6,7},{9,10},{10,11},{13,14},{14,15},{17,18},{18... | collective-permute-start | bytes 2015240 | tf_op jit(solution)/shard_map/ppermute | solution.py:1024
  77.3 26.9 %collective-permute-start.6 = (bf16[328,1024]{1,0:T(8,128)(2,1)S(1)}, bf16[328,1024]{1,0:T(8,128)(2,1)}, u32[]{:S(2)}, u32[]{:S(2)}) collective-permute-start(bf16[328,1024]{1,0:T(8,128)(2,1)S(1)} %copy-done.19), channel_id=1, source_target_pairs={{1,0},{2,1},{5,4},{6,5},{9,8},{10,9},{13,12},{14,13},{17,16},{18,1... | collective-permute-start | bytes 2015240 | tf_op jit(solution)/shard_map/ppermute | solution.py:1025
  86.8 23.0 %collective-permute-start.15 = (bf16[2,64,1024]{2,1,0:T(8,128)(2,1)S(1)}, bf16[2,64,1024]{2,1,0:T(8,128)(2,1)S(1)}, u32[]{:S(2)}, u32[]{:S(2)}) collective-permute-start(bf16[2,64,1024]{2,1,0:T(8,128)(2,1)S(1)} %reverse_select_fusion.2), channel_id=1, source_target_pairs={{0,4},{4,0},{8,12},{12,8},{1,5},{5,1},{9,13},{13,9},{2,6},{6,2},{1... | collective-permute-start | bytes 786440 | tf_op jit(solution)/shard_map/ppermute | solution.py:403
  104.2 31.5 %collective-permute-start.9 = (bf16[328,1024]{1,0:T(8,128)(2,1)}, bf16[328,1024]{1,0:T(8,128)(2,1)S(1)}, u32[]{:S(2)}, u32[]{:S(2)}) collective-permute-start(bf16[328,1024]{1,0:T(8,128)(2,1)} %collective-permute-done.6), channel_id=1, source_target_pairs={{1,0},{5,4},{9,8},{13,12},{17,16},{21,20},{25,24},{29,28}} | collective-permute-start | bytes 2015240 | tf_op jit(solution)/shard_map/ppermute | solution.py:1025
  107.0 28.7 %collective-permute-start.8 = (bf16[328,1024]{1,0:T(8,128)(2,1)S(1)}, bf16[328,1024]{1,0:T(8,128)(2,1)S(1)}, u32[]{:S(2)}, u32[]{:S(2)}) collective-permute-start(bf16[328,1024]{1,0:T(8,128)(2,1)S(1)} %copy-done.32), channel_id=1, source_target_pairs={{2,3},{6,7},{10,11},{14,15},{18,19},{22,23},{26,27},{30,31}} | collective-permute-start | bytes 2015240 | tf_op jit(solution)/shard_map/ppermute | solution.py:1024
  108.2 27.5 %collective-permute-start.10 = (bf16[1,328,1024]{2,1,0:T(8,128)(2,1)S(1)}, bf16[1,328,1024]{2,1,0:T(8,128)(2,1)S(1)}, u32[]{:S(2)}, u32[]{:S(2)}) collective-permute-start(bf16[1,328,1024]{2,1,0:T(8,128)(2,1)S(1)} %add_bitcast_fusion.refs_3_), channel_id=1, source_target_pairs={{0,16},{16,0},{1,17},{17,1},{2,18},{18,2},{3,19},{19,3},{4,20},{20... | collective-permute-start | bytes 2015240 | tf_op jit(solution)/shard_map/ppermute | solution.py:403
  109.9 25.8 %copy-start.20 = (bf16[328,1024]{1,0:T(8,128)(2,1)S(1)}, bf16[328,1024]{1,0:T(8,128)(2,1)}, u32[]{:S(2)}) copy-start(bf16[328,1024]{1,0:T(8,128)(2,1)} %copy-done.18) | copy-start | bytes 2015236
  135.9 16.8 %collective-permute-start.11 = (bf16[1,328,1024]{2,1,0:T(8,128)(2,1)S(1)}, bf16[1,328,1024]{2,1,0:T(8,128)(2,1)S(1)}, u32[]{:S(2)}, u32[]{:S(2)}) collective-permute-start(bf16[1,328,1024]{2,1,0:T(8,128)(2,1)S(1)} %select_bitcast_fusion.refs_5_), channel_id=1, source_target_pairs={{0,16},{16,0},{1,17},{17,1},{2,18},{18,2},{3,19},{19,3},{4,20},{20... | collective-permute-start | bytes 2015240 | tf_op jit(solution)/shard_map/ppermute | solution.py:403
  136.6 16.2 %collective-permute-start.16 = (bf16[2,64,1024]{2,1,0:T(8,128)(2,1)S(1)}, bf16[2,64,1024]{2,1,0:T(8,128)(2,1)S(1)}, u32[]{:S(2)}, u32[]{:S(2)}) collective-permute-start(bf16[2,64,1024]{2,1,0:T(8,128)(2,1)S(1)} %reverse_select_fusion.1), channel_id=1, source_target_pairs={{0,4},{4,0},{8,12},{12,8},{1,5},{5,1},{9,13},{13,9},{2,6},{6,2},{1... | collective-permute-start | bytes 786440 | tf_op jit(solution)/shard_map/ppermute | solution.py:403
  137.0 17.6 %collective-permute-start.12 = (bf16[384,256]{1,0:T(8,128)(2,1)S(1)}, bf16[384,256]{1,0:T(8,128)(2,1)S(1)}, u32[]{:S(2)}, u32[]{:S(2)}) collective-permute-start(bf16[384,256]{1,0:T(8,128)(2,1)S(1)} %get-tuple-element.267), channel_id=1, source_target_pairs={{0,1},{1,0},{2,3},{3,2},{4,5},{5,4},{6,7},{7,6},{8,9},{9,8},{10,11... | collective-permute-start | bytes 589832 | tf_op jit(solution)/shard_map/ppermute | solution.py:403
  139.8 17.1 %collective-permute-start.13 = (bf16[384,256]{1,0:T(8,128)(2,1)S(1)}, bf16[384,256]{1,0:T(8,128)(2,1)S(1)}, u32[]{:S(2)}, u32[]{:S(2)}) collective-permute-start(bf16[384,256]{1,0:T(8,128)(2,1)S(1)} %get-tuple-element.266), channel_id=1, source_target_pairs={{0,2},{1,3},{2,0},{3,1},{4,6},{5,7},{6,4},{7,5},{8,10},{9,11},{10,... | collective-permute-start | bytes 589832 | tf_op jit(solution)/shard_map/ppermute | solution.py:403
  141.0 15.9 %collective-permute-start.14 = (bf16[384,256]{1,0:T(8,128)(2,1)S(1)}, bf16[384,256]{1,0:T(8,128)(2,1)S(1)}, u32[]{:S(2)}, u32[]{:S(2)}) collective-permute-start(bf16[384,256]{1,0:T(8,128)(2,1)S(1)} %get-tuple-element.265), channel_id=1, source_target_pairs={{0,3},{1,2},{2,1},{3,0},{4,7},{5,6},{6,5},{7,4},{8,11},{9,10},{10,... | collective-permute-start | bytes 589832 | tf_op jit(solution)/shard_map/ppermute | solution.py:403
  152.7 1.6 collective-permute-start.17
  158.3 2.4 collective-permute-start.18
  158.4 20.0 %collective-permute-start.19 = (bf16[384,1024]{1,0:T(8,128)(2,1)S(1)}, bf16[384,1024]{1,0:T(8,128)(2,1)S(1)}, u32[]{:S(2)}, u32[]{:S(2)}) collective-permute-start(bf16[384,1024]{1,0:T(8,128)(2,1)S(1)} %get-tuple-element.132), channel_id=1, source_target_pairs={{0,8},{4,12},{8,0},{12,4},{1,9},{5,13},{9,1},{13,5},{2,10},{6,14},... | collective-permute-start | bytes 2359304 | tf_op jit(solution)/shard_map/ppermute | solution.py:403
  178.4 2.3 collective-permute-start.20
  193.3 2.4 collective-permute-start.21
  193.5 23.1 %collective-permute-start.23 = (bf16[384,1024]{1,0:T(8,128)(2,1)}, bf16[384,1024]{1,0:T(8,128)(2,1)S(1)}, u32[]{:S(2)}, u32[]{:S(2)}) collective-permute-start(bf16[384,1024]{1,0:T(8,128)(2,1)} %get-tuple-element.146), channel_id=1, source_target_pairs={{0,4},{4,0},{8,12},{12,8},{1,5},{5,1},{9,13},{13,9},{2,6},{6,2},{1... | collective-permute-start | bytes 2359304 | tf_op jit(solution)/shard_map/ppermute | solution.py:403
  196.9 19.8 %collective-permute-start.24 = (bf16[384,1024]{1,0:T(8,128)(2,1)}, bf16[384,1024]{1,0:T(8,128)(2,1)S(1)}, u32[]{:S(2)}, u32[]{:S(2)}) collective-permute-start(bf16[384,1024]{1,0:T(8,128)(2,1)} %add_convert_fusion.3), channel_id=1, source_target_pairs={{0,8},{4,12},{8,0},{12,4},{1,9},{5,13},{9,1},{13,5},{2,10},{6,14},... | collective-permute-start | bytes 2359304 | tf_op jit(solution)/shard_map/ppermute | solution.py:403
  199.6 42.2 %collective-permute-start.25 = (bf16[2,384,1024]{2,1,0:T(8,128)(2,1)}, bf16[2,384,1024]{2,1,0:T(8,128)(2,1)}, u32[]{:S(2)}, u32[]{:S(2)}) collective-permute-start(bf16[2,384,1024]{2,1,0:T(8,128)(2,1)} %pad_maximum_fusion.1), channel_id=1, source_target_pairs={{0,4},{4,0},{8,12},{12,8},{1,5},{5,1},{9,13},{13,9},{2,6},{6,2},{1... | collective-permute-start | bytes 4718600 | tf_op jit(solution)/shard_map/ppermute | solution.py:403
  199.6 17.0 %copy-start.5 = (bf16[384,1024]{1,0:T(8,128)(2,1)S(1)}, bf16[384,1024]{1,0:T(8,128)(2,1)}, u32[]{:S(2)}) copy-start(bf16[384,1024]{1,0:T(8,128)(2,1)} %grad_ref.1) | copy-start | bytes 2359300
  211.6 48.4 %collective-permute-start.22 = (bf16[4,1,2,128,1024]{4,3,2,1,0:T(8,128)(2,1)}, bf16[4,1,2,128,1024]{4,3,2,1,0:T(8,128)(2,1)}, u32[]{:S(2)}, u32[]{:S(2)}) collective-permute-start(bf16[4,1,2,128,1024]{4,3,2,1,0:T(8,128)(2,1)} %get-tuple-element.145), channel_id=1, source_target_pairs={{0,16},{16,0},{1,17},{17,1},{2,18},{18,2},{3,19},{19,3},{4,20},{20... | collective-permute-start | bytes 6291464 | tf_op jit(solution)/shard_map/ppermute | solution.py:403
  220.9 11.2 %collective-permute-start.26 = (bf16[384,256]{1,0:T(8,128)(2,1)S(1)}, bf16[384,256]{1,0:T(8,128)(2,1)S(1)}, u32[]{:S(2)}, u32[]{:S(2)}) collective-permute-start(bf16[384,256]{1,0:T(8,128)(2,1)S(1)} %get-tuple-element.152), channel_id=1, source_target_pairs={{0,1},{1,0},{2,3},{3,2},{4,5},{5,4},{6,7},{7,6},{8,9},{9,8},{10,11... | collective-permute-start | bytes 589832 | tf_op jit(solution)/shard_map/ppermute | solution.py:403
  224.7 17.2 %collective-permute-start.27 = (bf16[384,256]{1,0:T(8,128)(2,1)S(1)}, bf16[384,256]{1,0:T(8,128)(2,1)S(1)}, u32[]{:S(2)}, u32[]{:S(2)}) collective-permute-start(bf16[384,256]{1,0:T(8,128)(2,1)S(1)} %get-tuple-element.153), channel_id=1, source_target_pairs={{0,2},{1,3},{2,0},{3,1},{4,6},{5,7},{6,4},{7,5},{8,10},{9,11},{10,... | collective-permute-start | bytes 589832 | tf_op jit(solution)/shard_map/ppermute | solution.py:403
  225.7 16.1 %collective-permute-start.28 = (bf16[384,256]{1,0:T(8,128)(2,1)S(1)}, bf16[384,256]{1,0:T(8,128)(2,1)S(1)}, u32[]{:S(2)}, u32[]{:S(2)}) collective-permute-start(bf16[384,256]{1,0:T(8,128)(2,1)S(1)} %get-tuple-element.154), channel_id=1, source_target_pairs={{0,3},{1,2},{2,1},{3,0},{4,7},{5,6},{6,5},{7,4},{8,11},{9,10},{10,... | collective-permute-start | bytes 589832 | tf_op jit(solution)/shard_map/ppermute | solution.py:403
  245.5 6.0 %collective-permute-start.29 = (bf16[4,128,1024]{2,1,0:T(8,128)(2,1)}, bf16[4,128,1024]{2,1,0:T(8,128)(2,1)S(1)}, u32[]{:S(2)}, u32[]{:S(2)}) collective-permute-start(bf16[4,128,1024]{2,1,0:T(8,128)(2,1)} %get-tuple-element.164), channel_id=1, source_target_pairs={{0,4},{4,0},{8,12},{12,8},{1,5},{5,1},{9,13},{13,9},{2,6},{6,2},{1... | collective-permute-start | bytes 3145736 | tf_op jit(solution)/shard_map/ppermute | solution.py:403
  263.8 117.1 %reduce-scatter.5.cloned.1.call-start = ((), (), s32[]{:S(2)}) async-start(), calls=%async_computation.4 | async-start | bytes 3932160 | tf_op jit(solution)/shard_map/reduce_scatter | solution.py:1175
  263.9 32.0 %collective-permute-start.31 = (bf16[384,1024]{1,0:T(8,128)(2,1)}, bf16[384,1024]{1,0:T(8,128)(2,1)}, u32[]{:S(2)}, u32[]{:S(2)}) collective-permute-start(bf16[384,1024]{1,0:T(8,128)(2,1)} %fusion.4), channel_id=1, source_target_pairs={{0,8},{4,12},{8,0},{12,4},{1,9},{5,13},{9,1},{13,5},{2,10},{6,14},... | collective-permute-start | bytes 2359304 | tf_op jit(solution)/shard_map/ppermute | solution.py:403
  264.5 31.4 %collective-permute-start.30 = (bf16[4,2,32,1024]{3,2,1,0:T(8,128)(2,1)S(1)}, bf16[4,2,32,1024]{3,2,1,0:T(8,128)(2,1)S(1)}, u32[]{:S(2)}, u32[]{:S(2)}) collective-permute-start(bf16[4,2,32,1024]{3,2,1,0:T(8,128)(2,1)S(1)} %get-tuple-element.170), channel_id=1, source_target_pairs={{0,8},{4,12},{8,0},{12,4},{1,9},{5,13},{9,1},{13,5},{2,10},{6,14},... | collective-permute-start | bytes 1572872 | tf_op jit(solution)/shard_map/ppermute | solution.py:403
  304.0 18.0 %collective-permute-start.32 = (bf16[512,768]{1,0:T(8,128)(2,1)}, bf16[512,768]{1,0:T(8,128)(2,1)}, u32[]{:S(2)}, u32[]{:S(2)}) collective-permute-start(bf16[512,768]{1,0:T(8,128)(2,1)} %get-tuple-element.180), channel_id=1, source_target_pairs={{0,4},{4,0},{8,12},{12,8},{1,5},{5,1},{9,13},{13,9},{2,6},{6,2},{1... | collective-permute-start | bytes 2359304 | tf_op jit(solution)/shard_map/ppermute | solution.py:403
  313.3 8.8 %collective-permute-start.33 = (bf16[4,1,32,1024]{3,2,1,0:T(8,128)(2,1)S(1)}, bf16[4,1,32,1024]{3,2,1,0:T(8,128)(2,1)S(1)}, u32[]{:S(2)}, u32[]{:S(2)}) collective-permute-start(bf16[4,1,32,1024]{3,2,1,0:T(8,128)(2,1)S(1)} %get-tuple-element.269), channel_id=1, source_target_pairs={{0,16},{16,0},{1,17},{17,1},{2,18},{18,2},{3,19},{19,3},{4,20},{20... | collective-permute-start | bytes 786440 | tf_op jit(solution)/shard_map/ppermute | solution.py:403
  323.0 6.4 %collective-permute-start.36 = (f32[10,1024]{1,0:T(8,128)S(1)}, f32[10,1024]{1,0:T(8,128)S(1)}, u32[]{:S(2)}, u32[]{:S(2)}) collective-permute-start(f32[10,1024]{1,0:T(8,128)S(1)} %reshape.212), channel_id=1, source_target_pairs={{0,4},{4,0},{8,12},{12,8},{1,5},{5,1},{9,13},{13,9},{2,6},{6,2},{1... | collective-permute-start | bytes 122888 | tf_op jit(solution)/shard_map/ppermute | solution.py:403
  323.1 9.5 %collective-permute-start.35 = (bf16[256,1024]{1,0:T(8,128)(2,1)}, bf16[256,1024]{1,0:T(8,128)(2,1)S(1)}, u32[]{:S(2)}, u32[]{:S(2)}) collective-permute-start(bf16[256,1024]{1,0:T(8,128)(2,1)} %bitcast.154), channel_id=1, source_target_pairs={{0,16},{4,12},{8,24},{12,4},{16,0},{20,28},{24,8},{28,20},{1,17},{... | collective-permute-start | bytes 1572872 | tf_op jit(solution)/shard_map/ppermute | solution.py:792
  326.0 13.5 %collective-permute-start.34 = (bf16[2,128,768]{2,1,0:T(8,128)(2,1)S(1)}, bf16[2,128,768]{2,1,0:T(8,128)(2,1)S(1)}, u32[]{:S(2)}, u32[]{:S(2)}) collective-permute-start(bf16[2,128,768]{2,1,0:T(8,128)(2,1)S(1)} %dynamic-slice_bitcast_fusion.2), channel_id=1, source_target_pairs={{0,8},{4,12},{8,0},{12,4},{1,9},{5,13},{9,1},{13,5},{2,10},{6,14},... | collective-permute-start | bytes 1179656 | tf_op jit(solution)/shard_map/ppermute | solution.py:403
  329.4 10.6 %copy-start.35 = (bf16[4,1,32,1024]{3,2,1,0:T(8,128)(2,1)S(1)}, bf16[4,1,32,1024]{3,2,1,0:T(8,128)(2,1)}, u32[]{:S(2)}) copy-start(bf16[4,1,32,1024]{3,2,1,0:T(8,128)(2,1)} %copy-done.34) | copy-start | bytes 786436
  329.4 10.1 %collective-permute-start.37 = (f32[10,1024]{1,0:T(8,128)S(1)}, f32[10,1024]{1,0:T(8,128)S(1)}, u32[]{:S(2)}, u32[]{:S(2)}) collective-permute-start(f32[10,1024]{1,0:T(8,128)S(1)} %add.244), channel_id=1, source_target_pairs={{0,8},{4,12},{8,0},{12,4},{1,9},{5,13},{9,1},{13,5},{2,10},{6,14},... | collective-permute-start | bytes 122888 | tf_op jit(solution)/shard_map/ppermute | solution.py:403
  339.5 17.7 %collective-permute-start.40 = (bf16[2,256,1024]{2,1,0:T(8,128)(2,1)S(1)}, bf16[2,256,1024]{2,1,0:T(8,128)(2,1)S(1)}, u32[]{:S(2)}, u32[]{:S(2)}) collective-permute-start(bf16[2,256,1024]{2,1,0:T(8,128)(2,1)S(1)} %maximum_select_fusion.1), channel_id=1, source_target_pairs={{0,8},{4,20},{8,0},{12,28},{16,24},{20,4},{24,16},{28,12},{1,9},{5... | collective-permute-start | bytes 3145736 | tf_op jit(solution)/shard_map/ppermute | solution.py:792
  340.2 17.0 %collective-permute-start.38 = (bf16[1,128,768]{2,1,0:T(8,128)(2,1)S(1)}, bf16[1,128,768]{2,1,0:T(8,128)(2,1)}, u32[]{:S(2)}, u32[]{:S(2)}) collective-permute-start(bf16[1,128,768]{2,1,0:T(8,128)(2,1)S(1)} %constant_dynamic-slice_fusion.2), channel_id=1, source_target_pairs={{0,16},{16,0},{1,17},{17,1},{2,18},{18,2},{3,19},{19,3},{4,20},{20... | collective-permute-start | bytes 589832 | tf_op jit(solution)/shard_map/ppermute | solution.py:403
  341.3 10.9 %collective-permute-start.41 = (bf16[32,1024]{1,0:T(8,128)(2,1)S(1)}, bf16[32,1024]{1,0:T(8,128)(2,1)S(1)}, u32[]{:S(2)}, u32[]{:S(2)}) collective-permute-start(bf16[32,1024]{1,0:T(8,128)(2,1)S(1)} %get-tuple-element.273), channel_id=1, source_target_pairs={{0,1},{1,0},{2,3},{3,2},{4,5},{5,4},{6,7},{7,6},{8,9},{9,8},{10,11... | collective-permute-start | bytes 196616 | tf_op jit(solution)/shard_map/ppermute | solution.py:403
  345.0 8.6 %collective-permute-start.42 = (bf16[32,1024]{1,0:T(8,128)(2,1)S(1)}, bf16[32,1024]{1,0:T(8,128)(2,1)S(1)}, u32[]{:S(2)}, u32[]{:S(2)}) collective-permute-start(bf16[32,1024]{1,0:T(8,128)(2,1)S(1)} %get-tuple-element.272), channel_id=1, source_target_pairs={{0,2},{1,3},{2,0},{3,1},{4,6},{5,7},{6,4},{7,5},{8,10},{9,11},{10,... | collective-permute-start | bytes 196616 | tf_op jit(solution)/shard_map/ppermute | solution.py:403
  346.1 10.9 %collective-permute-start.43 = (bf16[32,1024]{1,0:T(8,128)(2,1)S(1)}, bf16[32,1024]{1,0:T(8,128)(2,1)S(1)}, u32[]{:S(2)}, u32[]{:S(2)}) collective-permute-start(bf16[32,1024]{1,0:T(8,128)(2,1)S(1)} %get-tuple-element.271), channel_id=1, source_target_pairs={{0,3},{1,2},{2,1},{3,0},{4,7},{5,6},{6,5},{7,4},{8,11},{9,10},{10,... | collective-permute-start | bytes 196616 | tf_op jit(solution)/shard_map/ppermute | solution.py:403
  352.2 5.0 %collective-permute-start.39 = (f32[10,1024]{1,0:T(8,128)S(1)}, f32[10,1024]{1,0:T(8,128)S(1)}, u32[]{:S(2)}, u32[]{:S(2)}) collective-permute-start(f32[10,1024]{1,0:T(8,128)S(1)} %add.251), channel_id=1, source_target_pairs={{0,16},{16,0},{1,17},{17,1},{2,18},{18,2},{3,19},{19,3},{4,20},{20... | collective-permute-start | bytes 122888 | tf_op jit(solution)/shard_map/ppermute | solution.py:403
  357.6 12.9 %copy-start.13 = (bf16[2,2,256,1024]{3,2,1,0:T(8,128)(2,1)}, bf16[2,2,256,1024]{3,2,1,0:T(8,128)(2,1)S(1)}, u32[]{:S(2)}) copy-start(bf16[2,2,256,1024]{3,2,1,0:T(8,128)(2,1)S(1)} %maximum_select_fusion) | copy-start | bytes 6291460
  357.6 11.5 %collective-permute-start.45 = (bf16[2,2,256,1024]{3,2,1,0:T(8,128)(2,1)S(1)}, bf16[2,2,256,1024]{3,2,1,0:T(8,128)(2,1)S(1)}, u32[]{:S(2)}, u32[]{:S(2)}) collective-permute-start(bf16[2,2,256,1024]{3,2,1,0:T(8,128)(2,1)S(1)} %maximum_select_fusion), channel_id=1, source_target_pairs={{0,4},{4,0},{8,12},{12,8},{1,5},{5,1},{9,13},{13,9},{2,6},{6,2},{1... | collective-permute-start | bytes 6291464 | tf_op jit(solution)/shard_map/ppermute | solution.py:403
  362.5 6.4 %collective-permute-start.44 = (bf16[512,256]{1,0:T(8,128)(2,1)S(1)}, bf16[512,256]{1,0:T(8,128)(2,1)S(1)}, u32[]{:S(2)}, u32[]{:S(2)}) collective-permute-start(bf16[512,256]{1,0:T(8,128)(2,1)S(1)} %constant_dynamic-update-slice_fusion.10), channel_id=1, source_target_pairs={{0,16},{4,12},{8,24},{12,4},{16,0},{20,28},{24,8},{28,20},{1,17},{... | collective-permute-start | bytes 786440 | tf_op jit(solution)/shard_map/ppermute | solution.py:792
  369.1 9.2 %collective-permute-start.46 = (bf16[2,512,256]{2,1,0:T(8,128)(2,1)S(1)}, bf16[2,512,256]{2,1,0:T(8,128)(2,1)S(1)}, u32[]{:S(2)}, u32[]{:S(2)}) collective-permute-start(bf16[2,512,256]{2,1,0:T(8,128)(2,1)S(1)} %maximum_select_fusion.6), channel_id=1, source_target_pairs={{0,8},{4,20},{8,0},{12,28},{16,24},{20,4},{24,16},{28,12},{1,9},{5... | collective-permute-start | bytes 1572872 | tf_op jit(solution)/shard_map/ppermute | solution.py:792
  370.5 13.0 %copy-start.7 = (f32[384,1024]{1,0:T(8,128)S(1)}, f32[384,1024]{1,0:T(8,128)}, u32[]{:S(2)}) copy-start(f32[384,1024]{1,0:T(8,128)} %copy-done.6) | copy-start | bytes 4718596
  380.9 5.6 %collective-permute-start.47 = (bf16[2,2,512,256]{3,2,1,0:T(8,128)(2,1)}, bf16[2,2,512,256]{3,2,1,0:T(8,128)(2,1)S(1)}, u32[]{:S(2)}, u32[]{:S(2)}) collective-permute-start(bf16[2,2,512,256]{3,2,1,0:T(8,128)(2,1)} %maximum_select_fusion.2), channel_id=1, source_target_pairs={{0,4},{4,0},{8,12},{12,8},{1,5},{5,1},{9,13},{13,9},{2,6},{6,2},{1... | collective-permute-start | bytes 3145736 | tf_op jit(solution)/shard_map/ppermute | solution.py:403
  380.9 5.6 %collective-permute-start.48 = (f32[10,1024]{1,0:T(8,128)S(1)}, f32[10,1024]{1,0:T(8,128)S(1)}, u32[]{:S(2)}, u32[]{:S(2)}) collective-permute-start(f32[10,1024]{1,0:T(8,128)S(1)} %add.257), channel_id=1, source_target_pairs={{0,1},{1,0},{2,3},{3,2},{4,5},{5,4},{6,7},{7,6},{8,9},{9,8},{10,11... | collective-permute-start | bytes 122888 | tf_op jit(solution)/shard_map/ppermute | solution.py:403
  387.5 6.5 %collective-permute-start.49 = (f32[10,1024]{1,0:T(8,128)S(1)}, f32[10,1024]{1,0:T(8,128)S(1)}, u32[]{:S(2)}, u32[]{:S(2)}) collective-permute-start(f32[10,1024]{1,0:T(8,128)S(1)} %add.258), channel_id=1, source_target_pairs={{0,2},{1,3},{2,0},{3,1},{4,6},{5,7},{6,4},{7,5},{8,10},{9,11},{10,... | collective-permute-start | bytes 122888 | tf_op jit(solution)/shard_map/ppermute | solution.py:403
  (33 other events, 128.0 us)
Sparse Core Ops, SparseCore 0:
  11.3 85.0 all-gather.1
  264.0 45.4 reduce-scatter.2
  315.4 65.4 reduce-scatter.4

commit v4 on v3

--- a/solution.py
+++ b/solution.py
@@ -934,7 +934,7 @@
             jax.ShapeDtypeStruct((1, width), jnp.float32),
         ],
         compiler_params=pltpu.CompilerParams(
-            dimension_semantics=("arbitrary",), vmem_limit_bytes=48 * 1024 * 1024
+            dimension_semantics=("arbitrary",), vmem_limit_bytes=54 * 1024 * 1024
         ),
         cost_estimate=LIGHT,
         name="feed_forward",

time: 407 us -> 416 us (1.022)
  starting transfers between devices: 60.5 us -> 68.6 us
  waiting for transfers between devices: 141 us -> 134 us
  other arithmetic: 29.3 us -> 34.4 us
    ppermute x40, starting transfers between devices: 45.4 us -> 53.1 us  [flip(): return lax.ppermute(value, axis, [(i, i ^ bit) for i in range(size)])]
    ppermute x3, waiting for transfers between devices: 35.3 us -> 30.8 us  [relay(): lax.ppermute(left, 'mp', to_left[:parts - step])]
    unnamed x109 -> x139, local copies, waits for them, and re-layouts: 15 us -> 16.6 us
  transfers between devices with their start and end apart: 53 -> 53, of which waited for: 25 -> 26; matrix products, arithmetic and copies ran while one was open for 11% -> 12% of each run, Pallas kernels for 28% -> 27%
where the time goes in v4:
time: 416 us; the launch traced here: 411 us
  waiting for transfers between devices  134 us (32%)
  Pallas kernels  128 us (31%)
  starting transfers between devices  68.6 us (16%)
  other arithmetic  34.4 us (8%)
  local copies, waits for them, and re-layouts  30.8 us (7%)
  between operations  15.3 us (4%)
    ppermute x40, waiting for transfers between devices, flip(): return lax.ppermute(value, axis, [(i, i ^ bit) for i in range(size)])  75.5 us
    ppermute x40, starting transfers between devices, flip(): return lax.ppermute(value, axis, [(i, i ^ bit) for i in range(size)])  53.1 us
    ppermute x3, waiting for transfers between devices, relay(): lax.ppermute(left, 'mp', to_left[:parts - step])  30.8 us
    pallas_call x1, Pallas kernels, attention_backward(): pl.pallas_call(attention_backward_kernel, grid_spec=pltpu.PrefetchScalarG...  27.3 us
    pallas_call x2, Pallas kernels, feed_forward(): pl.pallas_call(functools.partial(feed_kernel, unit=unit, count=len(weight...  26.3 us
    pallas_call x1, Pallas kernels, attention_forward(): pl.pallas_call(attention_forward_kernel, grid_spec=pltpu.PrefetchScalarGr...  24.3 us
    ppermute x3, waiting for transfers between devices, relay(): lax.ppermute(right, 'mp', to_right[step - 1:])  19.3 us
    unnamed x139, local copies, waits for them, and re-layouts  16.6 us
  transfers between devices with their start and end apart: 53, of which 26 were waited for; matrix products, arithmetic and copies ran while one was open for 12% of the time, Pallas kernels for 27%

profile of v4, /device:TPU:0, one launch (start us, length us, event | category | flops | bytes accessed | tf_op | source)
XLA Modules:
  0.0 411.2 jit_solution(5647343389436375227)
XLA Ops:
  8.6 2.6 first_norm.1
  11.3 1.8 constant_dynamic-slice_fusion.9
  15.1 1.8 constant_dynamic-slice_fusion.8
  17.7 5.0 %collective-permute-start.3 = (bf16[328,1024]{1,0:T(8,128)(2,1)}, bf16[328,1024]{1,0:T(8,128)(2,1)S(1)}, u32[]{:S(2)}, u32[]{:S(2)}) collective-permute-start(bf16[328,1024]{1,0:T(8,128)(2,1)} %pad_maximum_fusion.3), channel_id=1, source_target_pairs={{0,1},{1,2},{2,3},{4,5},{5,6},{6,7},{8,9},{9,10},{10,11},{12,13},{... | collective-permute-start | bytes 2015240 | tf_op jit(solution)/shard_map/ppermute | solution.py:1024
  24.0 1.6 collective-permute-start.1
  28.9 1.8 copy.46
  30.7 2.2 maximum_bitcast_fusion
  32.9 19.3 %collective-permute-done.3 = bf16[328,1024]{1,0:T(8,128)(2,1)S(1)} collective-permute-done((bf16[328,1024]{1,0:T(8,128)(2,1)}, bf16[328,1024]{1,0:T(8,128)(2,1)S(1)}, u32[]{:S(2)}, u32[]{:S(2)}) %collective-permute-start.3) | collective-permute-done | bytes 671776 | tf_op jit(solution)/shard_map/ppermute | solution.py:1024
  53.1 18.6 %collective-permute-done.5 = bf16[328,1024]{1,0:T(8,128)(2,1)} collective-permute-done((bf16[328,1024]{1,0:T(8,128)(2,1)}, bf16[328,1024]{1,0:T(8,128)(2,1)}, u32[]{:S(2)}, u32[]{:S(2)}) %collective-permute-start.5) | collective-permute-done | bytes 671776 | tf_op jit(solution)/shard_map/ppermute | solution.py:1025
  72.8 1.6 collective-permute-start.7
  75.2 2.3 pad_maximum_fusion.2.refs_0_
  79.7 2.1 constant_dynamic-update-slice_fusion.3
  82.9 4.8 %collective-permute-done.7.refs_2_ = bf16[1,328,1024]{2,1,0:T(8,128)(2,1)} collective-permute-done((bf16[1,328,1024]{2,1,0:T(8,128)(2,1)S(1)}, bf16[1,328,1024]{2,1,0:T(8,128)(2,1)}, u32[]{:S(2)}, u32[]{:S(2)}) %collective-permute-start.7) | collective-permute-done | bytes 671776 | tf_op jit(solution)/shard_map/ppermute | solution.py:403
  92.0 12.2 %collective-permute-done.6 = bf16[328,1024]{1,0:T(8,128)(2,1)} collective-permute-done((bf16[328,1024]{1,0:T(8,128)(2,1)}, bf16[328,1024]{1,0:T(8,128)(2,1)}, u32[]{:S(2)}, u32[]{:S(2)}) %collective-permute-start.6) | collective-permute-done | bytes 671776 | tf_op jit(solution)/shard_map/ppermute | solution.py:1025
  104.2 1.4 collective-permute-start.9
  108.2 1.5 collective-permute-start.10
  111.0 24.3 %attention_forward.1 = (bf16[1536,384]{1,0:T(8,128)(2,1)}, bf16[1536,384]{1,0:T(8,128)(2,1)}, bf16[1536,256]{1,0:T(8,128)(2,1)}, f32[8,1536]{1,0:T(8,128)}, f32[8,1536]{1,0:T(8,128)}) custom-call(s32[1]{0:T(128)} %bitcast.9.cut_ref, bf16[1536,1024]{1,0:T(8,128)(2,1)} %all-gather.2.cloned.1.call-done.rows_ref.normed_ref, bf16[3,1024,256]{2,1,0:T(8,128)(2,1)} %weight_b.1, ...), custom_call_target="tpu_custom_call" | custom-call | flops 1 | bytes 1 | tf_op jit(solution)/shard_map/attention_forward/pallas_call | solution.py:169
  135.7 2.2 collective-permute-start.11
  138.2 4.0 collective-permute-start.12
  142.7 2.0 collective-permute-start.14
  144.7 8.8 %collective-permute-done.11.refs_6_ = bf16[1,328,1024]{2,1,0:T(8,128)(2,1)S(1)} collective-permute-done((bf16[1,328,1024]{2,1,0:T(8,128)(2,1)S(1)}, bf16[1,328,1024]{2,1,0:T(8,128)(2,1)S(1)}, u32[]{:S(2)}, u32[]{:S(2)}) %collective-permute-start.11) | collective-permute-done | bytes 671776 | tf_op jit(solution)/shard_map/ppermute | solution.py:403
  155.6 3.7 collective-permute-done.13.refs_2_
  160.9 2.1 collective-permute-start.19
  164.8 13.0 %feed_forward.2 = (bf16[768,1024]{1,0:T(8,128)(2,1)}, bf16[768,1024]{1,0:T(8,128)(2,1)}, bf16[384,1024]{1,0:T(8,128)(2,1)}, bf16[384,1024]{1,0:T(8,128)(2,1)}, b...) custom-call(bf16[2,256,1024]{2,1,0:T(8,128)(2,1)} %pad_maximum_fusion.2.refs_0_, ...), custom_call_target="tpu_custom_call" | custom-call | flops 1 | bytes 1 | tf_op jit(solution)/shard_map/feed_forward/pallas_call | solution.py:924
  177.8 3.3 collective-permute-done.19
  181.2 2.2 collective-permute-done.20
  184.7 13.3 %feed_forward.3 = (bf16[768,1024]{1,0:T(8,128)(2,1)}, bf16[768,1024]{1,0:T(8,128)(2,1)}, bf16[384,1024]{1,0:T(8,128)(2,1)}, bf16[384,1024]{1,0:T(8,128)(2,1)}, b...) custom-call(bf16[2,256,1024]{2,1,0:T(8,128)(2,1)} %pad_maximum_fusion.2.refs_0_, ...), custom_call_target="tpu_custom_call" | custom-call | flops 1 | bytes 1 | tf_op jit(solution)/shard_map/feed_forward/pallas_call | solution.py:924
  198.5 2.0 collective-permute-done.21
  200.5 1.4 add_convert_fusion.3
  201.9 1.8 collective-permute-start.24
  205.2 11.9 %weight_grads.1 = (bf16[4,1,2,128,1024]{4,3,2,1,0:T(8,128)(2,1)}, bf16[4,1,2,128,1024]{4,3,2,1,0:T(8,128)(2,1)}) custom-call(s32[1]{0:T(128)} %bitcast.15.part_ref, bf16[768,1024]{1,0:T(8,128)(2,1)} %get-tuple-element.133.act_a, bf16[768,1024]{1,0:T(8,128)(2,1)} %get-tuple-element.142.act_b, bf16[768,1024]{1,0:T(8,128)(2,1)} %get-tuple-element.143.pre_a, ...), custom_call_target="tpu_custom_call" | custom-call | flops 99999997952 | bytes 1 | tf_op jit(solution)/shard_map/weight_grads/pallas_call | solution.py:968
  218.0 3.6 collective-permute-done.24.across_ref
  221.6 2.2 row_grads.1
  225.9 3.8 collective-permute-start.26
  230.0 2.0 collective-permute-start.28
  232.0 4.9 %collective-permute-done.26 = bf16[384,256]{1,0:T(8,128)(2,1)S(1)} collective-permute-done((bf16[384,256]{1,0:T(8,128)(2,1)S(1)}, bf16[384,256]{1,0:T(8,128)(2,1)S(1)}, u32[]{:S(2)}, u32[]{:S(2)}) %collective-permute-start.26) | collective-permute-done | bytes 196640 | tf_op jit(solution)/shard_map/ppermute | solution.py:403
  236.9 9.9 %collective-permute-done.27 = bf16[384,256]{1,0:T(8,128)(2,1)S(1)} collective-permute-done((bf16[384,256]{1,0:T(8,128)(2,1)S(1)}, bf16[384,256]{1,0:T(8,128)(2,1)S(1)}, u32[]{:S(2)}, u32[]{:S(2)}) %collective-permute-start.27) | collective-permute-done | bytes 196640 | tf_op jit(solution)/shard_map/ppermute | solution.py:403
  247.5 3.7 out_weight_grad.1
  252.6 2.7 fusion.4
  256.7 8.8 %collective-permute-done.22 = bf16[4,1,2,128,1024]{4,3,2,1,0:T(8,128)(2,1)} collective-permute-done((bf16[4,1,2,128,1024]{4,3,2,1,0:T(8,128)(2,1)}, bf16[4,1,2,128,1024]{4,3,2,1,0:T(8,128)(2,1)}, u32[]{:S(2)}, u32[]{:S(2)}) %collective-permute-start.22) | collective-permute-done | bytes 2097184 | tf_op jit(solution)/shard_map/ppermute | solution.py:403
  265.4 3.9 add_convert_fusion
  270.7 1.7 collective-permute-start.30
  272.5 27.3 %attention_backward.1 = (bf16[1536,384]{1,0:T(8,128)(2,1)}, bf16[1536,384]{1,0:T(8,128)(2,1)}, f32[8,512]{1,0:T(8,128)}) custom-call(s32[1]{0:T(128)} %bitcast.9.cut_ref, bf16[1536,384]{1,0:T(8,128)(2,1)} %get-tuple-element.125.qkv_a, bf16[1536,384]{1,0:T(8,128)(2,1)} %get-tuple-element.126.qkv_b, bf16[1536,256]{1,0:T(8,128)(2,1)} %bitcast.150, ...), custom_call_target="tpu_custom_call" | custom-call | flops 20000000000 | bytes 1 | tf_op jit(solution)/shard_map/attention_backward/pallas_call | solution.py:322
  303.0 7.1 %qkv_weight_grad.1 = (bf16[512,768]{1,0:T(8,128)(2,1)}, bf16[512,768]{1,0:T(8,128)(2,1)}) custom-call(s32[1]{0:T(128)} %bitcast.core_ref, bf16[1536,1024]{1,0:T(8,128)(2,1)} %all-gather.2.cloned.1.call-done.rows_ref.normed_ref, bf16[1536,384]{1,0:T(8,128)(2,1)} %get-tuple-element.181.grad_a, bf16[1536,384]{1,0:T(8,128)(2,1)} %get-tuple-element.176.grad_b), custom_call_target="tpu_custom_call" | custom-call | flops 1 | bytes 1 | tf_op jit(solution)/shard_map/qkv_weight_grad/pallas_call | solution.py:577
  311.7 8.6 %input_cotangent.1 = (bf16[1536,1024]{1,0:T(8,128)(2,1)}, f32[16,1024]{1,0:T(8,128)}) custom-call(bf16[1536,384]{1,0:T(8,128)(2,1)} %get-tuple-element.181.grad_a, bf16[1536,384]{1,0:T(8,128)(2,1)} %get-tuple-element.176.grad_b, bf16[3,1024,256]{2,1,0:T(8,128)(2,1)} %weight_b.1, bf16[3,1024,256]{2,1,0:T(8,128)(2,1)} %weight_b.1, ...), custom_call_target="tpu_custom_call" | custom-call | flops 1 | bytes 1 | tf_op jit(solution)/shard_map/input_cotangent/pallas_call | solution.py:840
  320.3 1.8 collective-permute-start.33
  323.0 6.4 %collective-permute-done.33 = bf16[4,1,32,1024]{3,2,1,0:T(8,128)(2,1)} collective-permute-done((bf16[4,1,32,1024]{3,2,1,0:T(8,128)(2,1)}, bf16[4,1,32,1024]{3,2,1,0:T(8,128)(2,1)}, u32[]{:S(2)}, u32[]{:S(2)}) %collective-permute-start.33) | collective-permute-done | bytes 262176 | tf_op jit(solution)/shard_map/ppermute | solution.py:403
  331.0 1.7 collective-permute-start.35
  333.3 2.8 fusion.3
  336.9 1.8 collective-permute-start.37
  338.8 1.7 collective-permute-done.35
  340.6 5.9 %collective-permute-done.37 = f32[10,1024]{1,0:T(8,128)S(1)} collective-permute-done((f32[10,1024]{1,0:T(8,128)S(1)}, f32[10,1024]{1,0:T(8,128)S(1)}, u32[]{:S(2)}, u32[]{:S(2)}) %collective-permute-start.37) | collective-permute-done | bytes 40992 | tf_op jit(solution)/shard_map/ppermute | solution.py:403
  349.1 3.9 collective-permute-start.41
  353.3 2.2 collective-permute-start.43
  355.5 3.9 collective-permute-done.41
  361.3 2.0 collective-permute-done.43
  365.1 5.5 %collective-permute-start.45 = (bf16[2,2,256,1024]{3,2,1,0:T(8,128)(2,1)S(1)}, bf16[2,2,256,1024]{3,2,1,0:T(8,128)(2,1)S(1)}, u32[]{:S(2)}, u32[]{:S(2)}) collective-permute-start(bf16[2,2,256,1024]{3,2,1,0:T(8,128)(2,1)S(1)} %maximum_select_fusion), channel_id=1, source_target_pairs={{0,4},{4,0},{8,12},{12,8},{1,5},{5,1},{9,13},{13,9},{2,6},{6,2},{1... | collective-permute-start | bytes 6291464 | tf_op jit(solution)/shard_map/ppermute | solution.py:403
  370.9 1.4 collective-permute-start.44
  372.3 5.0 %collective-permute-done.44 = bf16[512,256]{1,0:T(8,128)(2,1)S(1)} collective-permute-done((bf16[512,256]{1,0:T(8,128)(2,1)S(1)}, bf16[512,256]{1,0:T(8,128)(2,1)S(1)}, u32[]{:S(2)}, u32[]{:S(2)}) %collective-permute-start.44) | collective-permute-done | bytes 262176 | tf_op jit(solution)/shard_map/ppermute | solution.py:792
  378.8 6.6 %feed_grads_out.1 = (f32[1024,1024]{1,0:T(8,128)}, f32[1024,1024]{1,0:T(8,128)}) custom-call(s32[1]{0:T(128)} %bitcast.core_ref, bf16[4,2,128,1024]{3,2,1,0:T(8,128)(2,1)} %bitcast.134, bf16[4,2,128,1024]{3,2,1,0:T(8,128)(2,1)} %bitcast.142), custom_call_target="tpu_custom_call" | custom-call | flops 1 | bytes 1 | tf_op jit(solution)/shard_map/feed_grads_out/pallas_call | solution.py:480
  388.1 4.5 %collective-permute-start.48 = (f32[10,1024]{1,0:T(8,128)S(1)}, f32[10,1024]{1,0:T(8,128)S(1)}, u32[]{:S(2)}, u32[]{:S(2)}) collective-permute-start(f32[10,1024]{1,0:T(8,128)S(1)} %add.257), channel_id=1, source_target_pairs={{0,1},{1,0},{2,3},{3,2},{4,5},{5,4},{6,7},{7,6},{8,9},{9,8},{10,11... | collective-permute-start | bytes 122888 | tf_op jit(solution)/shard_map/ppermute | solution.py:403
  393.7 2.0 token_grads.1
  395.8 1.7 collective-permute-start.49
  397.5 3.7 attention_grads_out.1
  (322 shorter events, 64.3 us)
Async XLA Ops:
  7.2 18.4 %copy-start = (f32[32,4]{0,1:T(4,128)S(1)}, f32[32,4]{0,1:T(4,128)}, u32[]{:S(2)}) copy-start(f32[32,4]{0,1:T(4,128)} %param.21) | copy-start | bytes 1540
  7.2 97.0 %all-gather.2.cloned.1.call-start = ((), (), s32[]{:S(2)}) async-start(), calls=%async_computation.2 | async-start | bytes 3932160 | tf_op jit(solution)/shard_map/all_gather | solution.py:1033
  11.2 318.2 %reduce-scatter.3.cloned.1.call-start = ((), (), s32[]{:S(2)}) async-start(), calls=%async_computation.3 | async-start | bytes 2621440 | tf_op jit(solution)/shard_map/reduce_scatter | solution.py:1148
  13.0 12.8 %copy-start.51 = (s32[1,1536]{1,0:T(1,128)S(1)}, s32[1,1536]{1,0:T(1,128)}, u32[]{:S(2)}) copy-start(s32[1,1536]{1,0:T(1,128)} %param.16) | copy-start | bytes 18436
  13.2 14.9 %copy-start.25 = (bf16[1024,128]{0,1:T(8,128)(2,1)}, bf16[1024,128]{0,1:T(8,128)(2,1)S(1)}, u32[]{:S(2)}) copy-start(bf16[1024,128]{0,1:T(8,128)(2,1)S(1)} %copy.45) | copy-start | bytes 786436
  17.7 34.5 %collective-permute-start.3 = (bf16[328,1024]{1,0:T(8,128)(2,1)}, bf16[328,1024]{1,0:T(8,128)(2,1)S(1)}, u32[]{:S(2)}, u32[]{:S(2)}) collective-permute-start(bf16[328,1024]{1,0:T(8,128)(2,1)} %pad_maximum_fusion.3), channel_id=1, source_target_pairs={{0,1},{1,2},{2,3},{4,5},{5,6},{6,7},{8,9},{9,10},{10,11},{12,13},{... | collective-permute-start | bytes 2015240 | tf_op jit(solution)/shard_map/ppermute | solution.py:1024
  22.7 48.9 %collective-permute-start.5 = (bf16[328,1024]{1,0:T(8,128)(2,1)}, bf16[328,1024]{1,0:T(8,128)(2,1)}, u32[]{:S(2)}, u32[]{:S(2)}) collective-permute-start(bf16[328,1024]{1,0:T(8,128)(2,1)} %pad_maximum_fusion.3), channel_id=1, source_target_pairs={{1,0},{2,1},{3,2},{5,4},{6,5},{7,6},{9,8},{10,9},{11,10},{13,12},{... | collective-permute-start | bytes 2015240 | tf_op jit(solution)/shard_map/ppermute | solution.py:1025
  24.0 53.5 %collective-permute-start.1 = (bf16[384,1024]{1,0:T(8,128)(2,1)S(1)}, bf16[384,1024]{1,0:T(8,128)(2,1)}, u32[]{:S(2)}, u32[]{:S(2)}) collective-permute-start(bf16[384,1024]{1,0:T(8,128)(2,1)S(1)} %copy-done.4), channel_id=1, source_target_pairs={{0,8},{4,12},{8,0},{12,4},{1,9},{5,13},{9,1},{13,5},{2,10},{6,14},... | collective-permute-start | bytes 2359304 | tf_op jit(solution)/shard_map/ppermute | solution.py:403
  25.6 56.2 %collective-permute-start = (bf16[384,1024]{1,0:T(8,128)(2,1)S(1)}, bf16[384,1024]{1,0:T(8,128)(2,1)}, u32[]{:S(2)}, u32[]{:S(2)}) collective-permute-start(bf16[384,1024]{1,0:T(8,128)(2,1)S(1)} %copy-done.4), channel_id=1, source_target_pairs={{0,4},{4,0},{8,12},{12,8},{1,5},{5,1},{9,13},{13,9},{2,6},{6,2},{1... | collective-permute-start | bytes 2359304 | tf_op jit(solution)/shard_map/ppermute | solution.py:403
  72.8 14.9 %collective-permute-start.7 = (bf16[1,328,1024]{2,1,0:T(8,128)(2,1)S(1)}, bf16[1,328,1024]{2,1,0:T(8,128)(2,1)}, u32[]{:S(2)}, u32[]{:S(2)}) collective-permute-start(bf16[1,328,1024]{2,1,0:T(8,128)(2,1)S(1)} %select_bitcast_fusion.1.refs_1_), channel_id=1, source_target_pairs={{0,16},{16,0},{1,17},{17,1},{2,18},{18,2},{3,19},{19,3},{4,20},{20... | collective-permute-start | bytes 2015240 | tf_op jit(solution)/shard_map/ppermute | solution.py:403
  77.5 12.6 %collective-permute-start.2 = (bf16[384,1024]{1,0:T(8,128)(2,1)}, bf16[384,1024]{1,0:T(8,128)(2,1)S(1)}, u32[]{:S(2)}, u32[]{:S(2)}) collective-permute-start(bf16[384,1024]{1,0:T(8,128)(2,1)} %collective-permute-done.1), channel_id=1, source_target_pairs={{0,4},{4,0},{8,12},{12,8},{1,5},{5,1},{9,13},{13,9},{2,6},{6,2},{1... | collective-permute-start | bytes 2359304 | tf_op jit(solution)/shard_map/ppermute | solution.py:403
  77.6 13.5 %collective-permute-start.4 = (bf16[328,1024]{1,0:T(8,128)(2,1)S(1)}, bf16[328,1024]{1,0:T(8,128)(2,1)S(1)}, u32[]{:S(2)}, u32[]{:S(2)}) collective-permute-start(bf16[328,1024]{1,0:T(8,128)(2,1)S(1)} %copy-done.23), channel_id=1, source_target_pairs={{1,2},{2,3},{5,6},{6,7},{9,10},{10,11},{13,14},{14,15},{17,18},{18... | collective-permute-start | bytes 2015240 | tf_op jit(solution)/shard_map/ppermute | solution.py:1024
  78.4 25.8 %collective-permute-start.6 = (bf16[328,1024]{1,0:T(8,128)(2,1)}, bf16[328,1024]{1,0:T(8,128)(2,1)}, u32[]{:S(2)}, u32[]{:S(2)}) collective-permute-start(bf16[328,1024]{1,0:T(8,128)(2,1)} %collective-permute-done.5), channel_id=1, source_target_pairs={{1,0},{2,1},{5,4},{6,5},{9,8},{10,9},{13,12},{14,13},{17,16},{18,1... | collective-permute-start | bytes 2015240 | tf_op jit(solution)/shard_map/ppermute | solution.py:1025
  82.9 24.0 %copy-start.17 = (bf16[768,1024]{1,0:T(8,128)(2,1)}, bf16[768,1024]{1,0:T(8,128)(2,1)S(1)}, u32[]{:S(2)}) copy-start(bf16[768,1024]{1,0:T(8,128)(2,1)S(1)} %constant_dynamic-update-slice_fusion.refs_9_.grad_a) | copy-start | bytes 4718596
  89.5 20.4 %collective-permute-start.15 = (bf16[2,64,1024]{2,1,0:T(8,128)(2,1)}, bf16[2,64,1024]{2,1,0:T(8,128)(2,1)}, u32[]{:S(2)}, u32[]{:S(2)}) collective-permute-start(bf16[2,64,1024]{2,1,0:T(8,128)(2,1)} %reverse_select_fusion.2), channel_id=1, source_target_pairs={{0,4},{4,0},{8,12},{12,8},{1,5},{5,1},{9,13},{13,9},{2,6},{6,2},{1... | collective-permute-start | bytes 786440 | tf_op jit(solution)/shard_map/ppermute | solution.py:403
  104.2 31.3 %collective-permute-start.9 = (bf16[328,1024]{1,0:T(8,128)(2,1)}, bf16[328,1024]{1,0:T(8,128)(2,1)S(1)}, u32[]{:S(2)}, u32[]{:S(2)}) collective-permute-start(bf16[328,1024]{1,0:T(8,128)(2,1)} %collective-permute-done.6), channel_id=1, source_target_pairs={{1,0},{5,4},{9,8},{13,12},{17,16},{21,20},{25,24},{29,28}} | collective-permute-start | bytes 2015240 | tf_op jit(solution)/shard_map/ppermute | solution.py:1025
  107.0 28.4 %copy-start.15 = (bf16[1,328,1024]{2,1,0:T(8,128)(2,1)}, bf16[1,328,1024]{2,1,0:T(8,128)(2,1)S(1)}, u32[]{:S(2)}) copy-start(bf16[1,328,1024]{2,1,0:T(8,128)(2,1)S(1)} %add_bitcast_fusion.refs_3_) | copy-start | bytes 2015236
  107.0 28.4 %collective-permute-start.8 = (bf16[328,1024]{1,0:T(8,128)(2,1)S(1)}, bf16[328,1024]{1,0:T(8,128)(2,1)S(1)}, u32[]{:S(2)}, u32[]{:S(2)}) collective-permute-start(bf16[328,1024]{1,0:T(8,128)(2,1)S(1)} %copy-done.39), channel_id=1, source_target_pairs={{2,3},{6,7},{10,11},{14,15},{18,19},{22,23},{26,27},{30,31}} | collective-permute-start | bytes 2015240 | tf_op jit(solution)/shard_map/ppermute | solution.py:1024
  108.2 27.2 %collective-permute-start.10 = (bf16[1,328,1024]{2,1,0:T(8,128)(2,1)S(1)}, bf16[1,328,1024]{2,1,0:T(8,128)(2,1)S(1)}, u32[]{:S(2)}, u32[]{:S(2)}) collective-permute-start(bf16[1,328,1024]{2,1,0:T(8,128)(2,1)S(1)} %add_bitcast_fusion.refs_3_), channel_id=1, source_target_pairs={{0,16},{16,0},{1,17},{17,1},{2,18},{18,2},{3,19},{19,3},{4,20},{20... | collective-permute-start | bytes 2015240 | tf_op jit(solution)/shard_map/ppermute | solution.py:403
  111.0 24.4 %copy-start.24 = (bf16[328,1024]{1,0:T(8,128)(2,1)S(1)}, bf16[328,1024]{1,0:T(8,128)(2,1)}, u32[]{:S(2)}) copy-start(bf16[328,1024]{1,0:T(8,128)(2,1)} %copy-done.22) | copy-start | bytes 2015236
  135.4 25.5 %copy-start.20 = (bf16[1,328,1024]{2,1,0:T(8,128)(2,1)}, bf16[1,328,1024]{2,1,0:T(8,128)(2,1)S(1)}, u32[]{:S(2)}) copy-start(bf16[1,328,1024]{2,1,0:T(8,128)(2,1)S(1)} %collective-permute-done.10.refs_4_) | copy-start | bytes 2015236
  135.7 27.3 %copy-start.16 = (bf16[1,328,1024]{2,1,0:T(8,128)(2,1)}, bf16[1,328,1024]{2,1,0:T(8,128)(2,1)S(1)}, u32[]{:S(2)}) copy-start(bf16[1,328,1024]{2,1,0:T(8,128)(2,1)S(1)} %select_bitcast_fusion.refs_5_) | copy-start | bytes 2015236
  135.7 17.9 %collective-permute-start.11 = (bf16[1,328,1024]{2,1,0:T(8,128)(2,1)S(1)}, bf16[1,328,1024]{2,1,0:T(8,128)(2,1)S(1)}, u32[]{:S(2)}, u32[]{:S(2)}) collective-permute-start(bf16[1,328,1024]{2,1,0:T(8,128)(2,1)S(1)} %select_bitcast_fusion.refs_5_), channel_id=1, source_target_pairs={{0,16},{16,0},{1,17},{17,1},{2,18},{18,2},{3,19},{19,3},{4,20},{20... | collective-permute-start | bytes 2015240 | tf_op jit(solution)/shard_map/ppermute | solution.py:403
  138.0 16.1 %collective-permute-start.16 = (bf16[2,64,1024]{2,1,0:T(8,128)(2,1)S(1)}, bf16[2,64,1024]{2,1,0:T(8,128)(2,1)S(1)}, u32[]{:S(2)}, u32[]{:S(2)}) collective-permute-start(bf16[2,64,1024]{2,1,0:T(8,128)(2,1)S(1)} %reverse_select_fusion.1), channel_id=1, source_target_pairs={{0,4},{4,0},{8,12},{12,8},{1,5},{5,1},{9,13},{13,9},{2,6},{6,2},{1... | collective-permute-start | bytes 786440 | tf_op jit(solution)/shard_map/ppermute | solution.py:403
  138.2 17.4 %collective-permute-start.12 = (bf16[384,256]{1,0:T(8,128)(2,1)S(1)}, bf16[384,256]{1,0:T(8,128)(2,1)S(1)}, u32[]{:S(2)}, u32[]{:S(2)}) collective-permute-start(bf16[384,256]{1,0:T(8,128)(2,1)S(1)} %get-tuple-element.267), channel_id=1, source_target_pairs={{0,1},{1,0},{2,3},{3,2},{4,5},{5,4},{6,7},{7,6},{8,9},{9,8},{10,11... | collective-permute-start | bytes 589832 | tf_op jit(solution)/shard_map/ppermute | solution.py:403
  142.2 17.1 %collective-permute-start.13 = (bf16[384,256]{1,0:T(8,128)(2,1)S(1)}, bf16[384,256]{1,0:T(8,128)(2,1)S(1)}, u32[]{:S(2)}, u32[]{:S(2)}) collective-permute-start(bf16[384,256]{1,0:T(8,128)(2,1)S(1)} %get-tuple-element.266), channel_id=1, source_target_pairs={{0,2},{1,3},{2,0},{3,1},{4,6},{5,7},{6,4},{7,5},{8,10},{9,11},{10,... | collective-permute-start | bytes 589832 | tf_op jit(solution)/shard_map/ppermute | solution.py:403
  142.7 16.7 %collective-permute-start.14 = (bf16[384,256]{1,0:T(8,128)(2,1)S(1)}, bf16[384,256]{1,0:T(8,128)(2,1)S(1)}, u32[]{:S(2)}, u32[]{:S(2)}) collective-permute-start(bf16[384,256]{1,0:T(8,128)(2,1)S(1)} %get-tuple-element.265), channel_id=1, source_target_pairs={{0,3},{1,2},{2,1},{3,0},{4,7},{5,6},{6,5},{7,4},{8,11},{9,10},{10,... | collective-permute-start | bytes 589832 | tf_op jit(solution)/shard_map/ppermute | solution.py:403
  153.7 1.6 collective-permute-start.17
  160.8 2.4 collective-permute-start.18
  160.9 20.3 %collective-permute-start.19 = (bf16[384,1024]{1,0:T(8,128)(2,1)S(1)}, bf16[384,1024]{1,0:T(8,128)(2,1)S(1)}, u32[]{:S(2)}, u32[]{:S(2)}) collective-permute-start(bf16[384,1024]{1,0:T(8,128)(2,1)S(1)} %get-tuple-element.132), channel_id=1, source_target_pairs={{0,8},{4,12},{8,0},{12,4},{1,9},{5,13},{9,1},{13,5},{2,10},{6,14},... | collective-permute-start | bytes 2359304 | tf_op jit(solution)/shard_map/ppermute | solution.py:403
  181.2 2.3 collective-permute-start.20
  198.0 2.6 collective-permute-start.21
  198.2 23.5 %collective-permute-start.23 = (bf16[384,1024]{1,0:T(8,128)(2,1)}, bf16[384,1024]{1,0:T(8,128)(2,1)S(1)}, u32[]{:S(2)}, u32[]{:S(2)}) collective-permute-start(bf16[384,1024]{1,0:T(8,128)(2,1)} %get-tuple-element.146), channel_id=1, source_target_pairs={{0,4},{4,0},{8,12},{12,8},{1,5},{5,1},{9,13},{13,9},{2,6},{6,2},{1... | collective-permute-start | bytes 2359304 | tf_op jit(solution)/shard_map/ppermute | solution.py:403
  201.9 19.7 %collective-permute-start.24 = (bf16[384,1024]{1,0:T(8,128)(2,1)S(1)}, bf16[384,1024]{1,0:T(8,128)(2,1)S(1)}, u32[]{:S(2)}, u32[]{:S(2)}) collective-permute-start(bf16[384,1024]{1,0:T(8,128)(2,1)S(1)} %add_convert_fusion.3), channel_id=1, source_target_pairs={{0,8},{4,12},{8,0},{12,4},{1,9},{5,13},{9,1},{13,5},{2,10},{6,14},... | collective-permute-start | bytes 2359304 | tf_op jit(solution)/shard_map/ppermute | solution.py:403
  205.2 41.7 %collective-permute-start.25 = (bf16[2,384,1024]{2,1,0:T(8,128)(2,1)}, bf16[2,384,1024]{2,1,0:T(8,128)(2,1)}, u32[]{:S(2)}, u32[]{:S(2)}) collective-permute-start(bf16[2,384,1024]{2,1,0:T(8,128)(2,1)} %pad_maximum_fusion.1), channel_id=1, source_target_pairs={{0,4},{4,0},{8,12},{12,8},{1,5},{5,1},{9,13},{13,9},{2,6},{6,2},{1... | collective-permute-start | bytes 4718600 | tf_op jit(solution)/shard_map/ppermute | solution.py:403
  205.2 16.5 %copy-start.10 = (bf16[384,1024]{1,0:T(8,128)(2,1)S(1)}, bf16[384,1024]{1,0:T(8,128)(2,1)}, u32[]{:S(2)}) copy-start(bf16[384,1024]{1,0:T(8,128)(2,1)} %get-tuple-element.134.own_ref) | copy-start | bytes 2359300
  217.1 48.3 %collective-permute-start.22 = (bf16[4,1,2,128,1024]{4,3,2,1,0:T(8,128)(2,1)}, bf16[4,1,2,128,1024]{4,3,2,1,0:T(8,128)(2,1)}, u32[]{:S(2)}, u32[]{:S(2)}) collective-permute-start(bf16[4,1,2,128,1024]{4,3,2,1,0:T(8,128)(2,1)} %get-tuple-element.145), channel_id=1, source_target_pairs={{0,16},{16,0},{1,17},{17,1},{2,18},{18,2},{3,19},{19,3},{4,20},{20... | collective-permute-start | bytes 6291464 | tf_op jit(solution)/shard_map/ppermute | solution.py:403
  225.9 11.0 %collective-permute-start.26 = (bf16[384,256]{1,0:T(8,128)(2,1)S(1)}, bf16[384,256]{1,0:T(8,128)(2,1)S(1)}, u32[]{:S(2)}, u32[]{:S(2)}) collective-permute-start(bf16[384,256]{1,0:T(8,128)(2,1)S(1)} %get-tuple-element.152), channel_id=1, source_target_pairs={{0,1},{1,0},{2,3},{3,2},{4,5},{5,4},{6,7},{7,6},{8,9},{9,8},{10,11... | collective-permute-start | bytes 589832 | tf_op jit(solution)/shard_map/ppermute | solution.py:403
  229.7 17.2 %collective-permute-start.27 = (bf16[384,256]{1,0:T(8,128)(2,1)S(1)}, bf16[384,256]{1,0:T(8,128)(2,1)S(1)}, u32[]{:S(2)}, u32[]{:S(2)}) collective-permute-start(bf16[384,256]{1,0:T(8,128)(2,1)S(1)} %get-tuple-element.153), channel_id=1, source_target_pairs={{0,2},{1,3},{2,0},{3,1},{4,6},{5,7},{6,4},{7,5},{8,10},{9,11},{10,... | collective-permute-start | bytes 589832 | tf_op jit(solution)/shard_map/ppermute | solution.py:403
  230.0 16.8 %collective-permute-start.28 = (bf16[384,256]{1,0:T(8,128)(2,1)S(1)}, bf16[384,256]{1,0:T(8,128)(2,1)S(1)}, u32[]{:S(2)}, u32[]{:S(2)}) collective-permute-start(bf16[384,256]{1,0:T(8,128)(2,1)S(1)} %get-tuple-element.154), channel_id=1, source_target_pairs={{0,3},{1,2},{2,1},{3,0},{4,7},{5,6},{6,5},{7,4},{8,11},{9,10},{10,... | collective-permute-start | bytes 589832 | tf_op jit(solution)/shard_map/ppermute | solution.py:403
  251.2 4.1 collective-permute-start.29
  269.3 118.7 %reduce-scatter.5.cloned.1.call-start = ((), (), s32[]{:S(2)}) async-start(), calls=%async_computation.4 | async-start | bytes 3932160 | tf_op jit(solution)/shard_map/reduce_scatter | solution.py:1175
  270.5 30.5 %collective-permute-start.31 = (bf16[384,1024]{1,0:T(8,128)(2,1)S(1)}, bf16[384,1024]{1,0:T(8,128)(2,1)}, u32[]{:S(2)}, u32[]{:S(2)}) collective-permute-start(bf16[384,1024]{1,0:T(8,128)(2,1)S(1)} %copy-done.33), channel_id=1, source_target_pairs={{0,8},{4,12},{8,0},{12,4},{1,9},{5,13},{9,1},{13,5},{2,10},{6,14},... | collective-permute-start | bytes 2359304 | tf_op jit(solution)/shard_map/ppermute | solution.py:403
  270.7 30.2 %collective-permute-start.30 = (bf16[4,2,32,1024]{3,2,1,0:T(8,128)(2,1)}, bf16[4,2,32,1024]{3,2,1,0:T(8,128)(2,1)}, u32[]{:S(2)}, u32[]{:S(2)}) collective-permute-start(bf16[4,2,32,1024]{3,2,1,0:T(8,128)(2,1)} %get-tuple-element.170), channel_id=1, source_target_pairs={{0,8},{4,12},{8,0},{12,4},{1,9},{5,13},{9,1},{13,5},{2,10},{6,14},... | collective-permute-start | bytes 1572872 | tf_op jit(solution)/shard_map/ppermute | solution.py:403
  310.1 19.3 %collective-permute-start.32 = (bf16[512,768]{1,0:T(8,128)(2,1)}, bf16[512,768]{1,0:T(8,128)(2,1)S(1)}, u32[]{:S(2)}, u32[]{:S(2)}) collective-permute-start(bf16[512,768]{1,0:T(8,128)(2,1)} %get-tuple-element.180), channel_id=1, source_target_pairs={{0,4},{4,0},{8,12},{12,8},{1,5},{5,1},{9,13},{13,9},{2,6},{6,2},{1... | collective-permute-start | bytes 2359304 | tf_op jit(solution)/shard_map/ppermute | solution.py:403
  320.3 9.1 %collective-permute-start.33 = (bf16[4,1,32,1024]{3,2,1,0:T(8,128)(2,1)}, bf16[4,1,32,1024]{3,2,1,0:T(8,128)(2,1)}, u32[]{:S(2)}, u32[]{:S(2)}) collective-permute-start(bf16[4,1,32,1024]{3,2,1,0:T(8,128)(2,1)} %get-tuple-element.269), channel_id=1, source_target_pairs={{0,16},{16,0},{1,17},{17,1},{2,18},{18,2},{3,19},{19,3},{4,20},{20... | collective-permute-start | bytes 786440 | tf_op jit(solution)/shard_map/ppermute | solution.py:403
  331.0 5.1 %collective-permute-start.36 = (f32[10,1024]{1,0:T(8,128)}, f32[10,1024]{1,0:T(8,128)S(1)}, u32[]{:S(2)}, u32[]{:S(2)}) collective-permute-start(f32[10,1024]{1,0:T(8,128)} %reshape.212), channel_id=1, source_target_pairs={{0,4},{4,0},{8,12},{12,8},{1,5},{5,1},{9,13},{13,9},{2,6},{6,2},{1... | collective-permute-start | bytes 122888 | tf_op jit(solution)/shard_map/ppermute | solution.py:403
  331.0 9.4 %collective-permute-start.35 = (bf16[256,1024]{1,0:T(8,128)(2,1)}, bf16[256,1024]{1,0:T(8,128)(2,1)S(1)}, u32[]{:S(2)}, u32[]{:S(2)}) collective-permute-start(bf16[256,1024]{1,0:T(8,128)(2,1)} %bitcast.153), channel_id=1, source_target_pairs={{0,16},{4,12},{8,24},{12,4},{16,0},{20,28},{24,8},{28,20},{1,17},{... | collective-permute-start | bytes 1572872 | tf_op jit(solution)/shard_map/ppermute | solution.py:792
  333.0 13.5 %collective-permute-start.34 = (bf16[2,128,768]{2,1,0:T(8,128)(2,1)S(1)}, bf16[2,128,768]{2,1,0:T(8,128)(2,1)S(1)}, u32[]{:S(2)}, u32[]{:S(2)}) collective-permute-start(bf16[2,128,768]{2,1,0:T(8,128)(2,1)S(1)} %dynamic-slice_bitcast_fusion.2), channel_id=1, source_target_pairs={{0,8},{4,12},{8,0},{12,4},{1,9},{5,13},{9,1},{13,5},{2,10},{6,14},... | collective-permute-start | bytes 1179656 | tf_op jit(solution)/shard_map/ppermute | solution.py:403
  336.9 9.6 %collective-permute-start.37 = (f32[10,1024]{1,0:T(8,128)S(1)}, f32[10,1024]{1,0:T(8,128)S(1)}, u32[]{:S(2)}, u32[]{:S(2)}) collective-permute-start(f32[10,1024]{1,0:T(8,128)S(1)} %add.244), channel_id=1, source_target_pairs={{0,8},{4,12},{8,0},{12,4},{1,9},{5,13},{9,1},{13,5},{2,10},{6,14},... | collective-permute-start | bytes 122888 | tf_op jit(solution)/shard_map/ppermute | solution.py:403
  346.5 17.9 %collective-permute-start.40 = (bf16[2,256,1024]{2,1,0:T(8,128)(2,1)S(1)}, bf16[2,256,1024]{2,1,0:T(8,128)(2,1)S(1)}, u32[]{:S(2)}, u32[]{:S(2)}) collective-permute-start(bf16[2,256,1024]{2,1,0:T(8,128)(2,1)S(1)} %maximum_select_fusion.1), channel_id=1, source_target_pairs={{0,8},{4,20},{8,0},{12,28},{16,24},{20,4},{24,16},{28,12},{1,9},{5... | collective-permute-start | bytes 3145736 | tf_op jit(solution)/shard_map/ppermute | solution.py:792
  347.9 16.6 %collective-permute-start.38 = (bf16[1,128,768]{2,1,0:T(8,128)(2,1)S(1)}, bf16[1,128,768]{2,1,0:T(8,128)(2,1)S(1)}, u32[]{:S(2)}, u32[]{:S(2)}) collective-permute-start(bf16[1,128,768]{2,1,0:T(8,128)(2,1)S(1)} %constant_dynamic-slice_fusion.2), channel_id=1, source_target_pairs={{0,16},{16,0},{1,17},{17,1},{2,18},{18,2},{3,19},{19,3},{4,20},{20... | collective-permute-start | bytes 589832 | tf_op jit(solution)/shard_map/ppermute | solution.py:403
  349.1 10.3 %collective-permute-start.41 = (bf16[32,1024]{1,0:T(8,128)(2,1)S(1)}, bf16[32,1024]{1,0:T(8,128)(2,1)S(1)}, u32[]{:S(2)}, u32[]{:S(2)}) collective-permute-start(bf16[32,1024]{1,0:T(8,128)(2,1)S(1)} %get-tuple-element.273), channel_id=1, source_target_pairs={{0,1},{1,0},{2,3},{3,2},{4,5},{5,4},{6,7},{7,6},{8,9},{9,8},{10,11... | collective-permute-start | bytes 196616 | tf_op jit(solution)/shard_map/ppermute | solution.py:403
  353.1 8.2 %collective-permute-start.42 = (bf16[32,1024]{1,0:T(8,128)(2,1)S(1)}, bf16[32,1024]{1,0:T(8,128)(2,1)S(1)}, u32[]{:S(2)}, u32[]{:S(2)}) collective-permute-start(bf16[32,1024]{1,0:T(8,128)(2,1)S(1)} %get-tuple-element.272), channel_id=1, source_target_pairs={{0,2},{1,3},{2,0},{3,1},{4,6},{5,7},{6,4},{7,5},{8,10},{9,11},{10,... | collective-permute-start | bytes 196616 | tf_op jit(solution)/shard_map/ppermute | solution.py:403
  353.3 10.0 %collective-permute-start.43 = (bf16[32,1024]{1,0:T(8,128)(2,1)S(1)}, bf16[32,1024]{1,0:T(8,128)(2,1)S(1)}, u32[]{:S(2)}, u32[]{:S(2)}) collective-permute-start(bf16[32,1024]{1,0:T(8,128)(2,1)S(1)} %get-tuple-element.271), channel_id=1, source_target_pairs={{0,3},{1,2},{2,1},{3,0},{4,7},{5,6},{6,5},{7,4},{8,11},{9,10},{10,... | collective-permute-start | bytes 196616 | tf_op jit(solution)/shard_map/ppermute | solution.py:403
  359.4 5.0 %collective-permute-start.39 = (f32[10,1024]{1,0:T(8,128)S(1)}, f32[10,1024]{1,0:T(8,128)S(1)}, u32[]{:S(2)}, u32[]{:S(2)}) collective-permute-start(f32[10,1024]{1,0:T(8,128)S(1)} %add.251), channel_id=1, source_target_pairs={{0,16},{16,0},{1,17},{17,1},{2,18},{18,2},{3,19},{19,3},{4,20},{20... | collective-permute-start | bytes 122888 | tf_op jit(solution)/shard_map/ppermute | solution.py:403
  365.1 13.5 %copy-start.13 = (bf16[2,2,256,1024]{3,2,1,0:T(8,128)(2,1)}, bf16[2,2,256,1024]{3,2,1,0:T(8,128)(2,1)S(1)}, u32[]{:S(2)}) copy-start(bf16[2,2,256,1024]{3,2,1,0:T(8,128)(2,1)S(1)} %maximum_select_fusion) | copy-start | bytes 6291460
  365.1 12.3 %collective-permute-start.45 = (bf16[2,2,256,1024]{3,2,1,0:T(8,128)(2,1)S(1)}, bf16[2,2,256,1024]{3,2,1,0:T(8,128)(2,1)S(1)}, u32[]{:S(2)}, u32[]{:S(2)}) collective-permute-start(bf16[2,2,256,1024]{3,2,1,0:T(8,128)(2,1)S(1)} %maximum_select_fusion), channel_id=1, source_target_pairs={{0,4},{4,0},{8,12},{12,8},{1,5},{5,1},{9,13},{13,9},{2,6},{6,2},{1... | collective-permute-start | bytes 6291464 | tf_op jit(solution)/shard_map/ppermute | solution.py:403
  370.9 6.4 %collective-permute-start.44 = (bf16[512,256]{1,0:T(8,128)(2,1)S(1)}, bf16[512,256]{1,0:T(8,128)(2,1)S(1)}, u32[]{:S(2)}, u32[]{:S(2)}) collective-permute-start(bf16[512,256]{1,0:T(8,128)(2,1)S(1)} %constant_dynamic-update-slice_fusion.10), channel_id=1, source_target_pairs={{0,16},{4,12},{8,24},{12,4},{16,0},{20,28},{24,8},{28,20},{1,17},{... | collective-permute-start | bytes 786440 | tf_op jit(solution)/shard_map/ppermute | solution.py:792
  377.4 9.2 %collective-permute-start.46 = (bf16[2,512,256]{2,1,0:T(8,128)(2,1)S(1)}, bf16[2,512,256]{2,1,0:T(8,128)(2,1)S(1)}, u32[]{:S(2)}, u32[]{:S(2)}) collective-permute-start(bf16[2,512,256]{2,1,0:T(8,128)(2,1)S(1)} %maximum_select_fusion.6), channel_id=1, source_target_pairs={{0,8},{4,20},{8,0},{12,28},{16,24},{20,4},{24,16},{28,12},{1,9},{5... | collective-permute-start | bytes 1572872 | tf_op jit(solution)/shard_map/ppermute | solution.py:792
  378.8 13.8 %copy-start.6 = (f32[384,1024]{1,0:T(8,128)S(1)}, f32[384,1024]{1,0:T(8,128)}, u32[]{:S(2)}) copy-start(f32[384,1024]{1,0:T(8,128)} %copy-done.5) | copy-start | bytes 4718596
  388.1 7.7 %collective-permute-start.47 = (bf16[2,2,512,256]{3,2,1,0:T(8,128)(2,1)}, bf16[2,2,512,256]{3,2,1,0:T(8,128)(2,1)S(1)}, u32[]{:S(2)}, u32[]{:S(2)}) collective-permute-start(bf16[2,2,512,256]{3,2,1,0:T(8,128)(2,1)} %maximum_select_fusion.2), channel_id=1, source_target_pairs={{0,4},{4,0},{8,12},{12,8},{1,5},{5,1},{9,13},{13,9},{2,6},{6,2},{1... | collective-permute-start | bytes 3145736 | tf_op jit(solution)/shard_map/ppermute | solution.py:403
  388.1 7.7 %collective-permute-start.48 = (f32[10,1024]{1,0:T(8,128)S(1)}, f32[10,1024]{1,0:T(8,128)S(1)}, u32[]{:S(2)}, u32[]{:S(2)}) collective-permute-start(f32[10,1024]{1,0:T(8,128)S(1)} %add.257), channel_id=1, source_target_pairs={{0,1},{1,0},{2,3},{3,2},{4,5},{5,4},{6,7},{7,6},{8,9},{9,8},{10,11... | collective-permute-start | bytes 122888 | tf_op jit(solution)/shard_map/ppermute | solution.py:403
  395.8 6.6 %collective-permute-start.49 = (f32[10,1024]{1,0:T(8,128)S(1)}, f32[10,1024]{1,0:T(8,128)S(1)}, u32[]{:S(2)}, u32[]{:S(2)}) collective-permute-start(f32[10,1024]{1,0:T(8,128)S(1)} %add.258), channel_id=1, source_target_pairs={{0,2},{1,3},{2,0},{3,1},{4,6},{5,7},{6,4},{7,5},{8,10},{9,11},{10,... | collective-permute-start | bytes 122888 | tf_op jit(solution)/shard_map/ppermute | solution.py:403
  (48 other events, 223.9 us)
Sparse Core Ops, SparseCore 0:
  11.3 84.1 all-gather.1
  269.5 44.4 reduce-scatter.2
  323.1 64.9 reduce-scatter.4
